TPU v7x, 32 devices: a whole 2x2x4 slice. The times are simulated.
32 devices in a mesh: row: 8 (over y, x, core), col: 4 (over z).
Axes of the slice: x: 2, y: 2, z: 4, core: 2. Of those that a mesh axis runs over, the one named last changes fastest.
Arguments:
- raw_rows: bfloat16 [32768, 64], P(('row', 'col')), may hold values from -6 to 6
- raw_wide: int32 [32768], P(('row', 'col')), may hold values from 0 to 1
- raw_dest: int32 [32768], P(('row', 'col')), may hold values from 0 to 31, as said below
- raw_slot: int32 [32768], P(('row', 'col')), may hold values from 0 to 511
- proj_narrow: bfloat16 [32, 128], replicated, may hold values from -1 to 1
- proj_wide: bfloat16 [64, 128], replicated, may hold values from -0.75 to 0.75
- adj_values: bfloat16 [8192, 8192], P('row', 'col'), may hold values from -1 to 1
- tile_mask: int32 [64, 64], P('row', 'col'), may hold values 0 or 1
- tile_scale: float32 [64, 64], P('row', 'col'), may hold values from 0.008286407 to 0.082864076
- weight_sum: bfloat16 [2, 128, 128], replicated, may hold values from -0.5 to 0.5
- weight_product: bfloat16 [2, 128, 128], replicated, may hold values from -0.5 to 0.5
Outputs:
- user_out: bfloat16 [8192, 128], P(('row', 'col'))
- item_out: bfloat16 [4, 2048, 128], P('col', 'row')
Inputs may be any that keep to these rules, and one draw needn't show every extreme that they name: `raw_dest`: among the feature rows stored on one device at most 96 have any one destination; one device, drawn from the seed, is the destination of exactly 96 rows of every device.
All inputs are finite; a program needn't handle non-finite values. No bound on the sum of `tile_mask` on one device may be relied on, other than what follows from the above.
Results may differ from a plain program's by a relative error of at most 0.025.
Values may be sent and summed in bfloat16 or wider, within the bound.
No kernel may reach another device: no remote copies, remote signals or barrier semaphores. Data moves between devices by JAX's collectives and lax.ppermute only.
A program may use at most 128 MiB of HBM per device.

v0:
```python
import functools

import jax
import jax.numpy as jnp
from jax import lax
from jax.experimental import pallas as pl
from jax.experimental.pallas import tpu as pltpu
from jax.sharding import PartitionSpec as P


TILE = 128
LANES = 128
CODE_ROWS = 8
F32 = jnp.float32
BF16 = jnp.bfloat16
NT = (((1,), (1,)), ((), ()))


def power_of_two(n):
    return n & (n - 1) == 0


def peer_to(i, k, n):
    return i ^ k if power_of_two(n) else (i + k) % n


def vmem_spec():
    return pl.BlockSpec(memory_space=pltpu.VMEM)


def params():
    return pltpu.CompilerParams(vmem_limit_bytes=24 * 2**20)


def whole_vmem():
    return pltpu.CompilerParams(vmem_limit_bytes=67_043_328)


def no_room():
    return pltpu.CompilerParams(vmem_limit_bytes=52 * 2**20)


def dispatch_kernel(devices, slots, *refs):
    sources, out_ref, (raw_ref, dest_ref, slot_ref, wide_ref), sems = (
        refs[:4],
        refs[4],
        refs[5:9],
        refs[9],
    )
    copies = [
        pltpu.make_async_copy(source, ref, sems.at[n])
        for n, (source, ref) in enumerate(
            zip(sources, (raw_ref, dest_ref, slot_ref, wide_ref), strict=True)
        )
    ]
    for copy in copies:
        copy.start()
    copies[1].wait()
    features, rows = raw_ref.shape
    chunks = rows // LANES
    dest = dest_ref[...]
    hot = (lax.broadcasted_iota(jnp.int32, (devices, rows), 0) == dest).astype(F32)
    hot_bf = hot.astype(BF16)
    before = lax.broadcasted_iota(jnp.int32, (LANES, 2 * LANES), 0)
    column = lax.broadcasted_iota(jnp.int32, (LANES, 2 * LANES), 1)
    prefix = ((before < column) | (column >= LANES)).astype(F32).astype(BF16)
    base = jnp.zeros((devices, LANES), F32)
    ranks = []
    for chunk in range(chunks):
        lanes = slice(chunk * LANES, (chunk + 1) * LANES)
        counted = jnp.dot(hot_bf[:, lanes], prefix, preferred_element_type=F32)
        ranks.append(
            jnp.sum((counted[:, :LANES] + base) * hot[:, lanes], axis=0, keepdims=True)
        )
        base = base + counted[:, LANES:]
    rank = jnp.concatenate(ranks, axis=1)
    place = (
        lax.broadcasted_iota(jnp.int32, (slots, rows), 0).astype(F32) == rank
    ).astype(F32).astype(BF16)
    for copy in (copies[0], copies[2], copies[3]):
        copy.wait()
    slot = slot_ref[...]
    code = lax.broadcasted_iota(jnp.int32, (2 * CODE_ROWS, rows), 0)
    codes = jnp.where(
        code == 0,
        slot // 256,
        jnp.where(code == 1, slot % 256, jnp.where(code == 2, wide_ref[...], 0)),
    )
    ext = jnp.concatenate([raw_ref[...], codes.astype(F32).astype(BF16)], axis=0)
    group = 8
    for first in range(0, devices, group):
        masked = jnp.concatenate(
            [ext * hot_bf[d : d + 1, :] for d in range(first, first + group)], axis=0
        )
        placed = lax.dot_general(masked, place, NT, preferred_element_type=F32).astype(BF16)
        for d in range(group):
            start = d * (features + 2 * CODE_ROWS)
            out_ref[first + d] = placed[start : start + features + CODE_ROWS]


def dispatch(raw, dest, slot, wide, devices, slots):
    features, rows = raw.shape
    return pl.pallas_call(
        functools.partial(dispatch_kernel, devices, slots),
        out_shape=jax.ShapeDtypeStruct((devices, features + CODE_ROWS, slots), BF16),
        in_specs=[pl.BlockSpec(memory_space=pltpu.HBM)] * 4,
        out_specs=vmem_spec(),
        scratch_shapes=[
            pltpu.VMEM(raw.shape, raw.dtype),
            *[pltpu.VMEM((1, rows), jnp.int32) for _ in range(3)],
            pltpu.SemaphoreType.DMA((4,)),
        ],
        compiler_params=whole_vmem(),
        name="dispatch",
    )(raw, dest, slot, wide)


def segment_kernel(narrow, upd, cols, recv_ref, proj_narrow_ref, proj_wide_ref, *refs):
    adj_refs, (user_ref, user_t_ref, item_ref) = refs[:cols], refs[cols : cols + 3]
    held_refs, sems = refs[cols + 3 : -1], refs[-1]
    copies = [
        pltpu.make_async_copy(adj_ref, held_ref, sems.at[k])
        for k, (adj_ref, held_ref) in enumerate(zip(adj_refs, held_refs, strict=True))
    ]
    for copy in copies:
        copy.start()
    devices, height, slots = recv_ref.shape
    features = height - CODE_ROWS
    nodes = user_ref.shape[0] + item_ref.shape[0]
    group = 8
    total = jnp.zeros((nodes, features + narrow), F32)
    for first in range(0, devices, group):
        block = jnp.concatenate([recv_ref[first + p] for p in range(group)], axis=1)
        codes = block[features:].astype(F32)
        node = (codes[0:1] * 256 + codes[1:2]).astype(jnp.int32)
        wide = codes[2:3].astype(BF16)
        rows = block[:features]
        values = jnp.concatenate([rows * wide, rows[:narrow] * (1 - wide)], axis=0)
        hot = (
            lax.broadcasted_iota(jnp.int32, (nodes, group * slots), 0) == node
        ).astype(F32).astype(BF16)
        total = total + lax.dot_general(hot, values, NT, preferred_element_type=F32)
    weights = jnp.concatenate([proj_wide_ref[...], proj_narrow_ref[...]], axis=0)
    initial = jnp.zeros((nodes, weights.shape[1]), F32)
    rest = total
    for _ in range(3):
        part = rest.astype(BF16)
        initial = initial + jnp.dot(part, weights, preferred_element_type=F32)
        rest = rest - part.astype(F32)
    users = initial[:upd]
    items = initial[upd:].astype(BF16)
    user_ref[...] = users.astype(BF16)
    user_t_ref[...] = users.T.astype(BF16)
    item_ref[...] = items
    for copy in copies:
        copy.wait()


def segment(recv, proj_narrow, proj_wide, adjacency, upd, ipd):
    cols = len(adjacency)
    d = proj_wide.shape[1]
    return pl.pallas_call(
        functools.partial(segment_kernel, proj_narrow.shape[0], upd, cols),
        out_shape=(
            jax.ShapeDtypeStruct((upd, d), BF16),
            jax.ShapeDtypeStruct((d, upd), BF16),
            jax.ShapeDtypeStruct((ipd, d), BF16),
            *[jax.ShapeDtypeStruct(block.shape, BF16) for block in adjacency],
        ),
        in_specs=[vmem_spec()] * 3 + [pl.BlockSpec(memory_space=pltpu.HBM)] * cols,
        out_specs=(vmem_spec(),) * (3 + cols),
        scratch_shapes=[pltpu.SemaphoreType.DMA((cols,))],
        compiler_params=params(),
        name="segment",
    )(
        recv,
        proj_narrow,
        proj_wide,
        *[pltpu.with_memory_space_constraint(block, pltpu.HBM) for block in adjacency],
    )


def dequantize_kernel(shape, place_ref, mask_ref, scale_ref, values_ref, *refs):
    out_refs, (held, sems) = refs[:-2], refs[-2:]
    sides, chips, cols = shape
    upd, n = out_refs[0].shape
    ipd = n // (sides * chips)
    chip, side_here = place_ref[0] // sides, place_ref[0] % sides
    blocks = [peer_to(place_ref[1], k, cols) for k in range(cols)]
    lines = [
        peer_to(chip, k, chips) * sides + (side_here + side) % sides
        for side in range(sides)
        for k in range(chips)
    ]
    copies = []
    for k, block in enumerate(blocks):
        start = pl.multiple_of(block * upd, upd)
        for at, line in enumerate(lines):
            first = pl.multiple_of(line * ipd, ipd)
            copies.append(
                pltpu.make_async_copy(
                    values_ref.at[pl.ds(start, upd), pl.ds(first, ipd)],
                    held.at[k, :, pl.ds(at * ipd, ipd)],
                    sems.at[k, at],
                )
            )
            copies[-1].start()
    for k, (block, out_ref) in enumerate(zip(blocks, out_refs, strict=True)):
        for at, line in enumerate(lines):
            copies[k * len(lines) + at].wait()
            for i in range(upd // TILE):
                row = block * (upd // TILE) + i
                here = slice(i * TILE, (i + 1) * TILE)
                for j in range(ipd // TILE):
                    column = line * (ipd // TILE) + j
                    lanes = slice(at * ipd + j * TILE, at * ipd + (j + 1) * TILE)
                    factor = mask_ref[row, column].astype(F32) * scale_ref[row, column]
                    out_ref[here, lanes] = (
                        held[k, here, lanes].astype(F32) * factor
                    ).astype(BF16)


def dequantize(place, values, mask, scale, shape):
    m, n = values.shape
    sides, chips, cols = shape
    smem = pl.BlockSpec(memory_space=pltpu.SMEM)
    return pl.pallas_call(
        functools.partial(dequantize_kernel, shape),
        out_shape=(jax.ShapeDtypeStruct((m // cols, n), BF16),) * cols,
        in_specs=[smem, smem, smem, pl.BlockSpec(memory_space=pltpu.HBM)],
        out_specs=(vmem_spec(),) * cols,
        scratch_shapes=[
            pltpu.VMEM((cols, m // cols, n), BF16),
            pltpu.SemaphoreType.DMA((cols, sides * chips)),
        ],
        compiler_params=no_room(),
        cost_estimate=pl.CostEstimate(flops=m * n, bytes_accessed=4 * m * n, transcendentals=0),
        name="dequantize",
    )(place, mask, scale, values)


def from_order(n):
    return [k if power_of_two(n) else (n - k) % n for k in range(n)]


def user_sum_kernel(cols, *refs):
    adj_refs, items_refs, out_refs = refs[:cols], refs[cols:-cols], refs[-cols:]
    items = jnp.concatenate([ref[...] for ref in items_refs], axis=0)
    for adj_ref, out_ref in zip(adj_refs, out_refs, strict=True):
        out_ref[...] = jnp.dot(adj_ref[...], items, preferred_element_type=F32).astype(BF16)


def user_sums(adjacency, items):
    cols = len(adjacency)
    upd, n = adjacency[0].shape
    d = items[0].shape[1]
    return pl.pallas_call(
        functools.partial(user_sum_kernel, cols),
        out_shape=(jax.ShapeDtypeStruct((upd, d), BF16),) * cols,
        in_specs=[vmem_spec()] * (cols + len(items)),
        out_specs=(vmem_spec(),) * cols,
        compiler_params=params(),
        cost_estimate=pl.CostEstimate(
            flops=2 * cols * upd * n * d, bytes_accessed=2 * cols * upd * n, transcendentals=0
        ),
        name="user_sums",
    )(*adjacency, *items)


def item_sum_kernel(cols, *refs):
    adj_refs, users_refs, out_refs = refs[:cols], refs[cols : 2 * cols], refs[2 * cols :]
    order = from_order(cols)
    users = [ref[...] for ref in users_refs]
    at = 0
    for out_ref in reversed(out_refs):
        for r in range(out_ref.shape[0]):
            ipd = out_ref.shape[2]
            lanes = slice(at * ipd, (at + 1) * ipd)
            total = None
            for k in range(cols):
                part = jnp.dot(
                    users[k], adj_refs[order[k]][:, lanes], preferred_element_type=F32
                )
                total = part if total is None else total + part
            out_ref[r] = total.astype(out_ref.dtype)
            at += 1


def item_sums(adjacency, users_t, sides, chips):
    cols = len(adjacency)
    upd, n = adjacency[0].shape
    d = users_t[0].shape[0]
    block = (chips, d, n // (sides * chips))
    outs = [jax.ShapeDtypeStruct(block, BF16)] * (sides - 1)
    return pl.pallas_call(
        functools.partial(item_sum_kernel, cols),
        out_shape=[*outs, jax.ShapeDtypeStruct(block, F32)],
        in_specs=[vmem_spec()] * (2 * cols),
        out_specs=[vmem_spec()] * sides,
        compiler_params=params(),
        cost_estimate=pl.CostEstimate(
            flops=2 * cols * upd * n * d, bytes_accessed=2 * cols * upd * n, transcendentals=0
        ),
        name="item_sums",
    )(*adjacency, *users_t)


def item_add_kernel(chips, *refs):
    parts, outs = refs[:-chips], refs[-chips:]
    for k, out_ref in enumerate(outs):
        total = parts[0][k]
        for part in parts[1:]:
            total = total + part[k].astype(F32)
        out_ref[...] = total.astype(BF16)


def item_add(parts):
    chips, d, ipd = parts[0].shape
    return pl.pallas_call(
        functools.partial(item_add_kernel, chips),
        out_shape=(jax.ShapeDtypeStruct((d, ipd), BF16),) * chips,
        in_specs=[vmem_spec()] * len(parts),
        out_specs=(vmem_spec(),) * chips,
        compiler_params=params(),
        name="item_add",
    )(*parts)


def updated(side, own, weight_sum, weight_product):
    own = own.astype(F32)
    linear = jnp.dot((side + own).astype(BF16), weight_sum, preferred_element_type=F32)
    linear = linear + jnp.dot(
        (side * own).astype(BF16), weight_product, preferred_element_type=F32
    )
    return jnp.where(linear > 0, linear, 0.2 * linear)


def user_update_kernel(layer, own_ref, sum_ref, product_ref, *refs):
    parts, outs = refs[:-2], refs[-2:]
    side = parts[0][...].astype(F32)
    for part in parts[1:]:
        side = side + part[...].astype(F32)
    new = updated(side, own_ref[...], sum_ref[layer], product_ref[layer])
    outs[0][...] = new.astype(BF16)
    outs[1][...] = new.T.astype(BF16)


def user_update(layer, parts, own, weight_sum, weight_product):
    upd, d = own.shape
    return pl.pallas_call(
        functools.partial(user_update_kernel, layer),
        out_shape=(jax.ShapeDtypeStruct((upd, d), BF16), jax.ShapeDtypeStruct((d, upd), BF16)),
        in_specs=[vmem_spec()] * (3 + len(parts)),
        out_specs=(vmem_spec(),) * 2,
        compiler_params=params(),
        name="user_update",
    )(own, weight_sum, weight_product, *parts)


def item_update_kernel(layer, own_ref, sum_ref, product_ref, *refs):
    parts, new_ref = refs[:-1], refs[-1]
    side = parts[0][...].astype(F32)
    for part in parts[1:]:
        side = side + part[...].astype(F32)
    new = updated(side.T, own_ref[...], sum_ref[layer], product_ref[layer])
    new_ref[...] = new.astype(BF16)


def item_update(layer, parts, own, weight_sum, weight_product):
    return pl.pallas_call(
        functools.partial(item_update_kernel, layer),
        out_shape=jax.ShapeDtypeStruct(own.shape, BF16),
        in_specs=[vmem_spec()] * (3 + len(parts)),
        out_specs=vmem_spec(),
        compiler_params=params(),
        name="item_update",
    )(own, weight_sum, weight_product, *parts)


def exchange(blocks, axis, n, inner=1):
    received = [blocks[0]]
    for k in range(1, n):
        pairs = [
            (i * inner + j, peer_to(i, k, n) * inner + j) for i in range(n) for j in range(inner)
        ]
        received.append(lax.ppermute(blocks[k], axis, pairs))
    return received


def swap(block, axis, n):
    return lax.ppermute(block, axis, [(i, i ^ 1) for i in range(n)])


def ordered(received):
    order = from_order(len(received))
    return [received[order.index(k)] for k in range(len(received))]


def per_device(
    raw_rows,
    raw_wide,
    raw_dest,
    raw_slot,
    proj_narrow,
    proj_wide,
    adj_values,
    tile_mask,
    tile_scale,
    weight_sum,
    weight_product,
):
    rows = lax.axis_size("row")
    cols = lax.axis_size("col")
    devices = rows * cols
    count = raw_rows.shape[0]
    capacity = 3 * count // devices
    slots = -(-capacity // LANES) * LANES
    upd = adj_values.shape[0] // cols
    ipd = adj_values.shape[1] // rows
    layers = weight_sum.shape[0]
    sides = 2 if rows % 2 == 0 else 1
    chips = rows // sides
    place = jnp.stack([lax.axis_index("row"), lax.axis_index("col")]).astype(jnp.int32)
    send = dispatch(
        raw_rows.T,
        raw_dest.reshape(1, count),
        raw_slot.reshape(1, count),
        raw_wide.reshape(1, count),
        devices,
        slots,
    )
    recv = lax.all_to_all(send, ("row", "col"), split_axis=0, concat_axis=0, tiled=True)
    adjacency = dequantize(
        place, adj_values, tile_mask, tile_scale, (sides, chips, cols)
    )
    users, users_t, items, *adjacency = segment(recv, proj_narrow, proj_wide, adjacency, upd, ipd)
    for n in range(layers):
        all_users_t = exchange([users_t] * cols, "col", cols)
        own_swapped = [swap(items, "row", rows)]
        all_items = ordered(exchange([items] * chips, "row", chips, sides))
        swapped = [swap(block, "row", rows) for block in all_items[1:]]
        if sides > 1:
            all_items = [*all_items, *own_swapped, *swapped]
        *away, kept = item_sums(adjacency, all_users_t, sides, chips)
        came = [swap(part, "row", rows) for part in away]
        user_parts = user_sums(adjacency, all_items)
        item_parts = item_add([kept, *came])
        item_parts = exchange(item_parts, "row", chips, sides)
        user_parts = exchange(user_parts, "col", cols)
        items = item_update(n, item_parts, items, weight_sum, weight_product)
        users, users_t = user_update(n, user_parts, users, weight_sum, weight_product)
    return (users, items[None])


def solution(mesh):
    placed = (
        P(("row", "col"), None),
        P(("row", "col")),
        P(("row", "col")),
        P(("row", "col")),
        P(),
        P(),
        P("row", "col"),
        P("row", "col"),
        P("row", "col"),
        P(),
        P(),
    )
    return jax.shard_map(
        per_device,
        mesh=mesh,
        in_specs=placed,
        out_specs=(P(("row", "col"), None), P("col", "row", None)),
        check_vma=False,
    )
```

profile of v0, /device:TPU:0, one launch (start us, length us, event | category | flops | bytes accessed | tf_op | source)
XLA Modules:
  0.0 92.4 jit_solution(13531816712922107476)
XLA Ops:
  0.6 3.4 %dispatch.1 = bf16[32,72,128]{2,1,0:T(8,128)(2,1)} custom-call(bf16[64,1024]{1,0:T(8,128)(2,1)} %bitcast.7, s32[1,1024]{1,0:T(1,128)} %bitcast.9, s32[1,1024]{1,0:T(1,128)} %bitcast.10, s32[1,1024]{1,0:T(1,128)} %bitcast.11), custom_call_target="tpu_custom_call" | custom-call | tf_op jit(solution)/shard_map/dispatch/pallas_call | solution.py:103
  4.0 7.3 %all-to-all-start = ((bf16[32,72,128]{2,1,0:T(8,128)(2,1)}), bf16[32,72,128]{2,1,0:T(8,128)(2,1)S(1)}, u32[]{:S(2)}, u32[]{:S(2)}) async-start(bf16[32,72,128]{2,1,0:T(8,128)(2,1)} %dispatch.1), calls=%async_computation | async-start | bytes 1179648 | tf_op jit(solution)/shard_map/all_to_all | solution.py:432
  11.5 0.7 copy-done.5
  12.1 0.7 copy-done.6
  12.8 5.0 %dequantize.1 = (bf16[256,2048]{1,0:T(8,128)(2,1)S(1)}, bf16[256,2048]{1,0:T(8,128)(2,1)}, bf16[256,2048]{1,0:T(8,128)(2,1)}, bf16[256,2048]{1,0:T(8,128)(2,1)}) custom-call(s32[2]{0:T(128)S(1)} %pad_add_fusion.place_ref, s32[8,16]{1,0:T(8,128)S(1)} %copy-done.5, f32[8,16]{1,0:T(8,128)S(1)} %copy-done.6, bf16[1024,2048]{1,0:T(8,128)(2,1)} %values_ref.1), custom_call_target="tpu_custom_call" | custom-call | flops 2097152 | bytes 8388608 | tf_op jit(solution)/shard_map/dequantize/pallas_call | solution.py:227
  17.9 1.0 %copy-done = bf16[256,2048]{1,0:T(8,128)(2,1)} copy-done((bf16[256,2048]{1,0:T(8,128)(2,1)}, bf16[256,2048]{1,0:T(8,128)(2,1)S(1)}, u32[]{:S(2)}) %copy-start) | copy-done | bytes 1048600
  18.9 8.0 %all-to-all-done.recv_ref = bf16[32,72,128]{2,1,0:T(8,128)(2,1)S(1)} async-done(((bf16[32,72,128]{2,1,0:T(8,128)(2,1)}), bf16[32,72,128]{2,1,0:T(8,128)(2,1)S(1)}, u32[]{:S(2)}, u32[]{:S(2)}) %all-to-all-start) | async-done | bytes 589856 | tf_op jit(solution)/shard_map/all_to_all | solution.py:432
  26.9 2.2 %segment.1 = (bf16[256,128]{1,0:T(8,128)(2,1)S(1)}, bf16[128,256]{1,0:T(8,128)(2,1)S(1)}, bf16[256,128]{1,0:T(8,128)(2,1)S(1)}, bf16[256,2048]{1,0:T(8,128)(2,1)...) custom-call(bf16[32,72,128]{2,1,0:T(8,128)(2,1)S(1)} %all-to-all-done.recv_ref, ...), custom_call_target="tpu_custom_call" | custom-call | tf_op jit(solution)/shard_map/segment/pallas_call | solution.py:162
  29.1 3.1 %collective-permute-start.12 = (bf16[128,256]{1,0:T(8,128)(2,1)S(1)}, bf16[128,256]{1,0:T(8,128)(2,1)S(1)}, u32[]{:S(2)}, u32[]{:S(2)}) collective-permute-start(bf16[128,256]{1,0:T(8,128)(2,1)S(1)} %get-tuple-element.51.refs_4_), channel_id=1, source_target_pairs={{0,3},{1,2},{2,1},{3,0},{4,7},{5,6},{6,5},{7,4},{8,11},{9,10},{10,... | collective-permute-start | bytes 196616 | tf_op jit(solution)/shard_map/ppermute | solution.py:386
  32.2 1.1 %collective-permute-start.11 = (bf16[128,256]{1,0:T(8,128)(2,1)S(1)}, bf16[128,256]{1,0:T(8,128)(2,1)S(1)}, u32[]{:S(2)}, u32[]{:S(2)}) collective-permute-start(bf16[128,256]{1,0:T(8,128)(2,1)S(1)} %get-tuple-element.51.refs_4_), channel_id=1, source_target_pairs={{0,2},{1,3},{2,0},{3,1},{4,6},{5,7},{6,4},{7,5},{8,10},{9,11},{10,... | collective-permute-start | bytes 196616 | tf_op jit(solution)/shard_map/ppermute | solution.py:386
  33.3 0.7 collective-permute-start.2
  34.1 1.1 %collective-permute-start.1 = (bf16[256,128]{1,0:T(8,128)(2,1)S(1)}, bf16[256,128]{1,0:T(8,128)(2,1)S(1)}, u32[]{:S(2)}, u32[]{:S(2)}) collective-permute-start(bf16[256,128]{1,0:T(8,128)(2,1)S(1)} %get-tuple-element.45.refs_4_.own_ref), channel_id=1, source_target_pairs={{0,16},{4,20},{8,24},{12,28},{16,0},{20,4},{24,8},{28,12},{1,17},{... | collective-permute-start | bytes 196616 | tf_op jit(solution)/shard_map/ppermute | solution.py:386
  35.1 1.7 %collective-permute-start = (bf16[256,128]{1,0:T(8,128)(2,1)S(1)}, bf16[256,128]{1,0:T(8,128)(2,1)S(1)}, u32[]{:S(2)}, u32[]{:S(2)}) collective-permute-start(bf16[256,128]{1,0:T(8,128)(2,1)S(1)} %get-tuple-element.45.refs_4_.own_ref), channel_id=1, source_target_pairs={{0,8},{4,12},{8,0},{12,4},{16,24},{20,28},{24,16},{28,20},{1,9},{5... | collective-permute-start | bytes 196616 | tf_op jit(solution)/shard_map/ppermute | solution.py:386
  36.8 2.5 %collective-permute-start.10 = (bf16[128,256]{1,0:T(8,128)(2,1)S(1)}, bf16[128,256]{1,0:T(8,128)(2,1)S(1)}, u32[]{:S(2)}, u32[]{:S(2)}) collective-permute-start(bf16[128,256]{1,0:T(8,128)(2,1)S(1)} %get-tuple-element.51.refs_4_), channel_id=1, source_target_pairs={{0,1},{1,0},{2,3},{3,2},{4,5},{5,4},{6,7},{7,6},{8,9},{9,8},{10,11... | collective-permute-start | bytes 196616 | tf_op jit(solution)/shard_map/ppermute | solution.py:386
  39.6 0.5 collective-permute-start.6
  40.1 0.4 collective-permute-start.4
  40.6 1.0 %collective-permute-done.10.refs_5_ = bf16[128,256]{1,0:T(8,128)(2,1)S(1)} collective-permute-done((bf16[128,256]{1,0:T(8,128)(2,1)S(1)}, bf16[128,256]{1,0:T(8,128)(2,1)S(1)}, u32[]{:S(2)}, u32[]{:S(2)}) %collective-permute-start.10) | collective-permute-done | bytes 65568 | tf_op jit(solution)/shard_map/ppermute | solution.py:386
  41.6 0.7 item_sums.2
  42.4 1.3 %user_sums.2 = (bf16[256,128]{1,0:T(8,128)(2,1)S(1)}, bf16[256,128]{1,0:T(8,128)(2,1)S(1)}, bf16[256,128]{1,0:T(8,128)(2,1)S(1)}, bf16[256,128]{1,0:T(8,128)(2,1)S(1)}) custom-call(bf16[256,2048]{1,0:T(8,128)(2,1)S(1)} %get-tuple-element.41.refs_0_, bf16[256,2048]{1,0:T(8,128)(2,1)S(1)} %get-tuple-element.42.refs_1_, ...), custom_call_target="tpu_custom_call" | custom-call | flops 536870912 | bytes 4194304 | tf_op jit(solution)/shard_map/user_sums/pallas_call | solution.py:257
  43.7 2.1 %collective-permute-start.7 = (bf16[256,128]{1,0:T(8,128)(2,1)S(1)}, bf16[256,128]{1,0:T(8,128)(2,1)S(1)}, u32[]{:S(2)}, u32[]{:S(2)}) collective-permute-start(bf16[256,128]{1,0:T(8,128)(2,1)S(1)} %get-tuple-element.47), channel_id=1, source_target_pairs={{0,1},{1,0},{2,3},{3,2},{4,5},{5,4},{6,7},{7,6},{8,9},{9,8},{10,11... | collective-permute-start | bytes 196616 | tf_op jit(solution)/shard_map/ppermute | solution.py:386
  45.8 2.4 %collective-permute-start.9 = (bf16[256,128]{1,0:T(8,128)(2,1)S(1)}, bf16[256,128]{1,0:T(8,128)(2,1)S(1)}, u32[]{:S(2)}, u32[]{:S(2)}) collective-permute-start(bf16[256,128]{1,0:T(8,128)(2,1)S(1)} %get-tuple-element.49), channel_id=1, source_target_pairs={{0,3},{1,2},{2,1},{3,0},{4,7},{5,6},{6,5},{7,4},{8,11},{9,10},{10,... | collective-permute-start | bytes 196616 | tf_op jit(solution)/shard_map/ppermute | solution.py:386
  48.2 0.3 collective-permute-done.7.refs_1_
  48.5 5.1 %collective-permute-done.8.refs_2_ = bf16[256,128]{1,0:T(8,128)(2,1)S(1)} collective-permute-done((bf16[256,128]{1,0:T(8,128)(2,1)S(1)}, bf16[256,128]{1,0:T(8,128)(2,1)S(1)}, u32[]{:S(2)}, u32[]{:S(2)}) %collective-permute-start.8) | collective-permute-done | bytes 65568 | tf_op jit(solution)/shard_map/ppermute | solution.py:386
  53.9 1.5 %collective-permute-start.29 = (bf16[128,256]{1,0:T(8,128)(2,1)S(1)}, bf16[128,256]{1,0:T(8,128)(2,1)S(1)}, u32[]{:S(2)}, u32[]{:S(2)}) collective-permute-start(bf16[128,256]{1,0:T(8,128)(2,1)S(1)} %get-tuple-element.63.refs_4_), channel_id=1, source_target_pairs={{0,3},{1,2},{2,1},{3,0},{4,7},{5,6},{6,5},{7,4},{8,11},{9,10},{10,... | collective-permute-start | bytes 196616 | tf_op jit(solution)/shard_map/ppermute | solution.py:386
  55.3 1.9 %collective-permute-start.28 = (bf16[128,256]{1,0:T(8,128)(2,1)S(1)}, bf16[128,256]{1,0:T(8,128)(2,1)S(1)}, u32[]{:S(2)}, u32[]{:S(2)}) collective-permute-start(bf16[128,256]{1,0:T(8,128)(2,1)S(1)} %get-tuple-element.63.refs_4_), channel_id=1, source_target_pairs={{0,2},{1,3},{2,0},{3,1},{4,6},{5,7},{6,4},{7,5},{8,10},{9,11},{10,... | collective-permute-start | bytes 196616 | tf_op jit(solution)/shard_map/ppermute | solution.py:386
  57.3 1.0 %collective-permute-start.27 = (bf16[128,256]{1,0:T(8,128)(2,1)S(1)}, bf16[128,256]{1,0:T(8,128)(2,1)S(1)}, u32[]{:S(2)}, u32[]{:S(2)}) collective-permute-start(bf16[128,256]{1,0:T(8,128)(2,1)S(1)} %get-tuple-element.63.refs_4_), channel_id=1, source_target_pairs={{0,1},{1,0},{2,3},{3,2},{4,5},{5,4},{6,7},{7,6},{8,9},{9,8},{10,11... | collective-permute-start | bytes 196616 | tf_op jit(solution)/shard_map/ppermute | solution.py:386
  58.3 2.4 %collective-permute-done.29.refs_7_ = bf16[128,256]{1,0:T(8,128)(2,1)S(1)} collective-permute-done((bf16[128,256]{1,0:T(8,128)(2,1)S(1)}, bf16[128,256]{1,0:T(8,128)(2,1)S(1)}, u32[]{:S(2)}, u32[]{:S(2)}) %collective-permute-start.29) | collective-permute-done | bytes 65568 | tf_op jit(solution)/shard_map/ppermute | solution.py:386
  60.7 2.8 %collective-permute-done.28.refs_6_ = bf16[128,256]{1,0:T(8,128)(2,1)S(1)} collective-permute-done((bf16[128,256]{1,0:T(8,128)(2,1)S(1)}, bf16[128,256]{1,0:T(8,128)(2,1)S(1)}, u32[]{:S(2)}, u32[]{:S(2)}) %collective-permute-start.28) | collective-permute-done | bytes 65568 | tf_op jit(solution)/shard_map/ppermute | solution.py:386
  63.5 0.7 item_sums.3
  64.8 3.2 %collective-permute-start.16 = (bf16[128,256]{1,0:T(8,128)(2,1)S(1)}, bf16[128,256]{1,0:T(8,128)(2,1)S(1)}, u32[]{:S(2)}, u32[]{:S(2)}) collective-permute-start(bf16[128,256]{1,0:T(8,128)(2,1)S(1)} %get-tuple-element.57), channel_id=1, source_target_pairs={{0,24},{4,28},{8,16},{12,20},{16,8},{20,12},{24,0},{28,4},{1,25},{... | collective-permute-start | bytes 196616 | tf_op jit(solution)/shard_map/ppermute | solution.py:386
  67.9 1.1 %collective-permute-done.14.refs_1_ = bf16[128,256]{1,0:T(8,128)(2,1)S(1)} collective-permute-done((bf16[128,256]{1,0:T(8,128)(2,1)S(1)}, bf16[128,256]{1,0:T(8,128)(2,1)S(1)}, u32[]{:S(2)}, u32[]{:S(2)}) %collective-permute-start.14) | collective-permute-done | bytes 65568 | tf_op jit(solution)/shard_map/ppermute | solution.py:386
  69.1 1.3 %collective-permute-done.15.refs_2_ = bf16[128,256]{1,0:T(8,128)(2,1)S(1)} collective-permute-done((bf16[128,256]{1,0:T(8,128)(2,1)S(1)}, bf16[128,256]{1,0:T(8,128)(2,1)S(1)}, u32[]{:S(2)}, u32[]{:S(2)}) %collective-permute-start.15) | collective-permute-done | bytes 65568 | tf_op jit(solution)/shard_map/ppermute | solution.py:386
  70.7 2.8 %collective-permute-start.19 = (bf16[256,128]{1,0:T(8,128)(2,1)S(1)}, bf16[256,128]{1,0:T(8,128)(2,1)S(1)}, u32[]{:S(2)}, u32[]{:S(2)}) collective-permute-start(bf16[256,128]{1,0:T(8,128)(2,1)S(1)} %item_update.2.refs_4_.own_ref), channel_id=1, source_target_pairs={{0,24},{4,28},{8,16},{12,20},{16,8},{20,12},{24,0},{28,4},{1,25},{... | collective-permute-start | bytes 196616 | tf_op jit(solution)/shard_map/ppermute | solution.py:386
  73.4 0.5 collective-permute-start.18
  73.9 0.3 collective-permute-start.17
  74.2 1.9 %collective-permute-done.19.refs_7_ = bf16[256,128]{1,0:T(8,128)(2,1)S(1)} collective-permute-done((bf16[256,128]{1,0:T(8,128)(2,1)S(1)}, bf16[256,128]{1,0:T(8,128)(2,1)S(1)}, u32[]{:S(2)}, u32[]{:S(2)}) %collective-permute-start.19) | collective-permute-done | bytes 65568 | tf_op jit(solution)/shard_map/ppermute | solution.py:386
  76.1 1.6 %collective-permute-done.18.refs_6_ = bf16[256,128]{1,0:T(8,128)(2,1)S(1)} collective-permute-done((bf16[256,128]{1,0:T(8,128)(2,1)S(1)}, bf16[256,128]{1,0:T(8,128)(2,1)S(1)}, u32[]{:S(2)}, u32[]{:S(2)}) %collective-permute-start.18) | collective-permute-done | bytes 65568 | tf_op jit(solution)/shard_map/ppermute | solution.py:386
  77.7 0.5 collective-permute-done.17.refs_5_
  78.3 0.8 collective-permute-start.31
  79.1 0.9 collective-permute-start.32
  80.0 1.8 %collective-permute-start.33 = (bf16[128,256]{1,0:T(8,128)(2,1)S(1)}, bf16[128,256]{1,0:T(8,128)(2,1)S(1)}, u32[]{:S(2)}, u32[]{:S(2)}) collective-permute-start(bf16[128,256]{1,0:T(8,128)(2,1)S(1)} %get-tuple-element.69), channel_id=1, source_target_pairs={{0,24},{4,28},{8,16},{12,20},{16,8},{20,12},{24,0},{28,4},{1,25},{... | collective-permute-start | bytes 196616 | tf_op jit(solution)/shard_map/ppermute | solution.py:386
  81.8 1.2 %user_sums.3 = (bf16[256,128]{1,0:T(8,128)(2,1)S(1)}, bf16[256,128]{1,0:T(8,128)(2,1)S(1)}, bf16[256,128]{1,0:T(8,128)(2,1)S(1)}, bf16[256,128]{1,0:T(8,128)(2,1)S(1)}) custom-call(bf16[256,2048]{1,0:T(8,128)(2,1)S(1)} %get-tuple-element.41.refs_0_, bf16[256,2048]{1,0:T(8,128)(2,1)S(1)} %get-tuple-element.42.refs_1_, ...), custom_call_target="tpu_custom_call" | custom-call | flops 536870912 | bytes 4194304 | tf_op jit(solution)/shard_map/user_sums/pallas_call | solution.py:257
  83.2 2.2 %collective-permute-start.25 = (bf16[256,128]{1,0:T(8,128)(2,1)S(1)}, bf16[256,128]{1,0:T(8,128)(2,1)S(1)}, u32[]{:S(2)}, u32[]{:S(2)}) collective-permute-start(bf16[256,128]{1,0:T(8,128)(2,1)S(1)} %get-tuple-element.60), channel_id=1, source_target_pairs={{0,2},{1,3},{2,0},{3,1},{4,6},{5,7},{6,4},{7,5},{8,10},{9,11},{10,... | collective-permute-start | bytes 196616 | tf_op jit(solution)/shard_map/ppermute | solution.py:386
  85.4 2.1 %collective-permute-start.26 = (bf16[256,128]{1,0:T(8,128)(2,1)S(1)}, bf16[256,128]{1,0:T(8,128)(2,1)S(1)}, u32[]{:S(2)}, u32[]{:S(2)}) collective-permute-start(bf16[256,128]{1,0:T(8,128)(2,1)S(1)} %get-tuple-element.61), channel_id=1, source_target_pairs={{0,3},{1,2},{2,1},{3,0},{4,7},{5,6},{6,5},{7,4},{8,11},{9,10},{10,... | collective-permute-start | bytes 196616 | tf_op jit(solution)/shard_map/ppermute | solution.py:386
  87.5 0.9 item_update.3
  88.4 2.2 %collective-permute-done.25.refs_2_ = bf16[256,128]{1,0:T(8,128)(2,1)S(1)} collective-permute-done((bf16[256,128]{1,0:T(8,128)(2,1)S(1)}, bf16[256,128]{1,0:T(8,128)(2,1)S(1)}, u32[]{:S(2)}, u32[]{:S(2)}) %collective-permute-start.25) | collective-permute-done | bytes 65568 | tf_op jit(solution)/shard_map/ppermute | solution.py:386
  90.6 0.9 collective-permute-done.26.refs_3_
  91.5 0.9 user_update.3
  (50 shorter events, 1.7 us)
Async XLA Ops:
  4.0 22.9 %copy-start.3 = (bf16[64,128]{1,0:T(8,128)(2,1)S(1)}, bf16[64,128]{1,0:T(8,128)(2,1)}, u32[]{:S(2)}) copy-start(bf16[64,128]{1,0:T(8,128)(2,1)} %proj_wide_ref.1) | copy-start | bytes 49156
  4.0 22.9 %copy-start.4 = (bf16[32,128]{1,0:T(8,128)(2,1)S(1)}, bf16[32,128]{1,0:T(8,128)(2,1)}, u32[]{:S(2)}) copy-start(bf16[32,128]{1,0:T(8,128)(2,1)} %proj_narrow_ref.1) | copy-start | bytes 24580
  4.0 22.9 %all-to-all-start = ((bf16[32,72,128]{2,1,0:T(8,128)(2,1)}), bf16[32,72,128]{2,1,0:T(8,128)(2,1)S(1)}, u32[]{:S(2)}, u32[]{:S(2)}) async-start(bf16[32,72,128]{2,1,0:T(8,128)(2,1)} %dispatch.1), calls=%async_computation | async-start | bytes 1179648 | tf_op jit(solution)/shard_map/all_to_all | solution.py:432
  11.5 0.7 copy-start.5
  12.1 0.7 copy-start.6
  17.9 1.0 %copy-start = (bf16[256,2048]{1,0:T(8,128)(2,1)}, bf16[256,2048]{1,0:T(8,128)(2,1)S(1)}, u32[]{:S(2)}) copy-start(bf16[256,2048]{1,0:T(8,128)(2,1)S(1)} %get-tuple-element.36.refs_0_) | copy-start | bytes 3145732
  29.1 7.7 %collective-permute-start.12 = (bf16[128,256]{1,0:T(8,128)(2,1)S(1)}, bf16[128,256]{1,0:T(8,128)(2,1)S(1)}, u32[]{:S(2)}, u32[]{:S(2)}) collective-permute-start(bf16[128,256]{1,0:T(8,128)(2,1)S(1)} %get-tuple-element.51.refs_4_), channel_id=1, source_target_pairs={{0,3},{1,2},{2,1},{3,0},{4,7},{5,6},{6,5},{7,4},{8,11},{9,10},{10,... | collective-permute-start | bytes 196616 | tf_op jit(solution)/shard_map/ppermute | solution.py:386
  32.2 7.4 %collective-permute-start.11 = (bf16[128,256]{1,0:T(8,128)(2,1)S(1)}, bf16[128,256]{1,0:T(8,128)(2,1)S(1)}, u32[]{:S(2)}, u32[]{:S(2)}) collective-permute-start(bf16[128,256]{1,0:T(8,128)(2,1)S(1)} %get-tuple-element.51.refs_4_), channel_id=1, source_target_pairs={{0,2},{1,3},{2,0},{3,1},{4,6},{5,7},{6,4},{7,5},{8,10},{9,11},{10,... | collective-permute-start | bytes 196616 | tf_op jit(solution)/shard_map/ppermute | solution.py:386
  33.3 6.2 %collective-permute-start.2 = (bf16[256,128]{1,0:T(8,128)(2,1)S(1)}, bf16[256,128]{1,0:T(8,128)(2,1)S(1)}, u32[]{:S(2)}, u32[]{:S(2)}) collective-permute-start(bf16[256,128]{1,0:T(8,128)(2,1)S(1)} %get-tuple-element.45.refs_4_.own_ref), channel_id=1, source_target_pairs={{0,24},{4,28},{8,16},{12,20},{16,8},{20,12},{24,0},{28,4},{1,25},{... | collective-permute-start | bytes 196616 | tf_op jit(solution)/shard_map/ppermute | solution.py:386
  34.1 6.0 %collective-permute-start.1 = (bf16[256,128]{1,0:T(8,128)(2,1)S(1)}, bf16[256,128]{1,0:T(8,128)(2,1)S(1)}, u32[]{:S(2)}, u32[]{:S(2)}) collective-permute-start(bf16[256,128]{1,0:T(8,128)(2,1)S(1)} %get-tuple-element.45.refs_4_.own_ref), channel_id=1, source_target_pairs={{0,16},{4,20},{8,24},{12,28},{16,0},{20,4},{24,8},{28,12},{1,17},{... | collective-permute-start | bytes 196616 | tf_op jit(solution)/shard_map/ppermute | solution.py:386
  35.1 5.0 %collective-permute-start = (bf16[256,128]{1,0:T(8,128)(2,1)S(1)}, bf16[256,128]{1,0:T(8,128)(2,1)S(1)}, u32[]{:S(2)}, u32[]{:S(2)}) collective-permute-start(bf16[256,128]{1,0:T(8,128)(2,1)S(1)} %get-tuple-element.45.refs_4_.own_ref), channel_id=1, source_target_pairs={{0,8},{4,12},{8,0},{12,4},{16,24},{20,28},{24,16},{28,20},{1,9},{5... | collective-permute-start | bytes 196616 | tf_op jit(solution)/shard_map/ppermute | solution.py:386
  36.8 4.7 %collective-permute-start.10 = (bf16[128,256]{1,0:T(8,128)(2,1)S(1)}, bf16[128,256]{1,0:T(8,128)(2,1)S(1)}, u32[]{:S(2)}, u32[]{:S(2)}) collective-permute-start(bf16[128,256]{1,0:T(8,128)(2,1)S(1)} %get-tuple-element.51.refs_4_), channel_id=1, source_target_pairs={{0,1},{1,0},{2,3},{3,2},{4,5},{5,4},{6,7},{7,6},{8,9},{9,8},{10,11... | collective-permute-start | bytes 196616 | tf_op jit(solution)/shard_map/ppermute | solution.py:386
  39.6 2.8 %collective-permute-start.3 = (bf16[256,128]{1,0:T(8,128)(2,1)S(1)}, bf16[256,128]{1,0:T(8,128)(2,1)S(1)}, u32[]{:S(2)}, u32[]{:S(2)}) collective-permute-start(bf16[256,128]{1,0:T(8,128)(2,1)S(1)} %get-tuple-element.45.refs_4_.own_ref), channel_id=1, source_target_pairs={{0,4},{4,0},{8,12},{12,8},{16,20},{20,16},{24,28},{28,24},{1,5},{5... | collective-permute-start | bytes 196616 | tf_op jit(solution)/shard_map/ppermute | solution.py:391
  39.6 2.8 %collective-permute-start.6 = (bf16[256,128]{1,0:T(8,128)(2,1)S(1)}, bf16[256,128]{1,0:T(8,128)(2,1)S(1)}, u32[]{:S(2)}, u32[]{:S(2)}) collective-permute-start(bf16[256,128]{1,0:T(8,128)(2,1)S(1)} %collective-permute-done.2.refs_7_), channel_id=1, source_target_pairs={{0,4},{4,0},{8,12},{12,8},{16,20},{20,16},{24,28},{28,24},{1,5},{5... | collective-permute-start | bytes 196616 | tf_op jit(solution)/shard_map/ppermute | solution.py:391
  40.1 2.3 %collective-permute-start.5 = (bf16[256,128]{1,0:T(8,128)(2,1)S(1)}, bf16[256,128]{1,0:T(8,128)(2,1)S(1)}, u32[]{:S(2)}, u32[]{:S(2)}) collective-permute-start(bf16[256,128]{1,0:T(8,128)(2,1)S(1)} %collective-permute-done.1.refs_6_), channel_id=1, source_target_pairs={{0,4},{4,0},{8,12},{12,8},{16,20},{20,16},{24,28},{28,24},{1,5},{5... | collective-permute-start | bytes 196616 | tf_op jit(solution)/shard_map/ppermute | solution.py:391
  40.1 2.3 %collective-permute-start.4 = (bf16[256,128]{1,0:T(8,128)(2,1)S(1)}, bf16[256,128]{1,0:T(8,128)(2,1)S(1)}, u32[]{:S(2)}, u32[]{:S(2)}) collective-permute-start(bf16[256,128]{1,0:T(8,128)(2,1)S(1)} %collective-permute-done.refs_5_), channel_id=1, source_target_pairs={{0,4},{4,0},{8,12},{12,8},{16,20},{20,16},{24,28},{28,24},{1,5},{5... | collective-permute-start | bytes 196616 | tf_op jit(solution)/shard_map/ppermute | solution.py:391
  41.6 12.0 %copy-start.1 = (bf16[2,128,128]{2,1,0:T(8,128)(2,1)S(1)}, bf16[2,128,128]{2,1,0:T(8,128)(2,1)}, u32[]{:S(2)}) copy-start(bf16[2,128,128]{2,1,0:T(8,128)(2,1)} %sum_ref.7) | copy-start | bytes 196612
  41.6 12.0 %copy-start.2 = (bf16[2,128,128]{2,1,0:T(8,128)(2,1)S(1)}, bf16[2,128,128]{2,1,0:T(8,128)(2,1)}, u32[]{:S(2)}) copy-start(bf16[2,128,128]{2,1,0:T(8,128)(2,1)} %product_ref.7) | copy-start | bytes 196612
  42.3 22.0 %collective-permute-start.13 = (bf16[4,128,256]{2,1,0:T(8,128)(2,1)S(1)}, bf16[4,128,256]{2,1,0:T(8,128)(2,1)S(1)}, u32[]{:S(2)}, u32[]{:S(2)}) collective-permute-start(bf16[4,128,256]{2,1,0:T(8,128)(2,1)S(1)} %get-tuple-element.53), channel_id=1, source_target_pairs={{0,4},{4,0},{8,12},{12,8},{16,20},{20,16},{24,28},{28,24},{1,5},{5... | collective-permute-start | bytes 786440 | tf_op jit(solution)/shard_map/ppermute | solution.py:391
  43.7 4.8 %collective-permute-start.7 = (bf16[256,128]{1,0:T(8,128)(2,1)S(1)}, bf16[256,128]{1,0:T(8,128)(2,1)S(1)}, u32[]{:S(2)}, u32[]{:S(2)}) collective-permute-start(bf16[256,128]{1,0:T(8,128)(2,1)S(1)} %get-tuple-element.47), channel_id=1, source_target_pairs={{0,1},{1,0},{2,3},{3,2},{4,5},{5,4},{6,7},{7,6},{8,9},{9,8},{10,11... | collective-permute-start | bytes 196616 | tf_op jit(solution)/shard_map/ppermute | solution.py:386
  45.8 7.8 %collective-permute-start.8 = (bf16[256,128]{1,0:T(8,128)(2,1)S(1)}, bf16[256,128]{1,0:T(8,128)(2,1)S(1)}, u32[]{:S(2)}, u32[]{:S(2)}) collective-permute-start(bf16[256,128]{1,0:T(8,128)(2,1)S(1)} %get-tuple-element.48), channel_id=1, source_target_pairs={{0,2},{1,3},{2,0},{3,1},{4,6},{5,7},{6,4},{7,5},{8,10},{9,11},{10,... | collective-permute-start | bytes 196616 | tf_op jit(solution)/shard_map/ppermute | solution.py:386
  45.8 7.8 %collective-permute-start.9 = (bf16[256,128]{1,0:T(8,128)(2,1)S(1)}, bf16[256,128]{1,0:T(8,128)(2,1)S(1)}, u32[]{:S(2)}, u32[]{:S(2)}) collective-permute-start(bf16[256,128]{1,0:T(8,128)(2,1)S(1)} %get-tuple-element.49), channel_id=1, source_target_pairs={{0,3},{1,2},{2,1},{3,0},{4,7},{5,6},{6,5},{7,4},{8,11},{9,10},{10,... | collective-permute-start | bytes 196616 | tf_op jit(solution)/shard_map/ppermute | solution.py:386
  53.9 6.8 %collective-permute-start.29 = (bf16[128,256]{1,0:T(8,128)(2,1)S(1)}, bf16[128,256]{1,0:T(8,128)(2,1)S(1)}, u32[]{:S(2)}, u32[]{:S(2)}) collective-permute-start(bf16[128,256]{1,0:T(8,128)(2,1)S(1)} %get-tuple-element.63.refs_4_), channel_id=1, source_target_pairs={{0,3},{1,2},{2,1},{3,0},{4,7},{5,6},{6,5},{7,4},{8,11},{9,10},{10,... | collective-permute-start | bytes 196616 | tf_op jit(solution)/shard_map/ppermute | solution.py:386
  55.3 8.2 %collective-permute-start.28 = (bf16[128,256]{1,0:T(8,128)(2,1)S(1)}, bf16[128,256]{1,0:T(8,128)(2,1)S(1)}, u32[]{:S(2)}, u32[]{:S(2)}) collective-permute-start(bf16[128,256]{1,0:T(8,128)(2,1)S(1)} %get-tuple-element.63.refs_4_), channel_id=1, source_target_pairs={{0,2},{1,3},{2,0},{3,1},{4,6},{5,7},{6,4},{7,5},{8,10},{9,11},{10,... | collective-permute-start | bytes 196616 | tf_op jit(solution)/shard_map/ppermute | solution.py:386
  57.3 6.2 %collective-permute-start.27 = (bf16[128,256]{1,0:T(8,128)(2,1)S(1)}, bf16[128,256]{1,0:T(8,128)(2,1)S(1)}, u32[]{:S(2)}, u32[]{:S(2)}) collective-permute-start(bf16[128,256]{1,0:T(8,128)(2,1)S(1)} %get-tuple-element.63.refs_4_), channel_id=1, source_target_pairs={{0,1},{1,0},{2,3},{3,2},{4,5},{5,4},{6,7},{7,6},{8,9},{9,8},{10,11... | collective-permute-start | bytes 196616 | tf_op jit(solution)/shard_map/ppermute | solution.py:386
  64.2 14.0 %collective-permute-start.30 = (bf16[4,128,256]{2,1,0:T(8,128)(2,1)S(1)}, bf16[4,128,256]{2,1,0:T(8,128)(2,1)S(1)}, u32[]{:S(2)}, u32[]{:S(2)}) collective-permute-start(bf16[4,128,256]{2,1,0:T(8,128)(2,1)S(1)} %get-tuple-element.65), channel_id=1, source_target_pairs={{0,4},{4,0},{8,12},{12,8},{16,20},{20,16},{24,28},{28,24},{1,5},{5... | collective-permute-start | bytes 786440 | tf_op jit(solution)/shard_map/ppermute | solution.py:391
  64.4 4.7 %collective-permute-start.14 = (bf16[128,256]{1,0:T(8,128)(2,1)S(1)}, bf16[128,256]{1,0:T(8,128)(2,1)S(1)}, u32[]{:S(2)}, u32[]{:S(2)}) collective-permute-start(bf16[128,256]{1,0:T(8,128)(2,1)S(1)} %get-tuple-element.55), channel_id=1, source_target_pairs={{0,8},{4,12},{8,0},{12,4},{16,24},{20,28},{24,16},{28,20},{1,9},{5... | collective-permute-start | bytes 196616 | tf_op jit(solution)/shard_map/ppermute | solution.py:386
  64.5 6.0 %collective-permute-start.15 = (bf16[128,256]{1,0:T(8,128)(2,1)S(1)}, bf16[128,256]{1,0:T(8,128)(2,1)S(1)}, u32[]{:S(2)}, u32[]{:S(2)}) collective-permute-start(bf16[128,256]{1,0:T(8,128)(2,1)S(1)} %get-tuple-element.56), channel_id=1, source_target_pairs={{0,16},{4,20},{8,24},{12,28},{16,0},{20,4},{24,8},{28,12},{1,17},{... | collective-permute-start | bytes 196616 | tf_op jit(solution)/shard_map/ppermute | solution.py:386
  64.8 5.7 %collective-permute-start.16 = (bf16[128,256]{1,0:T(8,128)(2,1)S(1)}, bf16[128,256]{1,0:T(8,128)(2,1)S(1)}, u32[]{:S(2)}, u32[]{:S(2)}) collective-permute-start(bf16[128,256]{1,0:T(8,128)(2,1)S(1)} %get-tuple-element.57), channel_id=1, source_target_pairs={{0,24},{4,28},{8,16},{12,20},{16,8},{20,12},{24,0},{28,4},{1,25},{... | collective-permute-start | bytes 196616 | tf_op jit(solution)/shard_map/ppermute | solution.py:386
  70.7 5.4 %collective-permute-start.19 = (bf16[256,128]{1,0:T(8,128)(2,1)S(1)}, bf16[256,128]{1,0:T(8,128)(2,1)S(1)}, u32[]{:S(2)}, u32[]{:S(2)}) collective-permute-start(bf16[256,128]{1,0:T(8,128)(2,1)S(1)} %item_update.2.refs_4_.own_ref), channel_id=1, source_target_pairs={{0,24},{4,28},{8,16},{12,20},{16,8},{20,12},{24,0},{28,4},{1,25},{... | collective-permute-start | bytes 196616 | tf_op jit(solution)/shard_map/ppermute | solution.py:386
  73.4 4.3 %collective-permute-start.18 = (bf16[256,128]{1,0:T(8,128)(2,1)S(1)}, bf16[256,128]{1,0:T(8,128)(2,1)S(1)}, u32[]{:S(2)}, u32[]{:S(2)}) collective-permute-start(bf16[256,128]{1,0:T(8,128)(2,1)S(1)} %item_update.2.refs_4_.own_ref), channel_id=1, source_target_pairs={{0,16},{4,20},{8,24},{12,28},{16,0},{20,4},{24,8},{28,12},{1,17},{... | collective-permute-start | bytes 196616 | tf_op jit(solution)/shard_map/ppermute | solution.py:386
  73.9 4.3 %collective-permute-start.17 = (bf16[256,128]{1,0:T(8,128)(2,1)S(1)}, bf16[256,128]{1,0:T(8,128)(2,1)S(1)}, u32[]{:S(2)}, u32[]{:S(2)}) collective-permute-start(bf16[256,128]{1,0:T(8,128)(2,1)S(1)} %item_update.2.refs_4_.own_ref), channel_id=1, source_target_pairs={{0,8},{4,12},{8,0},{12,4},{16,24},{20,28},{24,16},{28,20},{1,9},{5... | collective-permute-start | bytes 196616 | tf_op jit(solution)/shard_map/ppermute | solution.py:386
  74.2 4.9 %collective-permute-start.20 = (bf16[256,128]{1,0:T(8,128)(2,1)S(1)}, bf16[256,128]{1,0:T(8,128)(2,1)S(1)}, u32[]{:S(2)}, u32[]{:S(2)}) collective-permute-start(bf16[256,128]{1,0:T(8,128)(2,1)S(1)} %item_update.2.refs_4_.own_ref), channel_id=1, source_target_pairs={{0,4},{4,0},{8,12},{12,8},{16,20},{20,16},{24,28},{28,24},{1,5},{5... | collective-permute-start | bytes 196616 | tf_op jit(solution)/shard_map/ppermute | solution.py:391
  76.1 3.9 %collective-permute-start.23 = (bf16[256,128]{1,0:T(8,128)(2,1)S(1)}, bf16[256,128]{1,0:T(8,128)(2,1)S(1)}, u32[]{:S(2)}, u32[]{:S(2)}) collective-permute-start(bf16[256,128]{1,0:T(8,128)(2,1)S(1)} %collective-permute-done.19.refs_7_), channel_id=1, source_target_pairs={{0,4},{4,0},{8,12},{12,8},{16,20},{20,16},{24,28},{28,24},{1,5},{5... | collective-permute-start | bytes 196616 | tf_op jit(solution)/shard_map/ppermute | solution.py:391
  77.7 4.1 %collective-permute-start.22 = (bf16[256,128]{1,0:T(8,128)(2,1)S(1)}, bf16[256,128]{1,0:T(8,128)(2,1)S(1)}, u32[]{:S(2)}, u32[]{:S(2)}) collective-permute-start(bf16[256,128]{1,0:T(8,128)(2,1)S(1)} %collective-permute-done.18.refs_6_), channel_id=1, source_target_pairs={{0,4},{4,0},{8,12},{12,8},{16,20},{20,16},{24,28},{28,24},{1,5},{5... | collective-permute-start | bytes 196616 | tf_op jit(solution)/shard_map/ppermute | solution.py:391
  78.2 3.6 %collective-permute-start.21 = (bf16[256,128]{1,0:T(8,128)(2,1)S(1)}, bf16[256,128]{1,0:T(8,128)(2,1)S(1)}, u32[]{:S(2)}, u32[]{:S(2)}) collective-permute-start(bf16[256,128]{1,0:T(8,128)(2,1)S(1)} %collective-permute-done.17.refs_5_), channel_id=1, source_target_pairs={{0,4},{4,0},{8,12},{12,8},{16,20},{20,16},{24,28},{28,24},{1,5},{5... | collective-permute-start | bytes 196616 | tf_op jit(solution)/shard_map/ppermute | solution.py:391
  78.3 7.1 %collective-permute-start.31 = (bf16[128,256]{1,0:T(8,128)(2,1)S(1)}, bf16[128,256]{1,0:T(8,128)(2,1)S(1)}, u32[]{:S(2)}, u32[]{:S(2)}) collective-permute-start(bf16[128,256]{1,0:T(8,128)(2,1)S(1)} %get-tuple-element.67), channel_id=1, source_target_pairs={{0,8},{4,12},{8,0},{12,4},{16,24},{20,28},{24,16},{28,20},{1,9},{5... | collective-permute-start | bytes 196616 | tf_op jit(solution)/shard_map/ppermute | solution.py:386
  79.1 8.5 %collective-permute-start.32 = (bf16[128,256]{1,0:T(8,128)(2,1)S(1)}, bf16[128,256]{1,0:T(8,128)(2,1)S(1)}, u32[]{:S(2)}, u32[]{:S(2)}) collective-permute-start(bf16[128,256]{1,0:T(8,128)(2,1)S(1)} %get-tuple-element.68), channel_id=1, source_target_pairs={{0,16},{4,20},{8,24},{12,28},{16,0},{20,4},{24,8},{28,12},{1,17},{... | collective-permute-start | bytes 196616 | tf_op jit(solution)/shard_map/ppermute | solution.py:386
  80.0 7.5 %collective-permute-start.33 = (bf16[128,256]{1,0:T(8,128)(2,1)S(1)}, bf16[128,256]{1,0:T(8,128)(2,1)S(1)}, u32[]{:S(2)}, u32[]{:S(2)}) collective-permute-start(bf16[128,256]{1,0:T(8,128)(2,1)S(1)} %get-tuple-element.69), channel_id=1, source_target_pairs={{0,24},{4,28},{8,16},{12,20},{16,8},{20,12},{24,0},{28,4},{1,25},{... | collective-permute-start | bytes 196616 | tf_op jit(solution)/shard_map/ppermute | solution.py:386
  83.1 5.3 %collective-permute-start.24 = (bf16[256,128]{1,0:T(8,128)(2,1)S(1)}, bf16[256,128]{1,0:T(8,128)(2,1)S(1)}, u32[]{:S(2)}, u32[]{:S(2)}) collective-permute-start(bf16[256,128]{1,0:T(8,128)(2,1)S(1)} %get-tuple-element.59), channel_id=1, source_target_pairs={{0,1},{1,0},{2,3},{3,2},{4,5},{5,4},{6,7},{7,6},{8,9},{9,8},{10,11... | collective-permute-start | bytes 196616 | tf_op jit(solution)/shard_map/ppermute | solution.py:386
  83.2 7.4 %collective-permute-start.25 = (bf16[256,128]{1,0:T(8,128)(2,1)S(1)}, bf16[256,128]{1,0:T(8,128)(2,1)S(1)}, u32[]{:S(2)}, u32[]{:S(2)}) collective-permute-start(bf16[256,128]{1,0:T(8,128)(2,1)S(1)} %get-tuple-element.60), channel_id=1, source_target_pairs={{0,2},{1,3},{2,0},{3,1},{4,6},{5,7},{6,4},{7,5},{8,10},{9,11},{10,... | collective-permute-start | bytes 196616 | tf_op jit(solution)/shard_map/ppermute | solution.py:386
  85.4 6.1 %collective-permute-start.26 = (bf16[256,128]{1,0:T(8,128)(2,1)S(1)}, bf16[256,128]{1,0:T(8,128)(2,1)S(1)}, u32[]{:S(2)}, u32[]{:S(2)}) collective-permute-start(bf16[256,128]{1,0:T(8,128)(2,1)S(1)} %get-tuple-element.61), channel_id=1, source_target_pairs={{0,3},{1,2},{2,1},{3,0},{4,7},{5,6},{6,5},{7,4},{8,11},{9,10},{10,... | collective-permute-start | bytes 196616 | tf_op jit(solution)/shard_map/ppermute | solution.py:386
where the time goes:
time: 92.7 us; the launch traced here: 92.4 us
  starting transfers between devices  42.8 us (46%)
  waiting for transfers between devices  29.3 us (32%)
  Pallas kernels  17 us (18%)
  local copies, waits for them, and re-layouts  2.36 us (3%)
    ppermute x24, starting transfers between devices, exchange(): received.append(lax.ppermute(blocks[k], axis, pairs))  34.3 us
    ppermute x24, waiting for transfers between devices, exchange(): received.append(lax.ppermute(blocks[k], axis, pairs))  21.3 us
    all_to_all x1, waiting for transfers between devices, per_device(): lax.all_to_all(send, ('row', 'col'), split_axis=0, concat_axis=0, tiled=T...  8.03 us
    all_to_all x1, starting transfers between devices, per_device(): lax.all_to_all(send, ('row', 'col'), split_axis=0, concat_axis=0, tiled=T...  7.33 us
    pallas_call x1, Pallas kernels, dequantize(): pl.pallas_call(functools.partial(dequantize_kernel, shape), out_shape=(ja...  5.04 us
    pallas_call x1, Pallas kernels, dispatch(): pl.pallas_call(functools.partial(dispatch_kernel, devices, slots), out_sh...  3.37 us
    pallas_call x2, Pallas kernels, user_sums(): pl.pallas_call(functools.partial(user_sum_kernel, cols), out_shape=(jax.S...  2.5 us
    unnamed x14, local copies, waits for them, and re-layouts  2.36 us
  transfers between devices with their start and end apart: 35, of which 14 were waited for; matrix products, arithmetic and copies ran while one was open for 0% of the time, Pallas kernels for 11%

commit v1 on v0

--- a/solution.py
+++ b/solution.py
@@ -11,6 +11,7 @@
 TILE = 128
 LANES = 128
 CODE_ROWS = 8
+GROUP = 8
 F32 = jnp.float32
 BF16 = jnp.bfloat16
 NT = (((1,), (1,)), ((), ()))
@@ -40,12 +41,71 @@
     return pltpu.CompilerParams(vmem_limit_bytes=52 * 2**20)
 
 
-def dispatch_kernel(devices, slots, *refs):
-    sources, out_ref, (raw_ref, dest_ref, slot_ref, wide_ref), sems = (
+def chunks_of(capacity, features):
+    chunks, base, row = [], 0, 0
+    size = LANES // 2
+    while base < capacity:
+        while size > max(8, capacity - base):
+            size //= 2
+        height = features * size // LANES
+        chunks.append((base, size, row, height))
+        base += size
+        row += height
+    return chunks, -(-row // CODE_ROWS) * CODE_ROWS
+
+
+def turned(block, shift):
+    shift = shift % LANES
+    return block if shift == 0 else pltpu.roll(block, shift, 1)
+
+
+def packed(placed, codes, capacity):
+    features = placed.shape[0]
+    chunks, code_row = chunks_of(capacity, features)
+    lane = lax.broadcasted_iota(jnp.int32, (1, LANES), 1)
+    blocks, code_rows, height = [], jnp.zeros((CODE_ROWS, LANES), F32), 0
+    code = lax.broadcasted_iota(jnp.int32, (CODE_ROWS, LANES), 0)
+    for n, (base, size, row, rows) in enumerate(chunks):
+        block = None
+        for part in range(LANES // size):
+            piece = turned(placed[part * rows : (part + 1) * rows], part * size - base)
+            here = lane >= part * size
+            block = piece if block is None else jnp.where(here, piece, block)
+        blocks.append(block)
+        height += rows
+        low = turned(codes, -base)[0:1]
+        high = turned(codes, size - base)[1:2]
+        both = jnp.where(lane < size, low, jnp.where(lane < 2 * size, high, 0.0))
+        code_rows = jnp.where(code == n, both, code_rows)
+    if height < code_row:
+        blocks.append(jnp.zeros((code_row - height, LANES), F32))
+    return jnp.concatenate([*blocks, code_rows], axis=0)
+
+
+def unpacked(block, features, capacity):
+    chunks, code_row = chunks_of(capacity, features)
+    lane = lax.broadcasted_iota(jnp.int32, (1, LANES), 1)
+    placed = jnp.zeros((features, LANES), F32)
+    low = jnp.zeros((1, LANES), F32)
+    high = jnp.zeros((1, LANES), F32)
+    codes = block[code_row:]
+    for n, (base, size, row, rows) in enumerate(chunks):
+        pieces = [
+            turned(block[row : row + rows], base - part * size) for part in range(LANES // size)
+        ]
+        here = (lane >= base) & (lane < min(base + size, capacity))
+        placed = jnp.where(here, jnp.concatenate(pieces, axis=0), placed)
+        low = jnp.where(here, turned(codes, base)[n : n + 1], low)
+        high = jnp.where(here, turned(codes, base - size)[n : n + 1], high)
+    return placed, low, high
+
+
+def dispatch_kernel(devices, capacity, *refs):
+    sources, out_ref, (raw_ref, dest_ref, slot_ref, wide_ref, held), (sems, out_sems) = (
         refs[:4],
         refs[4],
-        refs[5:9],
-        refs[9],
+        refs[5:10],
+        refs[10:],
     )
     copies = [
         pltpu.make_async_copy(source, ref, sems.at[n])
@@ -75,7 +135,7 @@
         base = base + counted[:, LANES:]
     rank = jnp.concatenate(ranks, axis=1)
     place = (
-        lax.broadcasted_iota(jnp.int32, (slots, rows), 0).astype(F32) == rank
+        lax.broadcasted_iota(jnp.int32, (LANES, rows), 0).astype(F32) == rank
     ).astype(F32).astype(BF16)
     for copy in (copies[0], copies[2], copies[3]):
         copy.wait()
@@ -83,39 +143,53 @@
     code = lax.broadcasted_iota(jnp.int32, (2 * CODE_ROWS, rows), 0)
     codes = jnp.where(
         code == 0,
-        slot // 256,
-        jnp.where(code == 1, slot % 256, jnp.where(code == 2, wide_ref[...], 0)),
+        slot % 256,
+        jnp.where(code == 1, slot // 256 * 2 + wide_ref[...], 0),
     )
     ext = jnp.concatenate([raw_ref[...], codes.astype(F32).astype(BF16)], axis=0)
-    group = 8
-    for first in range(0, devices, group):
+    height = ext.shape[0]
+    writes = []
+    for n, first in enumerate(range(0, devices, GROUP)):
         masked = jnp.concatenate(
-            [ext * hot_bf[d : d + 1, :] for d in range(first, first + group)], axis=0
+            [ext * hot_bf[d : d + 1, :] for d in range(first, first + GROUP)], axis=0
         )
-        placed = lax.dot_general(masked, place, NT, preferred_element_type=F32).astype(BF16)
-        for d in range(group):
-            start = d * (features + 2 * CODE_ROWS)
-            out_ref[first + d] = placed[start : start + features + CODE_ROWS]
-
-
-def dispatch(raw, dest, slot, wide, devices, slots):
+        placed = lax.dot_general(masked, place, NT, preferred_element_type=F32)
+        for d in range(GROUP):
+            mine = placed[d * height : (d + 1) * height]
+            held[first + d] = packed(
+                mine[:features], mine[features : features + CODE_ROWS], capacity
+            ).astype(BF16)
+        writes.append(
+            pltpu.make_async_copy(
+                held.at[pl.ds(first, GROUP)], out_ref.at[pl.ds(first, GROUP)], out_sems.at[n]
+            )
+        )
+        writes[-1].start()
+    for write in writes:
+        write.wait()
+
+
+def dispatch(raw, dest, slot, wide, devices, capacity):
     features, rows = raw.shape
-    return pl.pallas_call(
-        functools.partial(dispatch_kernel, devices, slots),
-        out_shape=jax.ShapeDtypeStruct((devices, features + CODE_ROWS, slots), BF16),
+    shape = (devices, chunks_of(capacity, features)[1] + CODE_ROWS, LANES)
+    return pl.pallas_call(
+        functools.partial(dispatch_kernel, devices, capacity),
+        out_shape=jax.ShapeDtypeStruct(shape, BF16),
         in_specs=[pl.BlockSpec(memory_space=pltpu.HBM)] * 4,
-        out_specs=vmem_spec(),
+        out_specs=pl.BlockSpec(memory_space=pltpu.HBM),
         scratch_shapes=[
             pltpu.VMEM(raw.shape, raw.dtype),
             *[pltpu.VMEM((1, rows), jnp.int32) for _ in range(3)],
+            pltpu.VMEM(shape, BF16),
             pltpu.SemaphoreType.DMA((4,)),
+            pltpu.SemaphoreType.DMA((devices // GROUP,)),
         ],
         compiler_params=whole_vmem(),
         name="dispatch",
     )(raw, dest, slot, wide)
 
 
-def segment_kernel(narrow, upd, cols, recv_ref, proj_narrow_ref, proj_wide_ref, *refs):
+def segment_kernel(capacity, upd, cols, recv_ref, proj_narrow_ref, proj_wide_ref, *refs):
     adj_refs, (user_ref, user_t_ref, item_ref) = refs[:cols], refs[cols : cols + 3]
     held_refs, sems = refs[cols + 3 : -1], refs[-1]
     copies = [
@@ -124,20 +198,22 @@
     ]
     for copy in copies:
         copy.start()
-    devices, height, slots = recv_ref.shape
-    features = height - CODE_ROWS
+    devices = recv_ref.shape[0]
+    narrow, features = proj_narrow_ref.shape[0], proj_wide_ref.shape[0]
     nodes = user_ref.shape[0] + item_ref.shape[0]
-    group = 8
     total = jnp.zeros((nodes, features + narrow), F32)
-    for first in range(0, devices, group):
-        block = jnp.concatenate([recv_ref[first + p] for p in range(group)], axis=1)
-        codes = block[features:].astype(F32)
-        node = (codes[0:1] * 256 + codes[1:2]).astype(jnp.int32)
-        wide = codes[2:3].astype(BF16)
-        rows = block[:features]
+    for first in range(0, devices, GROUP):
+        parts = [
+            unpacked(recv_ref[first + p].astype(F32), features, capacity) for p in range(GROUP)
+        ]
+        rows, low, high = (jnp.concatenate(part, axis=1) for part in zip(*parts, strict=True))
+        rows = rows.astype(BF16)
+        high = high.astype(jnp.int32)
+        node = low.astype(jnp.int32) + (high >> 1) * 256
+        wide = (high & 1).astype(F32).astype(BF16)
         values = jnp.concatenate([rows * wide, rows[:narrow] * (1 - wide)], axis=0)
         hot = (
-            lax.broadcasted_iota(jnp.int32, (nodes, group * slots), 0) == node
+            lax.broadcasted_iota(jnp.int32, (nodes, GROUP * LANES), 0) == node
         ).astype(F32).astype(BF16)
         total = total + lax.dot_general(hot, values, NT, preferred_element_type=F32)
     weights = jnp.concatenate([proj_wide_ref[...], proj_narrow_ref[...]], axis=0)
@@ -156,11 +232,11 @@
         copy.wait()
 
 
-def segment(recv, proj_narrow, proj_wide, adjacency, upd, ipd):
+def segment(recv, proj_narrow, proj_wide, adjacency, upd, ipd, capacity):
     cols = len(adjacency)
     d = proj_wide.shape[1]
     return pl.pallas_call(
-        functools.partial(segment_kernel, proj_narrow.shape[0], upd, cols),
+        functools.partial(segment_kernel, capacity, upd, cols),
         out_shape=(
             jax.ShapeDtypeStruct((upd, d), BF16),
             jax.ShapeDtypeStruct((d, upd), BF16),
@@ -414,7 +490,6 @@
     devices = rows * cols
     count = raw_rows.shape[0]
     capacity = 3 * count // devices
-    slots = -(-capacity // LANES) * LANES
     upd = adj_values.shape[0] // cols
     ipd = adj_values.shape[1] // rows
     layers = weight_sum.shape[0]
@@ -427,13 +502,15 @@
         raw_slot.reshape(1, count),
         raw_wide.reshape(1, count),
         devices,
-        slots,
+        capacity,
     )
     recv = lax.all_to_all(send, ("row", "col"), split_axis=0, concat_axis=0, tiled=True)
     adjacency = dequantize(
         place, adj_values, tile_mask, tile_scale, (sides, chips, cols)
     )
-    users, users_t, items, *adjacency = segment(recv, proj_narrow, proj_wide, adjacency, upd, ipd)
+    users, users_t, items, *adjacency = segment(
+        recv, proj_narrow, proj_wide, adjacency, upd, ipd, capacity
+    )
     for n in range(layers):
         all_users_t = exchange([users_t] * cols, "col", cols)
         own_swapped = [swap(items, "row", rows)]

time: 92.7 us -> 91.2 us (0.984)
  waiting for transfers between devices: 29.3 us -> 26.6 us
  Pallas kernels: 17 us -> 18.3 us
    all_to_all x1, waiting for transfers between devices: 8.03 us -> 5.49 us  [per_device(): lax.all_to_all(send, ('row', 'col'), split_axis=0, concat_axis=0, tiled=T...]
    pallas_call x2, Pallas kernels: 5.58 us -> 6.88 us  [the longest x1 3.54 us: segment(): pl.pallas_call(functools.partial(segment_kernel, capacity, upd, cols), ou...]
  transfers between devices with their start and end apart: 35 -> 35, of which waited for: 14 -> 14; matrix products, arithmetic and copies ran while one was open for 0% -> 0% of each run, Pallas kernels for 11% -> 12%
where the time goes in v1:
time: 91.2 us; the launch traced here: 90.9 us
  starting transfers between devices  42.8 us (47%)
  waiting for transfers between devices  26.6 us (29%)
  Pallas kernels  18.3 us (20%)
  local copies, waits for them, and re-layouts  2.36 us (3%)
    ppermute x24, starting transfers between devices, exchange(): received.append(lax.ppermute(blocks[k], axis, pairs))  34.3 us
    ppermute x24, waiting for transfers between devices, exchange(): received.append(lax.ppermute(blocks[k], axis, pairs))  21.1 us
    all_to_all x1, starting transfers between devices, per_device(): lax.all_to_all(send, ('row', 'col'), split_axis=0, concat_axis=0, tiled=T...  7.33 us
    all_to_all x1, waiting for transfers between devices, per_device(): lax.all_to_all(send, ('row', 'col'), split_axis=0, concat_axis=0, tiled=T...  5.49 us
    pallas_call x1, Pallas kernels, dequantize(): pl.pallas_call(functools.partial(dequantize_kernel, shape), out_shape=(ja...  5.04 us
    pallas_call x1, Pallas kernels, segment(): pl.pallas_call(functools.partial(segment_kernel, capacity, upd, cols), ou...  3.54 us
    pallas_call x1, Pallas kernels, dispatch(): pl.pallas_call(functools.partial(dispatch_kernel, devices, capacity), out...  3.34 us
    pallas_call x2, Pallas kernels, user_sums(): pl.pallas_call(functools.partial(user_sum_kernel, cols), out_shape=(jax.S...  2.49 us
  transfers between devices with their start and end apart: 35, of which 14 were waited for; matrix products, arithmetic and copies ran while one was open for 0% of the time, Pallas kernels for 12%

profile of v1, /device:TPU:0, one launch (start us, length us, event | category | flops | bytes accessed | tf_op | source)
XLA Modules:
  0.0 90.9 jit_solution(18443749974504087639)
XLA Ops:
  0.6 3.3 %dispatch.1 = bf16[32,56,128]{2,1,0:T(8,128)(2,1)} custom-call(bf16[64,1024]{1,0:T(8,128)(2,1)} %bitcast.7, s32[1,1024]{1,0:T(1,128)} %bitcast.9, s32[1,1024]{1,0:T(1,128)} %bitcast.10, s32[1,1024]{1,0:T(1,128)} %bitcast.11), custom_call_target="tpu_custom_call" | custom-call | tf_op jit(solution)/shard_map/dispatch/pallas_call | solution.py:175
  4.0 7.3 %all-to-all-start = ((bf16[32,56,128]{2,1,0:T(8,128)(2,1)}), bf16[32,56,128]{2,1,0:T(8,128)(2,1)S(1)}, u32[]{:S(2)}, u32[]{:S(2)}) async-start(bf16[32,56,128]{2,1,0:T(8,128)(2,1)} %dispatch.1), calls=%async_computation | async-start | bytes 917504 | tf_op jit(solution)/shard_map/all_to_all | solution.py:507
  11.4 0.7 copy-done.5
  12.1 0.7 copy-done.6
  12.8 5.0 %dequantize.1 = (bf16[256,2048]{1,0:T(8,128)(2,1)S(1)}, bf16[256,2048]{1,0:T(8,128)(2,1)}, bf16[256,2048]{1,0:T(8,128)(2,1)}, bf16[256,2048]{1,0:T(8,128)(2,1)}) custom-call(s32[2]{0:T(128)S(1)} %pad_add_fusion.place_ref, s32[8,16]{1,0:T(8,128)S(1)} %copy-done.5, f32[8,16]{1,0:T(8,128)S(1)} %copy-done.6, bf16[1024,2048]{1,0:T(8,128)(2,1)} %values_ref.1), custom_call_target="tpu_custom_call" | custom-call | flops 2097152 | bytes 8388608 | tf_op jit(solution)/shard_map/dequantize/pallas_call | solution.py:303
  17.9 1.0 %copy-done = bf16[256,2048]{1,0:T(8,128)(2,1)} copy-done((bf16[256,2048]{1,0:T(8,128)(2,1)}, bf16[256,2048]{1,0:T(8,128)(2,1)S(1)}, u32[]{:S(2)}) %copy-start) | copy-done | bytes 1048600
  18.8 5.5 %all-to-all-done.recv_ref = bf16[32,56,128]{2,1,0:T(8,128)(2,1)S(1)} async-done(((bf16[32,56,128]{2,1,0:T(8,128)(2,1)}), bf16[32,56,128]{2,1,0:T(8,128)(2,1)S(1)}, u32[]{:S(2)}, u32[]{:S(2)}) %all-to-all-start) | async-done | bytes 458784 | tf_op jit(solution)/shard_map/all_to_all | solution.py:507
  24.3 3.5 %segment.1 = (bf16[256,128]{1,0:T(8,128)(2,1)S(1)}, bf16[128,256]{1,0:T(8,128)(2,1)S(1)}, bf16[256,128]{1,0:T(8,128)(2,1)S(1)}, bf16[256,2048]{1,0:T(8,128)(2,1)...) custom-call(bf16[32,56,128]{2,1,0:T(8,128)(2,1)S(1)} %all-to-all-done.recv_ref, ...), custom_call_target="tpu_custom_call" | custom-call | tf_op jit(solution)/shard_map/segment/pallas_call | solution.py:238
  27.9 2.9 %collective-permute-start.12 = (bf16[128,256]{1,0:T(8,128)(2,1)S(1)}, bf16[128,256]{1,0:T(8,128)(2,1)S(1)}, u32[]{:S(2)}, u32[]{:S(2)}) collective-permute-start(bf16[128,256]{1,0:T(8,128)(2,1)S(1)} %get-tuple-element.51.refs_4_), channel_id=1, source_target_pairs={{0,3},{1,2},{2,1},{3,0},{4,7},{5,6},{6,5},{7,4},{8,11},{9,10},{10,... | collective-permute-start | bytes 196616 | tf_op jit(solution)/shard_map/ppermute | solution.py:462
  30.7 1.1 %collective-permute-start.11 = (bf16[128,256]{1,0:T(8,128)(2,1)S(1)}, bf16[128,256]{1,0:T(8,128)(2,1)S(1)}, u32[]{:S(2)}, u32[]{:S(2)}) collective-permute-start(bf16[128,256]{1,0:T(8,128)(2,1)S(1)} %get-tuple-element.51.refs_4_), channel_id=1, source_target_pairs={{0,2},{1,3},{2,0},{3,1},{4,6},{5,7},{6,4},{7,5},{8,10},{9,11},{10,... | collective-permute-start | bytes 196616 | tf_op jit(solution)/shard_map/ppermute | solution.py:462
  31.8 0.8 collective-permute-start.2
  32.6 1.1 %collective-permute-start.1 = (bf16[256,128]{1,0:T(8,128)(2,1)S(1)}, bf16[256,128]{1,0:T(8,128)(2,1)S(1)}, u32[]{:S(2)}, u32[]{:S(2)}) collective-permute-start(bf16[256,128]{1,0:T(8,128)(2,1)S(1)} %get-tuple-element.45.refs_4_.own_ref), channel_id=1, source_target_pairs={{0,16},{4,20},{8,24},{12,28},{16,0},{20,4},{24,8},{28,12},{1,17},{... | collective-permute-start | bytes 196616 | tf_op jit(solution)/shard_map/ppermute | solution.py:462
  33.7 1.6 %collective-permute-start = (bf16[256,128]{1,0:T(8,128)(2,1)S(1)}, bf16[256,128]{1,0:T(8,128)(2,1)S(1)}, u32[]{:S(2)}, u32[]{:S(2)}) collective-permute-start(bf16[256,128]{1,0:T(8,128)(2,1)S(1)} %get-tuple-element.45.refs_4_.own_ref), channel_id=1, source_target_pairs={{0,8},{4,12},{8,0},{12,4},{16,24},{20,28},{24,16},{28,20},{1,9},{5... | collective-permute-start | bytes 196616 | tf_op jit(solution)/shard_map/ppermute | solution.py:462
  35.3 2.7 %collective-permute-start.10 = (bf16[128,256]{1,0:T(8,128)(2,1)S(1)}, bf16[128,256]{1,0:T(8,128)(2,1)S(1)}, u32[]{:S(2)}, u32[]{:S(2)}) collective-permute-start(bf16[128,256]{1,0:T(8,128)(2,1)S(1)} %get-tuple-element.51.refs_4_), channel_id=1, source_target_pairs={{0,1},{1,0},{2,3},{3,2},{4,5},{5,4},{6,7},{7,6},{8,9},{9,8},{10,11... | collective-permute-start | bytes 196616 | tf_op jit(solution)/shard_map/ppermute | solution.py:462
  38.3 0.5 collective-permute-start.6
  38.9 0.4 collective-permute-start.4
  39.3 1.0 %collective-permute-done.10.refs_5_ = bf16[128,256]{1,0:T(8,128)(2,1)S(1)} collective-permute-done((bf16[128,256]{1,0:T(8,128)(2,1)S(1)}, bf16[128,256]{1,0:T(8,128)(2,1)S(1)}, u32[]{:S(2)}, u32[]{:S(2)}) %collective-permute-start.10) | collective-permute-done | bytes 65568 | tf_op jit(solution)/shard_map/ppermute | solution.py:462
  40.3 0.7 item_sums.2
  41.1 1.2 %user_sums.2 = (bf16[256,128]{1,0:T(8,128)(2,1)S(1)}, bf16[256,128]{1,0:T(8,128)(2,1)S(1)}, bf16[256,128]{1,0:T(8,128)(2,1)S(1)}, bf16[256,128]{1,0:T(8,128)(2,1)S(1)}) custom-call(bf16[256,2048]{1,0:T(8,128)(2,1)S(1)} %get-tuple-element.41.refs_0_, bf16[256,2048]{1,0:T(8,128)(2,1)S(1)} %get-tuple-element.42.refs_1_, ...), custom_call_target="tpu_custom_call" | custom-call | flops 536870912 | bytes 4194304 | tf_op jit(solution)/shard_map/user_sums/pallas_call | solution.py:333
  42.4 2.1 %collective-permute-start.7 = (bf16[256,128]{1,0:T(8,128)(2,1)S(1)}, bf16[256,128]{1,0:T(8,128)(2,1)S(1)}, u32[]{:S(2)}, u32[]{:S(2)}) collective-permute-start(bf16[256,128]{1,0:T(8,128)(2,1)S(1)} %get-tuple-element.47), channel_id=1, source_target_pairs={{0,1},{1,0},{2,3},{3,2},{4,5},{5,4},{6,7},{7,6},{8,9},{9,8},{10,11... | collective-permute-start | bytes 196616 | tf_op jit(solution)/shard_map/ppermute | solution.py:462
  44.5 2.4 %collective-permute-start.9 = (bf16[256,128]{1,0:T(8,128)(2,1)S(1)}, bf16[256,128]{1,0:T(8,128)(2,1)S(1)}, u32[]{:S(2)}, u32[]{:S(2)}) collective-permute-start(bf16[256,128]{1,0:T(8,128)(2,1)S(1)} %get-tuple-element.49), channel_id=1, source_target_pairs={{0,3},{1,2},{2,1},{3,0},{4,7},{5,6},{6,5},{7,4},{8,11},{9,10},{10,... | collective-permute-start | bytes 196616 | tf_op jit(solution)/shard_map/ppermute | solution.py:462
  46.9 0.3 collective-permute-done.7.refs_1_
  47.2 5.0 %collective-permute-done.8.refs_2_ = bf16[256,128]{1,0:T(8,128)(2,1)S(1)} collective-permute-done((bf16[256,128]{1,0:T(8,128)(2,1)S(1)}, bf16[256,128]{1,0:T(8,128)(2,1)S(1)}, u32[]{:S(2)}, u32[]{:S(2)}) %collective-permute-start.8) | collective-permute-done | bytes 65568 | tf_op jit(solution)/shard_map/ppermute | solution.py:462
  52.5 1.5 %collective-permute-start.29 = (bf16[128,256]{1,0:T(8,128)(2,1)S(1)}, bf16[128,256]{1,0:T(8,128)(2,1)S(1)}, u32[]{:S(2)}, u32[]{:S(2)}) collective-permute-start(bf16[128,256]{1,0:T(8,128)(2,1)S(1)} %get-tuple-element.63.refs_4_), channel_id=1, source_target_pairs={{0,3},{1,2},{2,1},{3,0},{4,7},{5,6},{6,5},{7,4},{8,11},{9,10},{10,... | collective-permute-start | bytes 196616 | tf_op jit(solution)/shard_map/ppermute | solution.py:462
  54.0 2.0 %collective-permute-start.28 = (bf16[128,256]{1,0:T(8,128)(2,1)S(1)}, bf16[128,256]{1,0:T(8,128)(2,1)S(1)}, u32[]{:S(2)}, u32[]{:S(2)}) collective-permute-start(bf16[128,256]{1,0:T(8,128)(2,1)S(1)} %get-tuple-element.63.refs_4_), channel_id=1, source_target_pairs={{0,2},{1,3},{2,0},{3,1},{4,6},{5,7},{6,4},{7,5},{8,10},{9,11},{10,... | collective-permute-start | bytes 196616 | tf_op jit(solution)/shard_map/ppermute | solution.py:462
  56.0 1.0 %collective-permute-start.27 = (bf16[128,256]{1,0:T(8,128)(2,1)S(1)}, bf16[128,256]{1,0:T(8,128)(2,1)S(1)}, u32[]{:S(2)}, u32[]{:S(2)}) collective-permute-start(bf16[128,256]{1,0:T(8,128)(2,1)S(1)} %get-tuple-element.63.refs_4_), channel_id=1, source_target_pairs={{0,1},{1,0},{2,3},{3,2},{4,5},{5,4},{6,7},{7,6},{8,9},{9,8},{10,11... | collective-permute-start | bytes 196616 | tf_op jit(solution)/shard_map/ppermute | solution.py:462
  57.0 2.4 %collective-permute-done.29.refs_7_ = bf16[128,256]{1,0:T(8,128)(2,1)S(1)} collective-permute-done((bf16[128,256]{1,0:T(8,128)(2,1)S(1)}, bf16[128,256]{1,0:T(8,128)(2,1)S(1)}, u32[]{:S(2)}, u32[]{:S(2)}) %collective-permute-start.29) | collective-permute-done | bytes 65568 | tf_op jit(solution)/shard_map/ppermute | solution.py:462
  59.4 2.8 %collective-permute-done.28.refs_6_ = bf16[128,256]{1,0:T(8,128)(2,1)S(1)} collective-permute-done((bf16[128,256]{1,0:T(8,128)(2,1)S(1)}, bf16[128,256]{1,0:T(8,128)(2,1)S(1)}, u32[]{:S(2)}, u32[]{:S(2)}) %collective-permute-start.28) | collective-permute-done | bytes 65568 | tf_op jit(solution)/shard_map/ppermute | solution.py:462
  62.2 0.7 item_sums.3
  63.3 3.3 %collective-permute-start.16 = (bf16[128,256]{1,0:T(8,128)(2,1)S(1)}, bf16[128,256]{1,0:T(8,128)(2,1)S(1)}, u32[]{:S(2)}, u32[]{:S(2)}) collective-permute-start(bf16[128,256]{1,0:T(8,128)(2,1)S(1)} %get-tuple-element.57), channel_id=1, source_target_pairs={{0,24},{4,28},{8,16},{12,20},{16,8},{20,12},{24,0},{28,4},{1,25},{... | collective-permute-start | bytes 196616 | tf_op jit(solution)/shard_map/ppermute | solution.py:462
  66.6 1.1 %collective-permute-done.14.refs_1_ = bf16[128,256]{1,0:T(8,128)(2,1)S(1)} collective-permute-done((bf16[128,256]{1,0:T(8,128)(2,1)S(1)}, bf16[128,256]{1,0:T(8,128)(2,1)S(1)}, u32[]{:S(2)}, u32[]{:S(2)}) %collective-permute-start.14) | collective-permute-done | bytes 65568 | tf_op jit(solution)/shard_map/ppermute | solution.py:462
  67.7 1.3 %collective-permute-done.15.refs_2_ = bf16[128,256]{1,0:T(8,128)(2,1)S(1)} collective-permute-done((bf16[128,256]{1,0:T(8,128)(2,1)S(1)}, bf16[128,256]{1,0:T(8,128)(2,1)S(1)}, u32[]{:S(2)}, u32[]{:S(2)}) %collective-permute-start.15) | collective-permute-done | bytes 65568 | tf_op jit(solution)/shard_map/ppermute | solution.py:462
  69.3 2.8 %collective-permute-start.19 = (bf16[256,128]{1,0:T(8,128)(2,1)S(1)}, bf16[256,128]{1,0:T(8,128)(2,1)S(1)}, u32[]{:S(2)}, u32[]{:S(2)}) collective-permute-start(bf16[256,128]{1,0:T(8,128)(2,1)S(1)} %item_update.2.refs_4_.own_ref), channel_id=1, source_target_pairs={{0,24},{4,28},{8,16},{12,20},{16,8},{20,12},{24,0},{28,4},{1,25},{... | collective-permute-start | bytes 196616 | tf_op jit(solution)/shard_map/ppermute | solution.py:462
  72.1 0.5 collective-permute-start.18
  72.6 0.3 collective-permute-start.17
  72.9 1.9 %collective-permute-done.19.refs_7_ = bf16[256,128]{1,0:T(8,128)(2,1)S(1)} collective-permute-done((bf16[256,128]{1,0:T(8,128)(2,1)S(1)}, bf16[256,128]{1,0:T(8,128)(2,1)S(1)}, u32[]{:S(2)}, u32[]{:S(2)}) %collective-permute-start.19) | collective-permute-done | bytes 65568 | tf_op jit(solution)/shard_map/ppermute | solution.py:462
  74.8 1.6 %collective-permute-done.18.refs_6_ = bf16[256,128]{1,0:T(8,128)(2,1)S(1)} collective-permute-done((bf16[256,128]{1,0:T(8,128)(2,1)S(1)}, bf16[256,128]{1,0:T(8,128)(2,1)S(1)}, u32[]{:S(2)}, u32[]{:S(2)}) %collective-permute-start.18) | collective-permute-done | bytes 65568 | tf_op jit(solution)/shard_map/ppermute | solution.py:462
  76.4 0.5 collective-permute-done.17.refs_5_
  76.9 0.8 collective-permute-start.31
  77.8 0.9 %collective-permute-start.32 = (bf16[128,256]{1,0:T(8,128)(2,1)S(1)}, bf16[128,256]{1,0:T(8,128)(2,1)S(1)}, u32[]{:S(2)}, u32[]{:S(2)}) collective-permute-start(bf16[128,256]{1,0:T(8,128)(2,1)S(1)} %get-tuple-element.68), channel_id=1, source_target_pairs={{0,16},{4,20},{8,24},{12,28},{16,0},{20,4},{24,8},{28,12},{1,17},{... | collective-permute-start | bytes 196616 | tf_op jit(solution)/shard_map/ppermute | solution.py:462
  78.7 1.8 %collective-permute-start.33 = (bf16[128,256]{1,0:T(8,128)(2,1)S(1)}, bf16[128,256]{1,0:T(8,128)(2,1)S(1)}, u32[]{:S(2)}, u32[]{:S(2)}) collective-permute-start(bf16[128,256]{1,0:T(8,128)(2,1)S(1)} %get-tuple-element.69), channel_id=1, source_target_pairs={{0,24},{4,28},{8,16},{12,20},{16,8},{20,12},{24,0},{28,4},{1,25},{... | collective-permute-start | bytes 196616 | tf_op jit(solution)/shard_map/ppermute | solution.py:462
  80.5 1.2 %user_sums.3 = (bf16[256,128]{1,0:T(8,128)(2,1)S(1)}, bf16[256,128]{1,0:T(8,128)(2,1)S(1)}, bf16[256,128]{1,0:T(8,128)(2,1)S(1)}, bf16[256,128]{1,0:T(8,128)(2,1)S(1)}) custom-call(bf16[256,2048]{1,0:T(8,128)(2,1)S(1)} %get-tuple-element.41.refs_0_, bf16[256,2048]{1,0:T(8,128)(2,1)S(1)} %get-tuple-element.42.refs_1_, ...), custom_call_target="tpu_custom_call" | custom-call | flops 536870912 | bytes 4194304 | tf_op jit(solution)/shard_map/user_sums/pallas_call | solution.py:333
  81.8 2.1 %collective-permute-start.25 = (bf16[256,128]{1,0:T(8,128)(2,1)S(1)}, bf16[256,128]{1,0:T(8,128)(2,1)S(1)}, u32[]{:S(2)}, u32[]{:S(2)}) collective-permute-start(bf16[256,128]{1,0:T(8,128)(2,1)S(1)} %get-tuple-element.60), channel_id=1, source_target_pairs={{0,2},{1,3},{2,0},{3,1},{4,6},{5,7},{6,4},{7,5},{8,10},{9,11},{10,... | collective-permute-start | bytes 196616 | tf_op jit(solution)/shard_map/ppermute | solution.py:462
  83.9 2.3 %collective-permute-start.26 = (bf16[256,128]{1,0:T(8,128)(2,1)S(1)}, bf16[256,128]{1,0:T(8,128)(2,1)S(1)}, u32[]{:S(2)}, u32[]{:S(2)}) collective-permute-start(bf16[256,128]{1,0:T(8,128)(2,1)S(1)} %get-tuple-element.61), channel_id=1, source_target_pairs={{0,3},{1,2},{2,1},{3,0},{4,7},{5,6},{6,5},{7,4},{8,11},{9,10},{10,... | collective-permute-start | bytes 196616 | tf_op jit(solution)/shard_map/ppermute | solution.py:462
  86.2 0.9 item_update.3
  87.1 2.2 %collective-permute-done.25.refs_2_ = bf16[256,128]{1,0:T(8,128)(2,1)S(1)} collective-permute-done((bf16[256,128]{1,0:T(8,128)(2,1)S(1)}, bf16[256,128]{1,0:T(8,128)(2,1)S(1)}, u32[]{:S(2)}, u32[]{:S(2)}) %collective-permute-start.25) | collective-permute-done | bytes 65568 | tf_op jit(solution)/shard_map/ppermute | solution.py:462
  89.3 0.7 collective-permute-done.26.refs_3_
  90.0 0.9 user_update.3
  (50 shorter events, 1.5 us)
Async XLA Ops:
  4.0 20.3 %copy-start.3 = (bf16[64,128]{1,0:T(8,128)(2,1)S(1)}, bf16[64,128]{1,0:T(8,128)(2,1)}, u32[]{:S(2)}) copy-start(bf16[64,128]{1,0:T(8,128)(2,1)} %proj_wide_ref.1) | copy-start | bytes 49156
  4.0 20.3 %copy-start.4 = (bf16[32,128]{1,0:T(8,128)(2,1)S(1)}, bf16[32,128]{1,0:T(8,128)(2,1)}, u32[]{:S(2)}) copy-start(bf16[32,128]{1,0:T(8,128)(2,1)} %proj_narrow_ref.1) | copy-start | bytes 24580
  4.0 20.3 %all-to-all-start = ((bf16[32,56,128]{2,1,0:T(8,128)(2,1)}), bf16[32,56,128]{2,1,0:T(8,128)(2,1)S(1)}, u32[]{:S(2)}, u32[]{:S(2)}) async-start(bf16[32,56,128]{2,1,0:T(8,128)(2,1)} %dispatch.1), calls=%async_computation | async-start | bytes 917504 | tf_op jit(solution)/shard_map/all_to_all | solution.py:507
  11.4 0.7 copy-start.5
  12.1 0.7 copy-start.6
  17.8 1.0 %copy-start = (bf16[256,2048]{1,0:T(8,128)(2,1)}, bf16[256,2048]{1,0:T(8,128)(2,1)S(1)}, u32[]{:S(2)}) copy-start(bf16[256,2048]{1,0:T(8,128)(2,1)S(1)} %get-tuple-element.36.refs_0_) | copy-start | bytes 3145732
  27.9 7.4 %collective-permute-start.12 = (bf16[128,256]{1,0:T(8,128)(2,1)S(1)}, bf16[128,256]{1,0:T(8,128)(2,1)S(1)}, u32[]{:S(2)}, u32[]{:S(2)}) collective-permute-start(bf16[128,256]{1,0:T(8,128)(2,1)S(1)} %get-tuple-element.51.refs_4_), channel_id=1, source_target_pairs={{0,3},{1,2},{2,1},{3,0},{4,7},{5,6},{6,5},{7,4},{8,11},{9,10},{10,... | collective-permute-start | bytes 196616 | tf_op jit(solution)/shard_map/ppermute | solution.py:462
  30.7 7.5 %collective-permute-start.11 = (bf16[128,256]{1,0:T(8,128)(2,1)S(1)}, bf16[128,256]{1,0:T(8,128)(2,1)S(1)}, u32[]{:S(2)}, u32[]{:S(2)}) collective-permute-start(bf16[128,256]{1,0:T(8,128)(2,1)S(1)} %get-tuple-element.51.refs_4_), channel_id=1, source_target_pairs={{0,2},{1,3},{2,0},{3,1},{4,6},{5,7},{6,4},{7,5},{8,10},{9,11},{10,... | collective-permute-start | bytes 196616 | tf_op jit(solution)/shard_map/ppermute | solution.py:462
  31.8 6.5 %collective-permute-start.2 = (bf16[256,128]{1,0:T(8,128)(2,1)S(1)}, bf16[256,128]{1,0:T(8,128)(2,1)S(1)}, u32[]{:S(2)}, u32[]{:S(2)}) collective-permute-start(bf16[256,128]{1,0:T(8,128)(2,1)S(1)} %get-tuple-element.45.refs_4_.own_ref), channel_id=1, source_target_pairs={{0,24},{4,28},{8,16},{12,20},{16,8},{20,12},{24,0},{28,4},{1,25},{... | collective-permute-start | bytes 196616 | tf_op jit(solution)/shard_map/ppermute | solution.py:462
  32.6 6.1 %collective-permute-start.1 = (bf16[256,128]{1,0:T(8,128)(2,1)S(1)}, bf16[256,128]{1,0:T(8,128)(2,1)S(1)}, u32[]{:S(2)}, u32[]{:S(2)}) collective-permute-start(bf16[256,128]{1,0:T(8,128)(2,1)S(1)} %get-tuple-element.45.refs_4_.own_ref), channel_id=1, source_target_pairs={{0,16},{4,20},{8,24},{12,28},{16,0},{20,4},{24,8},{28,12},{1,17},{... | collective-permute-start | bytes 196616 | tf_op jit(solution)/shard_map/ppermute | solution.py:462
  33.7 5.1 %collective-permute-start = (bf16[256,128]{1,0:T(8,128)(2,1)S(1)}, bf16[256,128]{1,0:T(8,128)(2,1)S(1)}, u32[]{:S(2)}, u32[]{:S(2)}) collective-permute-start(bf16[256,128]{1,0:T(8,128)(2,1)S(1)} %get-tuple-element.45.refs_4_.own_ref), channel_id=1, source_target_pairs={{0,8},{4,12},{8,0},{12,4},{16,24},{20,28},{24,16},{28,20},{1,9},{5... | collective-permute-start | bytes 196616 | tf_op jit(solution)/shard_map/ppermute | solution.py:462
  35.3 5.0 %collective-permute-start.10 = (bf16[128,256]{1,0:T(8,128)(2,1)S(1)}, bf16[128,256]{1,0:T(8,128)(2,1)S(1)}, u32[]{:S(2)}, u32[]{:S(2)}) collective-permute-start(bf16[128,256]{1,0:T(8,128)(2,1)S(1)} %get-tuple-element.51.refs_4_), channel_id=1, source_target_pairs={{0,1},{1,0},{2,3},{3,2},{4,5},{5,4},{6,7},{7,6},{8,9},{9,8},{10,11... | collective-permute-start | bytes 196616 | tf_op jit(solution)/shard_map/ppermute | solution.py:462
  38.3 2.8 %collective-permute-start.3 = (bf16[256,128]{1,0:T(8,128)(2,1)S(1)}, bf16[256,128]{1,0:T(8,128)(2,1)S(1)}, u32[]{:S(2)}, u32[]{:S(2)}) collective-permute-start(bf16[256,128]{1,0:T(8,128)(2,1)S(1)} %get-tuple-element.45.refs_4_.own_ref), channel_id=1, source_target_pairs={{0,4},{4,0},{8,12},{12,8},{16,20},{20,16},{24,28},{28,24},{1,5},{5... | collective-permute-start | bytes 196616 | tf_op jit(solution)/shard_map/ppermute | solution.py:467
  38.3 2.8 %collective-permute-start.6 = (bf16[256,128]{1,0:T(8,128)(2,1)S(1)}, bf16[256,128]{1,0:T(8,128)(2,1)S(1)}, u32[]{:S(2)}, u32[]{:S(2)}) collective-permute-start(bf16[256,128]{1,0:T(8,128)(2,1)S(1)} %collective-permute-done.2.refs_7_), channel_id=1, source_target_pairs={{0,4},{4,0},{8,12},{12,8},{16,20},{20,16},{24,28},{28,24},{1,5},{5... | collective-permute-start | bytes 196616 | tf_op jit(solution)/shard_map/ppermute | solution.py:467
  38.8 2.3 %collective-permute-start.5 = (bf16[256,128]{1,0:T(8,128)(2,1)S(1)}, bf16[256,128]{1,0:T(8,128)(2,1)S(1)}, u32[]{:S(2)}, u32[]{:S(2)}) collective-permute-start(bf16[256,128]{1,0:T(8,128)(2,1)S(1)} %collective-permute-done.1.refs_6_), channel_id=1, source_target_pairs={{0,4},{4,0},{8,12},{12,8},{16,20},{20,16},{24,28},{28,24},{1,5},{5... | collective-permute-start | bytes 196616 | tf_op jit(solution)/shard_map/ppermute | solution.py:467
  38.9 2.3 %collective-permute-start.4 = (bf16[256,128]{1,0:T(8,128)(2,1)S(1)}, bf16[256,128]{1,0:T(8,128)(2,1)S(1)}, u32[]{:S(2)}, u32[]{:S(2)}) collective-permute-start(bf16[256,128]{1,0:T(8,128)(2,1)S(1)} %collective-permute-done.refs_5_), channel_id=1, source_target_pairs={{0,4},{4,0},{8,12},{12,8},{16,20},{20,16},{24,28},{28,24},{1,5},{5... | collective-permute-start | bytes 196616 | tf_op jit(solution)/shard_map/ppermute | solution.py:467
  40.3 12.0 %copy-start.1 = (bf16[2,128,128]{2,1,0:T(8,128)(2,1)S(1)}, bf16[2,128,128]{2,1,0:T(8,128)(2,1)}, u32[]{:S(2)}) copy-start(bf16[2,128,128]{2,1,0:T(8,128)(2,1)} %sum_ref.7) | copy-start | bytes 196612
  40.3 12.0 %copy-start.2 = (bf16[2,128,128]{2,1,0:T(8,128)(2,1)S(1)}, bf16[2,128,128]{2,1,0:T(8,128)(2,1)}, u32[]{:S(2)}) copy-start(bf16[2,128,128]{2,1,0:T(8,128)(2,1)} %product_ref.7) | copy-start | bytes 196612
  41.0 22.0 %collective-permute-start.13 = (bf16[4,128,256]{2,1,0:T(8,128)(2,1)S(1)}, bf16[4,128,256]{2,1,0:T(8,128)(2,1)S(1)}, u32[]{:S(2)}, u32[]{:S(2)}) collective-permute-start(bf16[4,128,256]{2,1,0:T(8,128)(2,1)S(1)} %get-tuple-element.53), channel_id=1, source_target_pairs={{0,4},{4,0},{8,12},{12,8},{16,20},{20,16},{24,28},{28,24},{1,5},{5... | collective-permute-start | bytes 786440 | tf_op jit(solution)/shard_map/ppermute | solution.py:467
  42.4 4.8 %collective-permute-start.7 = (bf16[256,128]{1,0:T(8,128)(2,1)S(1)}, bf16[256,128]{1,0:T(8,128)(2,1)S(1)}, u32[]{:S(2)}, u32[]{:S(2)}) collective-permute-start(bf16[256,128]{1,0:T(8,128)(2,1)S(1)} %get-tuple-element.47), channel_id=1, source_target_pairs={{0,1},{1,0},{2,3},{3,2},{4,5},{5,4},{6,7},{7,6},{8,9},{9,8},{10,11... | collective-permute-start | bytes 196616 | tf_op jit(solution)/shard_map/ppermute | solution.py:462
  44.5 7.8 %collective-permute-start.8 = (bf16[256,128]{1,0:T(8,128)(2,1)S(1)}, bf16[256,128]{1,0:T(8,128)(2,1)S(1)}, u32[]{:S(2)}, u32[]{:S(2)}) collective-permute-start(bf16[256,128]{1,0:T(8,128)(2,1)S(1)} %get-tuple-element.48), channel_id=1, source_target_pairs={{0,2},{1,3},{2,0},{3,1},{4,6},{5,7},{6,4},{7,5},{8,10},{9,11},{10,... | collective-permute-start | bytes 196616 | tf_op jit(solution)/shard_map/ppermute | solution.py:462
  44.5 7.8 %collective-permute-start.9 = (bf16[256,128]{1,0:T(8,128)(2,1)S(1)}, bf16[256,128]{1,0:T(8,128)(2,1)S(1)}, u32[]{:S(2)}, u32[]{:S(2)}) collective-permute-start(bf16[256,128]{1,0:T(8,128)(2,1)S(1)} %get-tuple-element.49), channel_id=1, source_target_pairs={{0,3},{1,2},{2,1},{3,0},{4,7},{5,6},{6,5},{7,4},{8,11},{9,10},{10,... | collective-permute-start | bytes 196616 | tf_op jit(solution)/shard_map/ppermute | solution.py:462
  52.5 6.8 %collective-permute-start.29 = (bf16[128,256]{1,0:T(8,128)(2,1)S(1)}, bf16[128,256]{1,0:T(8,128)(2,1)S(1)}, u32[]{:S(2)}, u32[]{:S(2)}) collective-permute-start(bf16[128,256]{1,0:T(8,128)(2,1)S(1)} %get-tuple-element.63.refs_4_), channel_id=1, source_target_pairs={{0,3},{1,2},{2,1},{3,0},{4,7},{5,6},{6,5},{7,4},{8,11},{9,10},{10,... | collective-permute-start | bytes 196616 | tf_op jit(solution)/shard_map/ppermute | solution.py:462
  54.0 8.2 %collective-permute-start.28 = (bf16[128,256]{1,0:T(8,128)(2,1)S(1)}, bf16[128,256]{1,0:T(8,128)(2,1)S(1)}, u32[]{:S(2)}, u32[]{:S(2)}) collective-permute-start(bf16[128,256]{1,0:T(8,128)(2,1)S(1)} %get-tuple-element.63.refs_4_), channel_id=1, source_target_pairs={{0,2},{1,3},{2,0},{3,1},{4,6},{5,7},{6,4},{7,5},{8,10},{9,11},{10,... | collective-permute-start | bytes 196616 | tf_op jit(solution)/shard_map/ppermute | solution.py:462
  56.0 6.2 %collective-permute-start.27 = (bf16[128,256]{1,0:T(8,128)(2,1)S(1)}, bf16[128,256]{1,0:T(8,128)(2,1)S(1)}, u32[]{:S(2)}, u32[]{:S(2)}) collective-permute-start(bf16[128,256]{1,0:T(8,128)(2,1)S(1)} %get-tuple-element.63.refs_4_), channel_id=1, source_target_pairs={{0,1},{1,0},{2,3},{3,2},{4,5},{5,4},{6,7},{7,6},{8,9},{9,8},{10,11... | collective-permute-start | bytes 196616 | tf_op jit(solution)/shard_map/ppermute | solution.py:462
  62.9 14.0 %collective-permute-start.30 = (bf16[4,128,256]{2,1,0:T(8,128)(2,1)S(1)}, bf16[4,128,256]{2,1,0:T(8,128)(2,1)S(1)}, u32[]{:S(2)}, u32[]{:S(2)}) collective-permute-start(bf16[4,128,256]{2,1,0:T(8,128)(2,1)S(1)} %get-tuple-element.65), channel_id=1, source_target_pairs={{0,4},{4,0},{8,12},{12,8},{16,20},{20,16},{24,28},{28,24},{1,5},{5... | collective-permute-start | bytes 786440 | tf_op jit(solution)/shard_map/ppermute | solution.py:467
  63.1 4.7 %collective-permute-start.14 = (bf16[128,256]{1,0:T(8,128)(2,1)S(1)}, bf16[128,256]{1,0:T(8,128)(2,1)S(1)}, u32[]{:S(2)}, u32[]{:S(2)}) collective-permute-start(bf16[128,256]{1,0:T(8,128)(2,1)S(1)} %get-tuple-element.55), channel_id=1, source_target_pairs={{0,8},{4,12},{8,0},{12,4},{16,24},{20,28},{24,16},{28,20},{1,9},{5... | collective-permute-start | bytes 196616 | tf_op jit(solution)/shard_map/ppermute | solution.py:462
  63.1 6.0 %collective-permute-start.15 = (bf16[128,256]{1,0:T(8,128)(2,1)S(1)}, bf16[128,256]{1,0:T(8,128)(2,1)S(1)}, u32[]{:S(2)}, u32[]{:S(2)}) collective-permute-start(bf16[128,256]{1,0:T(8,128)(2,1)S(1)} %get-tuple-element.56), channel_id=1, source_target_pairs={{0,16},{4,20},{8,24},{12,28},{16,0},{20,4},{24,8},{28,12},{1,17},{... | collective-permute-start | bytes 196616 | tf_op jit(solution)/shard_map/ppermute | solution.py:462
  63.3 5.8 %collective-permute-start.16 = (bf16[128,256]{1,0:T(8,128)(2,1)S(1)}, bf16[128,256]{1,0:T(8,128)(2,1)S(1)}, u32[]{:S(2)}, u32[]{:S(2)}) collective-permute-start(bf16[128,256]{1,0:T(8,128)(2,1)S(1)} %get-tuple-element.57), channel_id=1, source_target_pairs={{0,24},{4,28},{8,16},{12,20},{16,8},{20,12},{24,0},{28,4},{1,25},{... | collective-permute-start | bytes 196616 | tf_op jit(solution)/shard_map/ppermute | solution.py:462
  69.3 5.4 %collective-permute-start.19 = (bf16[256,128]{1,0:T(8,128)(2,1)S(1)}, bf16[256,128]{1,0:T(8,128)(2,1)S(1)}, u32[]{:S(2)}, u32[]{:S(2)}) collective-permute-start(bf16[256,128]{1,0:T(8,128)(2,1)S(1)} %item_update.2.refs_4_.own_ref), channel_id=1, source_target_pairs={{0,24},{4,28},{8,16},{12,20},{16,8},{20,12},{24,0},{28,4},{1,25},{... | collective-permute-start | bytes 196616 | tf_op jit(solution)/shard_map/ppermute | solution.py:462
  72.1 4.3 %collective-permute-start.18 = (bf16[256,128]{1,0:T(8,128)(2,1)S(1)}, bf16[256,128]{1,0:T(8,128)(2,1)S(1)}, u32[]{:S(2)}, u32[]{:S(2)}) collective-permute-start(bf16[256,128]{1,0:T(8,128)(2,1)S(1)} %item_update.2.refs_4_.own_ref), channel_id=1, source_target_pairs={{0,16},{4,20},{8,24},{12,28},{16,0},{20,4},{24,8},{28,12},{1,17},{... | collective-permute-start | bytes 196616 | tf_op jit(solution)/shard_map/ppermute | solution.py:462
  72.6 4.3 %collective-permute-start.17 = (bf16[256,128]{1,0:T(8,128)(2,1)S(1)}, bf16[256,128]{1,0:T(8,128)(2,1)S(1)}, u32[]{:S(2)}, u32[]{:S(2)}) collective-permute-start(bf16[256,128]{1,0:T(8,128)(2,1)S(1)} %item_update.2.refs_4_.own_ref), channel_id=1, source_target_pairs={{0,8},{4,12},{8,0},{12,4},{16,24},{20,28},{24,16},{28,20},{1,9},{5... | collective-permute-start | bytes 196616 | tf_op jit(solution)/shard_map/ppermute | solution.py:462
  72.9 4.9 %collective-permute-start.20 = (bf16[256,128]{1,0:T(8,128)(2,1)S(1)}, bf16[256,128]{1,0:T(8,128)(2,1)S(1)}, u32[]{:S(2)}, u32[]{:S(2)}) collective-permute-start(bf16[256,128]{1,0:T(8,128)(2,1)S(1)} %item_update.2.refs_4_.own_ref), channel_id=1, source_target_pairs={{0,4},{4,0},{8,12},{12,8},{16,20},{20,16},{24,28},{28,24},{1,5},{5... | collective-permute-start | bytes 196616 | tf_op jit(solution)/shard_map/ppermute | solution.py:467
  74.8 3.9 %collective-permute-start.23 = (bf16[256,128]{1,0:T(8,128)(2,1)S(1)}, bf16[256,128]{1,0:T(8,128)(2,1)S(1)}, u32[]{:S(2)}, u32[]{:S(2)}) collective-permute-start(bf16[256,128]{1,0:T(8,128)(2,1)S(1)} %collective-permute-done.19.refs_7_), channel_id=1, source_target_pairs={{0,4},{4,0},{8,12},{12,8},{16,20},{20,16},{24,28},{28,24},{1,5},{5... | collective-permute-start | bytes 196616 | tf_op jit(solution)/shard_map/ppermute | solution.py:467
  76.4 4.1 %collective-permute-start.22 = (bf16[256,128]{1,0:T(8,128)(2,1)S(1)}, bf16[256,128]{1,0:T(8,128)(2,1)S(1)}, u32[]{:S(2)}, u32[]{:S(2)}) collective-permute-start(bf16[256,128]{1,0:T(8,128)(2,1)S(1)} %collective-permute-done.18.refs_6_), channel_id=1, source_target_pairs={{0,4},{4,0},{8,12},{12,8},{16,20},{20,16},{24,28},{28,24},{1,5},{5... | collective-permute-start | bytes 196616 | tf_op jit(solution)/shard_map/ppermute | solution.py:467
  76.9 3.6 %collective-permute-start.21 = (bf16[256,128]{1,0:T(8,128)(2,1)S(1)}, bf16[256,128]{1,0:T(8,128)(2,1)S(1)}, u32[]{:S(2)}, u32[]{:S(2)}) collective-permute-start(bf16[256,128]{1,0:T(8,128)(2,1)S(1)} %collective-permute-done.17.refs_5_), channel_id=1, source_target_pairs={{0,4},{4,0},{8,12},{12,8},{16,20},{20,16},{24,28},{28,24},{1,5},{5... | collective-permute-start | bytes 196616 | tf_op jit(solution)/shard_map/ppermute | solution.py:467
  76.9 7.0 %collective-permute-start.31 = (bf16[128,256]{1,0:T(8,128)(2,1)S(1)}, bf16[128,256]{1,0:T(8,128)(2,1)S(1)}, u32[]{:S(2)}, u32[]{:S(2)}) collective-permute-start(bf16[128,256]{1,0:T(8,128)(2,1)S(1)} %get-tuple-element.67), channel_id=1, source_target_pairs={{0,8},{4,12},{8,0},{12,4},{16,24},{20,28},{24,16},{28,20},{1,9},{5... | collective-permute-start | bytes 196616 | tf_op jit(solution)/shard_map/ppermute | solution.py:462
  77.8 8.5 %collective-permute-start.32 = (bf16[128,256]{1,0:T(8,128)(2,1)S(1)}, bf16[128,256]{1,0:T(8,128)(2,1)S(1)}, u32[]{:S(2)}, u32[]{:S(2)}) collective-permute-start(bf16[128,256]{1,0:T(8,128)(2,1)S(1)} %get-tuple-element.68), channel_id=1, source_target_pairs={{0,16},{4,20},{8,24},{12,28},{16,0},{20,4},{24,8},{28,12},{1,17},{... | collective-permute-start | bytes 196616 | tf_op jit(solution)/shard_map/ppermute | solution.py:462
  78.7 7.5 %collective-permute-start.33 = (bf16[128,256]{1,0:T(8,128)(2,1)S(1)}, bf16[128,256]{1,0:T(8,128)(2,1)S(1)}, u32[]{:S(2)}, u32[]{:S(2)}) collective-permute-start(bf16[128,256]{1,0:T(8,128)(2,1)S(1)} %get-tuple-element.69), channel_id=1, source_target_pairs={{0,24},{4,28},{8,16},{12,20},{16,8},{20,12},{24,0},{28,4},{1,25},{... | collective-permute-start | bytes 196616 | tf_op jit(solution)/shard_map/ppermute | solution.py:462
  81.7 5.3 %collective-permute-start.24 = (bf16[256,128]{1,0:T(8,128)(2,1)S(1)}, bf16[256,128]{1,0:T(8,128)(2,1)S(1)}, u32[]{:S(2)}, u32[]{:S(2)}) collective-permute-start(bf16[256,128]{1,0:T(8,128)(2,1)S(1)} %get-tuple-element.59), channel_id=1, source_target_pairs={{0,1},{1,0},{2,3},{3,2},{4,5},{5,4},{6,7},{7,6},{8,9},{9,8},{10,11... | collective-permute-start | bytes 196616 | tf_op jit(solution)/shard_map/ppermute | solution.py:462
  81.8 7.4 %collective-permute-start.25 = (bf16[256,128]{1,0:T(8,128)(2,1)S(1)}, bf16[256,128]{1,0:T(8,128)(2,1)S(1)}, u32[]{:S(2)}, u32[]{:S(2)}) collective-permute-start(bf16[256,128]{1,0:T(8,128)(2,1)S(1)} %get-tuple-element.60), channel_id=1, source_target_pairs={{0,2},{1,3},{2,0},{3,1},{4,6},{5,7},{6,4},{7,5},{8,10},{9,11},{10,... | collective-permute-start | bytes 196616 | tf_op jit(solution)/shard_map/ppermute | solution.py:462
  83.9 6.1 %collective-permute-start.26 = (bf16[256,128]{1,0:T(8,128)(2,1)S(1)}, bf16[256,128]{1,0:T(8,128)(2,1)S(1)}, u32[]{:S(2)}, u32[]{:S(2)}) collective-permute-start(bf16[256,128]{1,0:T(8,128)(2,1)S(1)} %get-tuple-element.61), channel_id=1, source_target_pairs={{0,3},{1,2},{2,1},{3,0},{4,7},{5,6},{6,5},{7,4},{8,11},{9,10},{10,... | collective-permute-start | bytes 196616 | tf_op jit(solution)/shard_map/ppermute | solution.py:462

commit v2 on v1

--- a/solution.py
+++ b/solution.py
@@ -59,48 +59,54 @@
     return block if shift == 0 else pltpu.roll(block, shift, 1)
 
 
-def packed(placed, codes, capacity):
-    features = placed.shape[0]
-    chunks, code_row = chunks_of(capacity, features)
-    lane = lax.broadcasted_iota(jnp.int32, (1, LANES), 1)
+def packed(placed, codes, chunks, code_row, shares):
     blocks, code_rows, height = [], jnp.zeros((CODE_ROWS, LANES), F32), 0
     code = lax.broadcasted_iota(jnp.int32, (CODE_ROWS, LANES), 0)
-    for n, (base, size, row, rows) in enumerate(chunks):
+    for n, (_, size, _, rows) in enumerate(chunks):
+        lanes = slice(n * LANES, (n + 1) * LANES)
         block = None
-        for part in range(LANES // size):
-            piece = turned(placed[part * rows : (part + 1) * rows], part * size - base)
-            here = lane >= part * size
-            block = piece if block is None else jnp.where(here, piece, block)
+        for q in range(LANES // size):
+            piece = turned(placed[q * rows : (q + 1) * rows, lanes], q * size)
+            block = piece if block is None else jnp.where(shares[n] == q, piece, block)
         blocks.append(block)
         height += rows
-        low = turned(codes, -base)[0:1]
-        high = turned(codes, size - base)[1:2]
-        both = jnp.where(lane < size, low, jnp.where(lane < 2 * size, high, 0.0))
+        low = codes[0:1, lanes]
+        high = turned(codes[:, lanes], size)[1:2]
+        both = jnp.where(shares[n] == 0, low, jnp.where(shares[n] == 1, high, 0.0))
         code_rows = jnp.where(code == n, both, code_rows)
     if height < code_row:
         blocks.append(jnp.zeros((code_row - height, LANES), F32))
     return jnp.concatenate([*blocks, code_rows], axis=0)
 
 
-def unpacked(block, features, capacity):
+def unpacked(recv_ref, first, count, features, capacity):
     chunks, code_row = chunks_of(capacity, features)
     lane = lax.broadcasted_iota(jnp.int32, (1, LANES), 1)
-    placed = jnp.zeros((features, LANES), F32)
-    low = jnp.zeros((1, LANES), F32)
-    high = jnp.zeros((1, LANES), F32)
-    codes = block[code_row:]
-    for n, (base, size, row, rows) in enumerate(chunks):
-        pieces = [
-            turned(block[row : row + rows], base - part * size) for part in range(LANES // size)
-        ]
-        here = (lane >= base) & (lane < min(base + size, capacity))
-        placed = jnp.where(here, jnp.concatenate(pieces, axis=0), placed)
-        low = jnp.where(here, turned(codes, base)[n : n + 1], low)
-        high = jnp.where(here, turned(codes, base - size)[n : n + 1], high)
-    return placed, low, high
-
-
-def dispatch_kernel(devices, capacity, *refs):
+    out = []
+    for n, (_, size, row, rows) in enumerate(chunks):
+        parts = LANES // size
+        share = lane // size
+        for start in range(first, first + count, parts):
+
+            def merged(q, lo, hi):
+                block = None
+                for s in range(parts):
+                    piece = recv_ref[start + s, lo:hi].astype(F32)
+                    here = share == (q + s) % parts
+                    block = piece if block is None else jnp.where(here, piece, block)
+                return turned(block, -q * size)
+
+            values = jnp.concatenate(
+                [merged(q, row, row + rows) for q in range(parts)], axis=0
+            )
+            low, high = (
+                merged(q, code_row, code_row + CODE_ROWS)[n : n + 1] for q in range(2)
+            )
+            out.append((values, low, high))
+    return [jnp.concatenate(part, axis=1) for part in zip(*out, strict=True)]
+
+
+def dispatch_kernel(devices, capacity, me_ref, *refs):
     sources, out_ref, (raw_ref, dest_ref, slot_ref, wide_ref, held), (sems, out_sems) = (
         refs[:4],
         refs[4],
@@ -134,9 +140,19 @@
         )
         base = base + counted[:, LANES:]
     rank = jnp.concatenate(ranks, axis=1)
-    place = (
-        lax.broadcasted_iota(jnp.int32, (LANES, rows), 0).astype(F32) == rank
-    ).astype(F32).astype(BF16)
+    plan, code_row = chunks_of(capacity, features)
+    lane = lax.broadcasted_iota(jnp.int32, (1, LANES), 1)
+    line = lax.broadcasted_iota(jnp.int32, (LANES, 1), 0)
+    shares, places = [], []
+    for first, size, _, _ in plan:
+        parts = LANES // size
+        turn = me_ref[0] % parts
+        shares.append((lane // size + parts - turn) % parts)
+        slot_of = line - turn * size
+        inside = (slot_of >= 0) & (slot_of < size)
+        wanted = jnp.where(inside, slot_of + first, -1).astype(F32)
+        places.append((wanted == rank).astype(F32).astype(BF16))
+    place = jnp.concatenate(places, axis=0)
     for copy in (copies[0], copies[2], copies[3]):
         copy.wait()
     slot = slot_ref[...]
@@ -157,7 +173,11 @@
         for d in range(GROUP):
             mine = placed[d * height : (d + 1) * height]
             held[first + d] = packed(
-                mine[:features], mine[features : features + CODE_ROWS], capacity
+                mine[:features],
+                mine[features : features + CODE_ROWS],
+                plan,
+                code_row,
+                shares,
             ).astype(BF16)
         writes.append(
             pltpu.make_async_copy(
@@ -169,13 +189,14 @@
         write.wait()
 
 
-def dispatch(raw, dest, slot, wide, devices, capacity):
+def dispatch(me, raw, dest, slot, wide, devices, capacity):
     features, rows = raw.shape
     shape = (devices, chunks_of(capacity, features)[1] + CODE_ROWS, LANES)
     return pl.pallas_call(
         functools.partial(dispatch_kernel, devices, capacity),
         out_shape=jax.ShapeDtypeStruct(shape, BF16),
-        in_specs=[pl.BlockSpec(memory_space=pltpu.HBM)] * 4,
+        in_specs=[pl.BlockSpec(memory_space=pltpu.SMEM)]
+        + [pl.BlockSpec(memory_space=pltpu.HBM)] * 4,
         out_specs=pl.BlockSpec(memory_space=pltpu.HBM),
         scratch_shapes=[
             pltpu.VMEM(raw.shape, raw.dtype),
@@ -186,7 +207,7 @@
         ],
         compiler_params=whole_vmem(),
         name="dispatch",
-    )(raw, dest, slot, wide)
+    )(me, raw, dest, slot, wide)
 
 
 def segment_kernel(capacity, upd, cols, recv_ref, proj_narrow_ref, proj_wide_ref, *refs):
@@ -202,18 +223,16 @@
     narrow, features = proj_narrow_ref.shape[0], proj_wide_ref.shape[0]
     nodes = user_ref.shape[0] + item_ref.shape[0]
     total = jnp.zeros((nodes, features + narrow), F32)
-    for first in range(0, devices, GROUP):
-        parts = [
-            unpacked(recv_ref[first + p].astype(F32), features, capacity) for p in range(GROUP)
-        ]
-        rows, low, high = (jnp.concatenate(part, axis=1) for part in zip(*parts, strict=True))
+    count = max(GROUP, *[LANES // chunk[1] for chunk in chunks_of(capacity, features)[0]])
+    for first in range(0, devices, count):
+        rows, low, high = unpacked(recv_ref, first, count, features, capacity)
         rows = rows.astype(BF16)
         high = high.astype(jnp.int32)
         node = low.astype(jnp.int32) + (high >> 1) * 256
         wide = (high & 1).astype(F32).astype(BF16)
         values = jnp.concatenate([rows * wide, rows[:narrow] * (1 - wide)], axis=0)
         hot = (
-            lax.broadcasted_iota(jnp.int32, (nodes, GROUP * LANES), 0) == node
+            lax.broadcasted_iota(jnp.int32, (nodes, node.shape[1]), 0) == node
         ).astype(F32).astype(BF16)
         total = total + lax.dot_general(hot, values, NT, preferred_element_type=F32)
     weights = jnp.concatenate([proj_wide_ref[...], proj_narrow_ref[...]], axis=0)
@@ -256,13 +275,14 @@
     )
 
 
-def dequantize_kernel(shape, place_ref, mask_ref, scale_ref, values_ref, *refs):
+def dequantize_kernel(shape, me_ref, mask_ref, scale_ref, values_ref, *refs):
     out_refs, (held, sems) = refs[:-2], refs[-2:]
     sides, chips, cols = shape
     upd, n = out_refs[0].shape
     ipd = n // (sides * chips)
-    chip, side_here = place_ref[0] // sides, place_ref[0] % sides
-    blocks = [peer_to(place_ref[1], k, cols) for k in range(cols)]
+    row_here, col_here = me_ref[0] // cols, me_ref[0] % cols
+    chip, side_here = row_here // sides, row_here % sides
+    blocks = [peer_to(col_here, k, cols) for k in range(cols)]
     lines = [
         peer_to(chip, k, chips) * sides + (side_here + side) % sides
         for side in range(sides)
@@ -296,7 +316,7 @@
                     ).astype(BF16)
 
 
-def dequantize(place, values, mask, scale, shape):
+def dequantize(me, values, mask, scale, shape):
     m, n = values.shape
     sides, chips, cols = shape
     smem = pl.BlockSpec(memory_space=pltpu.SMEM)
@@ -312,7 +332,7 @@
         compiler_params=no_room(),
         cost_estimate=pl.CostEstimate(flops=m * n, bytes_accessed=4 * m * n, transcendentals=0),
         name="dequantize",
-    )(place, mask, scale, values)
+    )(me, mask, scale, values)
 
 
 def from_order(n):
@@ -495,8 +515,9 @@
     layers = weight_sum.shape[0]
     sides = 2 if rows % 2 == 0 else 1
     chips = rows // sides
-    place = jnp.stack([lax.axis_index("row"), lax.axis_index("col")]).astype(jnp.int32)
+    me = lax.axis_index(("row", "col")).astype(jnp.int32).reshape(1)
     send = dispatch(
+        me,
         raw_rows.T,
         raw_dest.reshape(1, count),
         raw_slot.reshape(1, count),
@@ -506,7 +527,7 @@
     )
     recv = lax.all_to_all(send, ("row", "col"), split_axis=0, concat_axis=0, tiled=True)
     adjacency = dequantize(
-        place, adj_values, tile_mask, tile_scale, (sides, chips, cols)
+        me, adj_values, tile_mask, tile_scale, (sides, chips, cols)
     )
     users, users_t, items, *adjacency = segment(
         recv, proj_narrow, proj_wide, adjacency, upd, ipd, capacity

time: 91.2 us -> 91 us (level)
  no operation moved by 1% of the time
where the time goes in v2:
time: 91 us; the launch traced here: 90.7 us
  starting transfers between devices  42.8 us (47%)
  waiting for transfers between devices  26.7 us (29%)
  Pallas kernels  18.1 us (20%)
  local copies, waits for them, and re-layouts  2.35 us (3%)
    ppermute x24, starting transfers between devices, exchange(): received.append(lax.ppermute(blocks[k], axis, pairs))  34.2 us
    ppermute x24, waiting for transfers between devices, exchange(): received.append(lax.ppermute(blocks[k], axis, pairs))  21.1 us
    all_to_all x1, starting transfers between devices, per_device(): lax.all_to_all(send, ('row', 'col'), split_axis=0, concat_axis=0, tiled=T...  7.33 us
    all_to_all x1, waiting for transfers between devices, per_device(): lax.all_to_all(send, ('row', 'col'), split_axis=0, concat_axis=0, tiled=T...  5.57 us
    pallas_call x1, Pallas kernels, dequantize(): pl.pallas_call(functools.partial(dequantize_kernel, shape), out_shape=(ja...  5.04 us
    pallas_call x1, Pallas kernels, dispatch(): pl.pallas_call(functools.partial(dispatch_kernel, devices, capacity), out...  3.38 us
    pallas_call x1, Pallas kernels, segment(): pl.pallas_call(functools.partial(segment_kernel, capacity, upd, cols), ou...  3.3 us
    pallas_call x2, Pallas kernels, user_sums(): pl.pallas_call(functools.partial(user_sum_kernel, cols), out_shape=(jax.S...  2.49 us
  transfers between devices with their start and end apart: 35, of which 14 were waited for; matrix products, arithmetic and copies ran while one was open for 0% of the time, Pallas kernels for 12%

profile of v2, /device:TPU:0, one launch (start us, length us, event | category | flops | bytes accessed | tf_op | source)
XLA Modules:
  0.0 90.7 jit_solution(2470920683129979830)
XLA Ops:
  0.6 3.4 %dispatch.1 = bf16[32,56,128]{2,1,0:T(8,128)(2,1)} custom-call(s32[1]{0:T(128)} %bitcast.me_ref, bf16[64,1024]{1,0:T(8,128)(2,1)} %bitcast.6, s32[1,1024]{1,0:T(1,128)} %bitcast.8, s32[1,1024]{1,0:T(1,128)} %bitcast.9, s32[1,1024]{1,0:T(1,128)} %bitcast.10), custom_call_target="tpu_custom_call" | custom-call | tf_op jit(solution)/shard_map/dispatch/pallas_call | solution.py:195
  4.0 7.3 %all-to-all-start = ((bf16[32,56,128]{2,1,0:T(8,128)(2,1)}), bf16[32,56,128]{2,1,0:T(8,128)(2,1)S(1)}, u32[]{:S(2)}, u32[]{:S(2)}) async-start(bf16[32,56,128]{2,1,0:T(8,128)(2,1)} %dispatch.1), calls=%async_computation | async-start | bytes 917504 | tf_op jit(solution)/shard_map/all_to_all | solution.py:528
  11.4 0.7 copy-done.5
  12.1 0.7 copy-done.6
  12.8 5.0 %dequantize.1 = (bf16[256,2048]{1,0:T(8,128)(2,1)S(1)}, bf16[256,2048]{1,0:T(8,128)(2,1)}, bf16[256,2048]{1,0:T(8,128)(2,1)}, bf16[256,2048]{1,0:T(8,128)(2,1)}) custom-call(s32[1]{0:T(128)} %bitcast.me_ref, s32[8,16]{1,0:T(8,128)S(1)} %copy-done.5, f32[8,16]{1,0:T(8,128)S(1)} %copy-done.6, bf16[1024,2048]{1,0:T(8,128)(2,1)} %values_ref.1), custom_call_target="tpu_custom_call" | custom-call | flops 2097152 | bytes 8388608 | tf_op jit(solution)/shard_map/dequantize/pallas_call | solution.py:323
  17.8 1.0 %copy-done = bf16[256,2048]{1,0:T(8,128)(2,1)} copy-done((bf16[256,2048]{1,0:T(8,128)(2,1)}, bf16[256,2048]{1,0:T(8,128)(2,1)S(1)}, u32[]{:S(2)}) %copy-start) | copy-done | bytes 1048600
  18.8 5.6 %all-to-all-done.recv_ref = bf16[32,56,128]{2,1,0:T(8,128)(2,1)S(1)} async-done(((bf16[32,56,128]{2,1,0:T(8,128)(2,1)}), bf16[32,56,128]{2,1,0:T(8,128)(2,1)S(1)}, u32[]{:S(2)}, u32[]{:S(2)}) %all-to-all-start) | async-done | bytes 458784 | tf_op jit(solution)/shard_map/all_to_all | solution.py:528
  24.4 3.3 %segment.1 = (bf16[256,128]{1,0:T(8,128)(2,1)S(1)}, bf16[128,256]{1,0:T(8,128)(2,1)S(1)}, bf16[256,128]{1,0:T(8,128)(2,1)S(1)}, bf16[256,2048]{1,0:T(8,128)(2,1)...) custom-call(bf16[32,56,128]{2,1,0:T(8,128)(2,1)S(1)} %all-to-all-done.recv_ref, ...), custom_call_target="tpu_custom_call" | custom-call | tf_op jit(solution)/shard_map/segment/pallas_call | solution.py:257
  27.7 2.9 %collective-permute-start.12 = (bf16[128,256]{1,0:T(8,128)(2,1)S(1)}, bf16[128,256]{1,0:T(8,128)(2,1)S(1)}, u32[]{:S(2)}, u32[]{:S(2)}) collective-permute-start(bf16[128,256]{1,0:T(8,128)(2,1)S(1)} %get-tuple-element.51.refs_4_), channel_id=1, source_target_pairs={{0,3},{1,2},{2,1},{3,0},{4,7},{5,6},{6,5},{7,4},{8,11},{9,10},{10,... | collective-permute-start | bytes 196616 | tf_op jit(solution)/shard_map/ppermute | solution.py:482
  30.5 1.1 %collective-permute-start.11 = (bf16[128,256]{1,0:T(8,128)(2,1)S(1)}, bf16[128,256]{1,0:T(8,128)(2,1)S(1)}, u32[]{:S(2)}, u32[]{:S(2)}) collective-permute-start(bf16[128,256]{1,0:T(8,128)(2,1)S(1)} %get-tuple-element.51.refs_4_), channel_id=1, source_target_pairs={{0,2},{1,3},{2,0},{3,1},{4,6},{5,7},{6,4},{7,5},{8,10},{9,11},{10,... | collective-permute-start | bytes 196616 | tf_op jit(solution)/shard_map/ppermute | solution.py:482
  31.6 0.8 collective-permute-start.2
  32.5 1.1 %collective-permute-start.1 = (bf16[256,128]{1,0:T(8,128)(2,1)S(1)}, bf16[256,128]{1,0:T(8,128)(2,1)S(1)}, u32[]{:S(2)}, u32[]{:S(2)}) collective-permute-start(bf16[256,128]{1,0:T(8,128)(2,1)S(1)} %get-tuple-element.45.refs_4_.own_ref), channel_id=1, source_target_pairs={{0,16},{4,20},{8,24},{12,28},{16,0},{20,4},{24,8},{28,12},{1,17},{... | collective-permute-start | bytes 196616 | tf_op jit(solution)/shard_map/ppermute | solution.py:482
  33.5 1.6 %collective-permute-start = (bf16[256,128]{1,0:T(8,128)(2,1)S(1)}, bf16[256,128]{1,0:T(8,128)(2,1)S(1)}, u32[]{:S(2)}, u32[]{:S(2)}) collective-permute-start(bf16[256,128]{1,0:T(8,128)(2,1)S(1)} %get-tuple-element.45.refs_4_.own_ref), channel_id=1, source_target_pairs={{0,8},{4,12},{8,0},{12,4},{16,24},{20,28},{24,16},{28,20},{1,9},{5... | collective-permute-start | bytes 196616 | tf_op jit(solution)/shard_map/ppermute | solution.py:482
  35.1 2.7 %collective-permute-start.10 = (bf16[128,256]{1,0:T(8,128)(2,1)S(1)}, bf16[128,256]{1,0:T(8,128)(2,1)S(1)}, u32[]{:S(2)}, u32[]{:S(2)}) collective-permute-start(bf16[128,256]{1,0:T(8,128)(2,1)S(1)} %get-tuple-element.51.refs_4_), channel_id=1, source_target_pairs={{0,1},{1,0},{2,3},{3,2},{4,5},{5,4},{6,7},{7,6},{8,9},{9,8},{10,11... | collective-permute-start | bytes 196616 | tf_op jit(solution)/shard_map/ppermute | solution.py:482
  38.1 0.5 collective-permute-start.6
  38.7 0.4 collective-permute-start.4
  39.1 1.0 %collective-permute-done.10.refs_5_ = bf16[128,256]{1,0:T(8,128)(2,1)S(1)} collective-permute-done((bf16[128,256]{1,0:T(8,128)(2,1)S(1)}, bf16[128,256]{1,0:T(8,128)(2,1)S(1)}, u32[]{:S(2)}, u32[]{:S(2)}) %collective-permute-start.10) | collective-permute-done | bytes 65568 | tf_op jit(solution)/shard_map/ppermute | solution.py:482
  40.1 0.7 item_sums.2
  40.9 1.2 %user_sums.2 = (bf16[256,128]{1,0:T(8,128)(2,1)S(1)}, bf16[256,128]{1,0:T(8,128)(2,1)S(1)}, bf16[256,128]{1,0:T(8,128)(2,1)S(1)}, bf16[256,128]{1,0:T(8,128)(2,1)S(1)}) custom-call(bf16[256,2048]{1,0:T(8,128)(2,1)S(1)} %get-tuple-element.41.refs_0_, bf16[256,2048]{1,0:T(8,128)(2,1)S(1)} %get-tuple-element.42.refs_1_, ...), custom_call_target="tpu_custom_call" | custom-call | flops 536870912 | bytes 4194304 | tf_op jit(solution)/shard_map/user_sums/pallas_call | solution.py:353
  42.2 2.1 %collective-permute-start.7 = (bf16[256,128]{1,0:T(8,128)(2,1)S(1)}, bf16[256,128]{1,0:T(8,128)(2,1)S(1)}, u32[]{:S(2)}, u32[]{:S(2)}) collective-permute-start(bf16[256,128]{1,0:T(8,128)(2,1)S(1)} %get-tuple-element.47), channel_id=1, source_target_pairs={{0,1},{1,0},{2,3},{3,2},{4,5},{5,4},{6,7},{7,6},{8,9},{9,8},{10,11... | collective-permute-start | bytes 196616 | tf_op jit(solution)/shard_map/ppermute | solution.py:482
  44.3 2.4 %collective-permute-start.9 = (bf16[256,128]{1,0:T(8,128)(2,1)S(1)}, bf16[256,128]{1,0:T(8,128)(2,1)S(1)}, u32[]{:S(2)}, u32[]{:S(2)}) collective-permute-start(bf16[256,128]{1,0:T(8,128)(2,1)S(1)} %get-tuple-element.49), channel_id=1, source_target_pairs={{0,3},{1,2},{2,1},{3,0},{4,7},{5,6},{6,5},{7,4},{8,11},{9,10},{10,... | collective-permute-start | bytes 196616 | tf_op jit(solution)/shard_map/ppermute | solution.py:482
  46.7 0.3 collective-permute-done.7.refs_1_
  47.0 5.0 %collective-permute-done.8.refs_2_ = bf16[256,128]{1,0:T(8,128)(2,1)S(1)} collective-permute-done((bf16[256,128]{1,0:T(8,128)(2,1)S(1)}, bf16[256,128]{1,0:T(8,128)(2,1)S(1)}, u32[]{:S(2)}, u32[]{:S(2)}) %collective-permute-start.8) | collective-permute-done | bytes 65568 | tf_op jit(solution)/shard_map/ppermute | solution.py:482
  52.3 1.5 %collective-permute-start.29 = (bf16[128,256]{1,0:T(8,128)(2,1)S(1)}, bf16[128,256]{1,0:T(8,128)(2,1)S(1)}, u32[]{:S(2)}, u32[]{:S(2)}) collective-permute-start(bf16[128,256]{1,0:T(8,128)(2,1)S(1)} %get-tuple-element.63.refs_4_), channel_id=1, source_target_pairs={{0,3},{1,2},{2,1},{3,0},{4,7},{5,6},{6,5},{7,4},{8,11},{9,10},{10,... | collective-permute-start | bytes 196616 | tf_op jit(solution)/shard_map/ppermute | solution.py:482
  53.8 2.0 %collective-permute-start.28 = (bf16[128,256]{1,0:T(8,128)(2,1)S(1)}, bf16[128,256]{1,0:T(8,128)(2,1)S(1)}, u32[]{:S(2)}, u32[]{:S(2)}) collective-permute-start(bf16[128,256]{1,0:T(8,128)(2,1)S(1)} %get-tuple-element.63.refs_4_), channel_id=1, source_target_pairs={{0,2},{1,3},{2,0},{3,1},{4,6},{5,7},{6,4},{7,5},{8,10},{9,11},{10,... | collective-permute-start | bytes 196616 | tf_op jit(solution)/shard_map/ppermute | solution.py:482
  55.8 1.0 %collective-permute-start.27 = (bf16[128,256]{1,0:T(8,128)(2,1)S(1)}, bf16[128,256]{1,0:T(8,128)(2,1)S(1)}, u32[]{:S(2)}, u32[]{:S(2)}) collective-permute-start(bf16[128,256]{1,0:T(8,128)(2,1)S(1)} %get-tuple-element.63.refs_4_), channel_id=1, source_target_pairs={{0,1},{1,0},{2,3},{3,2},{4,5},{5,4},{6,7},{7,6},{8,9},{9,8},{10,11... | collective-permute-start | bytes 196616 | tf_op jit(solution)/shard_map/ppermute | solution.py:482
  56.8 2.4 %collective-permute-done.29.refs_7_ = bf16[128,256]{1,0:T(8,128)(2,1)S(1)} collective-permute-done((bf16[128,256]{1,0:T(8,128)(2,1)S(1)}, bf16[128,256]{1,0:T(8,128)(2,1)S(1)}, u32[]{:S(2)}, u32[]{:S(2)}) %collective-permute-start.29) | collective-permute-done | bytes 65568 | tf_op jit(solution)/shard_map/ppermute | solution.py:482
  59.2 2.8 %collective-permute-done.28.refs_6_ = bf16[128,256]{1,0:T(8,128)(2,1)S(1)} collective-permute-done((bf16[128,256]{1,0:T(8,128)(2,1)S(1)}, bf16[128,256]{1,0:T(8,128)(2,1)S(1)}, u32[]{:S(2)}, u32[]{:S(2)}) %collective-permute-start.28) | collective-permute-done | bytes 65568 | tf_op jit(solution)/shard_map/ppermute | solution.py:482
  62.0 0.7 item_sums.3
  63.1 3.3 %collective-permute-start.16 = (bf16[128,256]{1,0:T(8,128)(2,1)S(1)}, bf16[128,256]{1,0:T(8,128)(2,1)S(1)}, u32[]{:S(2)}, u32[]{:S(2)}) collective-permute-start(bf16[128,256]{1,0:T(8,128)(2,1)S(1)} %get-tuple-element.57), channel_id=1, source_target_pairs={{0,24},{4,28},{8,16},{12,20},{16,8},{20,12},{24,0},{28,4},{1,25},{... | collective-permute-start | bytes 196616 | tf_op jit(solution)/shard_map/ppermute | solution.py:482
  66.4 1.1 %collective-permute-done.14.refs_1_ = bf16[128,256]{1,0:T(8,128)(2,1)S(1)} collective-permute-done((bf16[128,256]{1,0:T(8,128)(2,1)S(1)}, bf16[128,256]{1,0:T(8,128)(2,1)S(1)}, u32[]{:S(2)}, u32[]{:S(2)}) %collective-permute-start.14) | collective-permute-done | bytes 65568 | tf_op jit(solution)/shard_map/ppermute | solution.py:482
  67.5 1.3 %collective-permute-done.15.refs_2_ = bf16[128,256]{1,0:T(8,128)(2,1)S(1)} collective-permute-done((bf16[128,256]{1,0:T(8,128)(2,1)S(1)}, bf16[128,256]{1,0:T(8,128)(2,1)S(1)}, u32[]{:S(2)}, u32[]{:S(2)}) %collective-permute-start.15) | collective-permute-done | bytes 65568 | tf_op jit(solution)/shard_map/ppermute | solution.py:482
  69.2 2.8 %collective-permute-start.19 = (bf16[256,128]{1,0:T(8,128)(2,1)S(1)}, bf16[256,128]{1,0:T(8,128)(2,1)S(1)}, u32[]{:S(2)}, u32[]{:S(2)}) collective-permute-start(bf16[256,128]{1,0:T(8,128)(2,1)S(1)} %item_update.2.refs_4_.own_ref), channel_id=1, source_target_pairs={{0,24},{4,28},{8,16},{12,20},{16,8},{20,12},{24,0},{28,4},{1,25},{... | collective-permute-start | bytes 196616 | tf_op jit(solution)/shard_map/ppermute | solution.py:482
  71.9 0.5 collective-permute-start.18
  72.4 0.3 collective-permute-start.17
  72.7 1.9 %collective-permute-done.19.refs_7_ = bf16[256,128]{1,0:T(8,128)(2,1)S(1)} collective-permute-done((bf16[256,128]{1,0:T(8,128)(2,1)S(1)}, bf16[256,128]{1,0:T(8,128)(2,1)S(1)}, u32[]{:S(2)}, u32[]{:S(2)}) %collective-permute-start.19) | collective-permute-done | bytes 65568 | tf_op jit(solution)/shard_map/ppermute | solution.py:482
  74.6 1.6 %collective-permute-done.18.refs_6_ = bf16[256,128]{1,0:T(8,128)(2,1)S(1)} collective-permute-done((bf16[256,128]{1,0:T(8,128)(2,1)S(1)}, bf16[256,128]{1,0:T(8,128)(2,1)S(1)}, u32[]{:S(2)}, u32[]{:S(2)}) %collective-permute-start.18) | collective-permute-done | bytes 65568 | tf_op jit(solution)/shard_map/ppermute | solution.py:482
  76.2 0.5 collective-permute-done.17.refs_5_
  76.7 0.8 collective-permute-start.31
  77.6 0.9 %collective-permute-start.32 = (bf16[128,256]{1,0:T(8,128)(2,1)S(1)}, bf16[128,256]{1,0:T(8,128)(2,1)S(1)}, u32[]{:S(2)}, u32[]{:S(2)}) collective-permute-start(bf16[128,256]{1,0:T(8,128)(2,1)S(1)} %get-tuple-element.68), channel_id=1, source_target_pairs={{0,16},{4,20},{8,24},{12,28},{16,0},{20,4},{24,8},{28,12},{1,17},{... | collective-permute-start | bytes 196616 | tf_op jit(solution)/shard_map/ppermute | solution.py:482
  78.5 1.8 %collective-permute-start.33 = (bf16[128,256]{1,0:T(8,128)(2,1)S(1)}, bf16[128,256]{1,0:T(8,128)(2,1)S(1)}, u32[]{:S(2)}, u32[]{:S(2)}) collective-permute-start(bf16[128,256]{1,0:T(8,128)(2,1)S(1)} %get-tuple-element.69), channel_id=1, source_target_pairs={{0,24},{4,28},{8,16},{12,20},{16,8},{20,12},{24,0},{28,4},{1,25},{... | collective-permute-start | bytes 196616 | tf_op jit(solution)/shard_map/ppermute | solution.py:482
  80.3 1.2 %user_sums.3 = (bf16[256,128]{1,0:T(8,128)(2,1)S(1)}, bf16[256,128]{1,0:T(8,128)(2,1)S(1)}, bf16[256,128]{1,0:T(8,128)(2,1)S(1)}, bf16[256,128]{1,0:T(8,128)(2,1)S(1)}) custom-call(bf16[256,2048]{1,0:T(8,128)(2,1)S(1)} %get-tuple-element.41.refs_0_, bf16[256,2048]{1,0:T(8,128)(2,1)S(1)} %get-tuple-element.42.refs_1_, ...), custom_call_target="tpu_custom_call" | custom-call | flops 536870912 | bytes 4194304 | tf_op jit(solution)/shard_map/user_sums/pallas_call | solution.py:353
  81.6 2.1 %collective-permute-start.25 = (bf16[256,128]{1,0:T(8,128)(2,1)S(1)}, bf16[256,128]{1,0:T(8,128)(2,1)S(1)}, u32[]{:S(2)}, u32[]{:S(2)}) collective-permute-start(bf16[256,128]{1,0:T(8,128)(2,1)S(1)} %get-tuple-element.60), channel_id=1, source_target_pairs={{0,2},{1,3},{2,0},{3,1},{4,6},{5,7},{6,4},{7,5},{8,10},{9,11},{10,... | collective-permute-start | bytes 196616 | tf_op jit(solution)/shard_map/ppermute | solution.py:482
  83.7 2.3 %collective-permute-start.26 = (bf16[256,128]{1,0:T(8,128)(2,1)S(1)}, bf16[256,128]{1,0:T(8,128)(2,1)S(1)}, u32[]{:S(2)}, u32[]{:S(2)}) collective-permute-start(bf16[256,128]{1,0:T(8,128)(2,1)S(1)} %get-tuple-element.61), channel_id=1, source_target_pairs={{0,3},{1,2},{2,1},{3,0},{4,7},{5,6},{6,5},{7,4},{8,11},{9,10},{10,... | collective-permute-start | bytes 196616 | tf_op jit(solution)/shard_map/ppermute | solution.py:482
  86.0 0.9 item_update.3
  86.9 2.2 %collective-permute-done.25.refs_2_ = bf16[256,128]{1,0:T(8,128)(2,1)S(1)} collective-permute-done((bf16[256,128]{1,0:T(8,128)(2,1)S(1)}, bf16[256,128]{1,0:T(8,128)(2,1)S(1)}, u32[]{:S(2)}, u32[]{:S(2)}) %collective-permute-start.25) | collective-permute-done | bytes 65568 | tf_op jit(solution)/shard_map/ppermute | solution.py:482
  89.1 0.7 collective-permute-done.26.refs_3_
  89.8 0.9 user_update.3
  (49 shorter events, 1.5 us)
Async XLA Ops:
  4.0 20.3 %copy-start.3 = (bf16[64,128]{1,0:T(8,128)(2,1)S(1)}, bf16[64,128]{1,0:T(8,128)(2,1)}, u32[]{:S(2)}) copy-start(bf16[64,128]{1,0:T(8,128)(2,1)} %proj_wide_ref.1) | copy-start | bytes 49156
  4.0 20.3 %copy-start.4 = (bf16[32,128]{1,0:T(8,128)(2,1)S(1)}, bf16[32,128]{1,0:T(8,128)(2,1)}, u32[]{:S(2)}) copy-start(bf16[32,128]{1,0:T(8,128)(2,1)} %proj_narrow_ref.1) | copy-start | bytes 24580
  4.0 20.3 %all-to-all-start = ((bf16[32,56,128]{2,1,0:T(8,128)(2,1)}), bf16[32,56,128]{2,1,0:T(8,128)(2,1)S(1)}, u32[]{:S(2)}, u32[]{:S(2)}) async-start(bf16[32,56,128]{2,1,0:T(8,128)(2,1)} %dispatch.1), calls=%async_computation | async-start | bytes 917504 | tf_op jit(solution)/shard_map/all_to_all | solution.py:528
  11.4 0.7 copy-start.5
  12.1 0.7 copy-start.6
  17.8 1.0 %copy-start = (bf16[256,2048]{1,0:T(8,128)(2,1)}, bf16[256,2048]{1,0:T(8,128)(2,1)S(1)}, u32[]{:S(2)}) copy-start(bf16[256,2048]{1,0:T(8,128)(2,1)S(1)} %get-tuple-element.36.refs_0_) | copy-start | bytes 3145732
  27.7 7.4 %collective-permute-start.12 = (bf16[128,256]{1,0:T(8,128)(2,1)S(1)}, bf16[128,256]{1,0:T(8,128)(2,1)S(1)}, u32[]{:S(2)}, u32[]{:S(2)}) collective-permute-start(bf16[128,256]{1,0:T(8,128)(2,1)S(1)} %get-tuple-element.51.refs_4_), channel_id=1, source_target_pairs={{0,3},{1,2},{2,1},{3,0},{4,7},{5,6},{6,5},{7,4},{8,11},{9,10},{10,... | collective-permute-start | bytes 196616 | tf_op jit(solution)/shard_map/ppermute | solution.py:482
  30.5 7.5 %collective-permute-start.11 = (bf16[128,256]{1,0:T(8,128)(2,1)S(1)}, bf16[128,256]{1,0:T(8,128)(2,1)S(1)}, u32[]{:S(2)}, u32[]{:S(2)}) collective-permute-start(bf16[128,256]{1,0:T(8,128)(2,1)S(1)} %get-tuple-element.51.refs_4_), channel_id=1, source_target_pairs={{0,2},{1,3},{2,0},{3,1},{4,6},{5,7},{6,4},{7,5},{8,10},{9,11},{10,... | collective-permute-start | bytes 196616 | tf_op jit(solution)/shard_map/ppermute | solution.py:482
  31.6 6.5 %collective-permute-start.2 = (bf16[256,128]{1,0:T(8,128)(2,1)S(1)}, bf16[256,128]{1,0:T(8,128)(2,1)S(1)}, u32[]{:S(2)}, u32[]{:S(2)}) collective-permute-start(bf16[256,128]{1,0:T(8,128)(2,1)S(1)} %get-tuple-element.45.refs_4_.own_ref), channel_id=1, source_target_pairs={{0,24},{4,28},{8,16},{12,20},{16,8},{20,12},{24,0},{28,4},{1,25},{... | collective-permute-start | bytes 196616 | tf_op jit(solution)/shard_map/ppermute | solution.py:482
  32.5 6.2 %collective-permute-start.1 = (bf16[256,128]{1,0:T(8,128)(2,1)S(1)}, bf16[256,128]{1,0:T(8,128)(2,1)S(1)}, u32[]{:S(2)}, u32[]{:S(2)}) collective-permute-start(bf16[256,128]{1,0:T(8,128)(2,1)S(1)} %get-tuple-element.45.refs_4_.own_ref), channel_id=1, source_target_pairs={{0,16},{4,20},{8,24},{12,28},{16,0},{20,4},{24,8},{28,12},{1,17},{... | collective-permute-start | bytes 196616 | tf_op jit(solution)/shard_map/ppermute | solution.py:482
  33.5 5.1 %collective-permute-start = (bf16[256,128]{1,0:T(8,128)(2,1)S(1)}, bf16[256,128]{1,0:T(8,128)(2,1)S(1)}, u32[]{:S(2)}, u32[]{:S(2)}) collective-permute-start(bf16[256,128]{1,0:T(8,128)(2,1)S(1)} %get-tuple-element.45.refs_4_.own_ref), channel_id=1, source_target_pairs={{0,8},{4,12},{8,0},{12,4},{16,24},{20,28},{24,16},{28,20},{1,9},{5... | collective-permute-start | bytes 196616 | tf_op jit(solution)/shard_map/ppermute | solution.py:482
  35.1 5.0 %collective-permute-start.10 = (bf16[128,256]{1,0:T(8,128)(2,1)S(1)}, bf16[128,256]{1,0:T(8,128)(2,1)S(1)}, u32[]{:S(2)}, u32[]{:S(2)}) collective-permute-start(bf16[128,256]{1,0:T(8,128)(2,1)S(1)} %get-tuple-element.51.refs_4_), channel_id=1, source_target_pairs={{0,1},{1,0},{2,3},{3,2},{4,5},{5,4},{6,7},{7,6},{8,9},{9,8},{10,11... | collective-permute-start | bytes 196616 | tf_op jit(solution)/shard_map/ppermute | solution.py:482
  38.1 2.8 %collective-permute-start.3 = (bf16[256,128]{1,0:T(8,128)(2,1)S(1)}, bf16[256,128]{1,0:T(8,128)(2,1)S(1)}, u32[]{:S(2)}, u32[]{:S(2)}) collective-permute-start(bf16[256,128]{1,0:T(8,128)(2,1)S(1)} %get-tuple-element.45.refs_4_.own_ref), channel_id=1, source_target_pairs={{0,4},{4,0},{8,12},{12,8},{16,20},{20,16},{24,28},{28,24},{1,5},{5... | collective-permute-start | bytes 196616 | tf_op jit(solution)/shard_map/ppermute | solution.py:487
  38.1 2.8 %collective-permute-start.6 = (bf16[256,128]{1,0:T(8,128)(2,1)S(1)}, bf16[256,128]{1,0:T(8,128)(2,1)S(1)}, u32[]{:S(2)}, u32[]{:S(2)}) collective-permute-start(bf16[256,128]{1,0:T(8,128)(2,1)S(1)} %collective-permute-done.2.refs_7_), channel_id=1, source_target_pairs={{0,4},{4,0},{8,12},{12,8},{16,20},{20,16},{24,28},{28,24},{1,5},{5... | collective-permute-start | bytes 196616 | tf_op jit(solution)/shard_map/ppermute | solution.py:487
  38.6 2.3 %collective-permute-start.5 = (bf16[256,128]{1,0:T(8,128)(2,1)S(1)}, bf16[256,128]{1,0:T(8,128)(2,1)S(1)}, u32[]{:S(2)}, u32[]{:S(2)}) collective-permute-start(bf16[256,128]{1,0:T(8,128)(2,1)S(1)} %collective-permute-done.1.refs_6_), channel_id=1, source_target_pairs={{0,4},{4,0},{8,12},{12,8},{16,20},{20,16},{24,28},{28,24},{1,5},{5... | collective-permute-start | bytes 196616 | tf_op jit(solution)/shard_map/ppermute | solution.py:487
  38.7 2.3 %collective-permute-start.4 = (bf16[256,128]{1,0:T(8,128)(2,1)S(1)}, bf16[256,128]{1,0:T(8,128)(2,1)S(1)}, u32[]{:S(2)}, u32[]{:S(2)}) collective-permute-start(bf16[256,128]{1,0:T(8,128)(2,1)S(1)} %collective-permute-done.refs_5_), channel_id=1, source_target_pairs={{0,4},{4,0},{8,12},{12,8},{16,20},{20,16},{24,28},{28,24},{1,5},{5... | collective-permute-start | bytes 196616 | tf_op jit(solution)/shard_map/ppermute | solution.py:487
  40.1 12.0 %copy-start.1 = (bf16[2,128,128]{2,1,0:T(8,128)(2,1)S(1)}, bf16[2,128,128]{2,1,0:T(8,128)(2,1)}, u32[]{:S(2)}) copy-start(bf16[2,128,128]{2,1,0:T(8,128)(2,1)} %sum_ref.7) | copy-start | bytes 196612
  40.1 12.0 %copy-start.2 = (bf16[2,128,128]{2,1,0:T(8,128)(2,1)S(1)}, bf16[2,128,128]{2,1,0:T(8,128)(2,1)}, u32[]{:S(2)}) copy-start(bf16[2,128,128]{2,1,0:T(8,128)(2,1)} %product_ref.7) | copy-start | bytes 196612
  40.8 22.0 %collective-permute-start.13 = (bf16[4,128,256]{2,1,0:T(8,128)(2,1)S(1)}, bf16[4,128,256]{2,1,0:T(8,128)(2,1)S(1)}, u32[]{:S(2)}, u32[]{:S(2)}) collective-permute-start(bf16[4,128,256]{2,1,0:T(8,128)(2,1)S(1)} %get-tuple-element.53), channel_id=1, source_target_pairs={{0,4},{4,0},{8,12},{12,8},{16,20},{20,16},{24,28},{28,24},{1,5},{5... | collective-permute-start | bytes 786440 | tf_op jit(solution)/shard_map/ppermute | solution.py:487
  42.2 4.8 %collective-permute-start.7 = (bf16[256,128]{1,0:T(8,128)(2,1)S(1)}, bf16[256,128]{1,0:T(8,128)(2,1)S(1)}, u32[]{:S(2)}, u32[]{:S(2)}) collective-permute-start(bf16[256,128]{1,0:T(8,128)(2,1)S(1)} %get-tuple-element.47), channel_id=1, source_target_pairs={{0,1},{1,0},{2,3},{3,2},{4,5},{5,4},{6,7},{7,6},{8,9},{9,8},{10,11... | collective-permute-start | bytes 196616 | tf_op jit(solution)/shard_map/ppermute | solution.py:482
  44.3 7.8 %collective-permute-start.8 = (bf16[256,128]{1,0:T(8,128)(2,1)S(1)}, bf16[256,128]{1,0:T(8,128)(2,1)S(1)}, u32[]{:S(2)}, u32[]{:S(2)}) collective-permute-start(bf16[256,128]{1,0:T(8,128)(2,1)S(1)} %get-tuple-element.48), channel_id=1, source_target_pairs={{0,2},{1,3},{2,0},{3,1},{4,6},{5,7},{6,4},{7,5},{8,10},{9,11},{10,... | collective-permute-start | bytes 196616 | tf_op jit(solution)/shard_map/ppermute | solution.py:482
  44.3 7.8 %collective-permute-start.9 = (bf16[256,128]{1,0:T(8,128)(2,1)S(1)}, bf16[256,128]{1,0:T(8,128)(2,1)S(1)}, u32[]{:S(2)}, u32[]{:S(2)}) collective-permute-start(bf16[256,128]{1,0:T(8,128)(2,1)S(1)} %get-tuple-element.49), channel_id=1, source_target_pairs={{0,3},{1,2},{2,1},{3,0},{4,7},{5,6},{6,5},{7,4},{8,11},{9,10},{10,... | collective-permute-start | bytes 196616 | tf_op jit(solution)/shard_map/ppermute | solution.py:482
  52.3 6.8 %collective-permute-start.29 = (bf16[128,256]{1,0:T(8,128)(2,1)S(1)}, bf16[128,256]{1,0:T(8,128)(2,1)S(1)}, u32[]{:S(2)}, u32[]{:S(2)}) collective-permute-start(bf16[128,256]{1,0:T(8,128)(2,1)S(1)} %get-tuple-element.63.refs_4_), channel_id=1, source_target_pairs={{0,3},{1,2},{2,1},{3,0},{4,7},{5,6},{6,5},{7,4},{8,11},{9,10},{10,... | collective-permute-start | bytes 196616 | tf_op jit(solution)/shard_map/ppermute | solution.py:482
  53.8 8.2 %collective-permute-start.28 = (bf16[128,256]{1,0:T(8,128)(2,1)S(1)}, bf16[128,256]{1,0:T(8,128)(2,1)S(1)}, u32[]{:S(2)}, u32[]{:S(2)}) collective-permute-start(bf16[128,256]{1,0:T(8,128)(2,1)S(1)} %get-tuple-element.63.refs_4_), channel_id=1, source_target_pairs={{0,2},{1,3},{2,0},{3,1},{4,6},{5,7},{6,4},{7,5},{8,10},{9,11},{10,... | collective-permute-start | bytes 196616 | tf_op jit(solution)/shard_map/ppermute | solution.py:482
  55.8 6.2 %collective-permute-start.27 = (bf16[128,256]{1,0:T(8,128)(2,1)S(1)}, bf16[128,256]{1,0:T(8,128)(2,1)S(1)}, u32[]{:S(2)}, u32[]{:S(2)}) collective-permute-start(bf16[128,256]{1,0:T(8,128)(2,1)S(1)} %get-tuple-element.63.refs_4_), channel_id=1, source_target_pairs={{0,1},{1,0},{2,3},{3,2},{4,5},{5,4},{6,7},{7,6},{8,9},{9,8},{10,11... | collective-permute-start | bytes 196616 | tf_op jit(solution)/shard_map/ppermute | solution.py:482
  62.7 14.0 %collective-permute-start.30 = (bf16[4,128,256]{2,1,0:T(8,128)(2,1)S(1)}, bf16[4,128,256]{2,1,0:T(8,128)(2,1)S(1)}, u32[]{:S(2)}, u32[]{:S(2)}) collective-permute-start(bf16[4,128,256]{2,1,0:T(8,128)(2,1)S(1)} %get-tuple-element.65), channel_id=1, source_target_pairs={{0,4},{4,0},{8,12},{12,8},{16,20},{20,16},{24,28},{28,24},{1,5},{5... | collective-permute-start | bytes 786440 | tf_op jit(solution)/shard_map/ppermute | solution.py:487
  62.9 4.7 %collective-permute-start.14 = (bf16[128,256]{1,0:T(8,128)(2,1)S(1)}, bf16[128,256]{1,0:T(8,128)(2,1)S(1)}, u32[]{:S(2)}, u32[]{:S(2)}) collective-permute-start(bf16[128,256]{1,0:T(8,128)(2,1)S(1)} %get-tuple-element.55), channel_id=1, source_target_pairs={{0,8},{4,12},{8,0},{12,4},{16,24},{20,28},{24,16},{28,20},{1,9},{5... | collective-permute-start | bytes 196616 | tf_op jit(solution)/shard_map/ppermute | solution.py:482
  62.9 6.0 %collective-permute-start.15 = (bf16[128,256]{1,0:T(8,128)(2,1)S(1)}, bf16[128,256]{1,0:T(8,128)(2,1)S(1)}, u32[]{:S(2)}, u32[]{:S(2)}) collective-permute-start(bf16[128,256]{1,0:T(8,128)(2,1)S(1)} %get-tuple-element.56), channel_id=1, source_target_pairs={{0,16},{4,20},{8,24},{12,28},{16,0},{20,4},{24,8},{28,12},{1,17},{... | collective-permute-start | bytes 196616 | tf_op jit(solution)/shard_map/ppermute | solution.py:482
  63.1 5.8 %collective-permute-start.16 = (bf16[128,256]{1,0:T(8,128)(2,1)S(1)}, bf16[128,256]{1,0:T(8,128)(2,1)S(1)}, u32[]{:S(2)}, u32[]{:S(2)}) collective-permute-start(bf16[128,256]{1,0:T(8,128)(2,1)S(1)} %get-tuple-element.57), channel_id=1, source_target_pairs={{0,24},{4,28},{8,16},{12,20},{16,8},{20,12},{24,0},{28,4},{1,25},{... | collective-permute-start | bytes 196616 | tf_op jit(solution)/shard_map/ppermute | solution.py:482
  69.2 5.4 %collective-permute-start.19 = (bf16[256,128]{1,0:T(8,128)(2,1)S(1)}, bf16[256,128]{1,0:T(8,128)(2,1)S(1)}, u32[]{:S(2)}, u32[]{:S(2)}) collective-permute-start(bf16[256,128]{1,0:T(8,128)(2,1)S(1)} %item_update.2.refs_4_.own_ref), channel_id=1, source_target_pairs={{0,24},{4,28},{8,16},{12,20},{16,8},{20,12},{24,0},{28,4},{1,25},{... | collective-permute-start | bytes 196616 | tf_op jit(solution)/shard_map/ppermute | solution.py:482
  71.9 4.3 %collective-permute-start.18 = (bf16[256,128]{1,0:T(8,128)(2,1)S(1)}, bf16[256,128]{1,0:T(8,128)(2,1)S(1)}, u32[]{:S(2)}, u32[]{:S(2)}) collective-permute-start(bf16[256,128]{1,0:T(8,128)(2,1)S(1)} %item_update.2.refs_4_.own_ref), channel_id=1, source_target_pairs={{0,16},{4,20},{8,24},{12,28},{16,0},{20,4},{24,8},{28,12},{1,17},{... | collective-permute-start | bytes 196616 | tf_op jit(solution)/shard_map/ppermute | solution.py:482
  72.4 4.3 %collective-permute-start.17 = (bf16[256,128]{1,0:T(8,128)(2,1)S(1)}, bf16[256,128]{1,0:T(8,128)(2,1)S(1)}, u32[]{:S(2)}, u32[]{:S(2)}) collective-permute-start(bf16[256,128]{1,0:T(8,128)(2,1)S(1)} %item_update.2.refs_4_.own_ref), channel_id=1, source_target_pairs={{0,8},{4,12},{8,0},{12,4},{16,24},{20,28},{24,16},{28,20},{1,9},{5... | collective-permute-start | bytes 196616 | tf_op jit(solution)/shard_map/ppermute | solution.py:482
  72.7 4.9 %collective-permute-start.20 = (bf16[256,128]{1,0:T(8,128)(2,1)S(1)}, bf16[256,128]{1,0:T(8,128)(2,1)S(1)}, u32[]{:S(2)}, u32[]{:S(2)}) collective-permute-start(bf16[256,128]{1,0:T(8,128)(2,1)S(1)} %item_update.2.refs_4_.own_ref), channel_id=1, source_target_pairs={{0,4},{4,0},{8,12},{12,8},{16,20},{20,16},{24,28},{28,24},{1,5},{5... | collective-permute-start | bytes 196616 | tf_op jit(solution)/shard_map/ppermute | solution.py:487
  74.6 3.9 %collective-permute-start.23 = (bf16[256,128]{1,0:T(8,128)(2,1)S(1)}, bf16[256,128]{1,0:T(8,128)(2,1)S(1)}, u32[]{:S(2)}, u32[]{:S(2)}) collective-permute-start(bf16[256,128]{1,0:T(8,128)(2,1)S(1)} %collective-permute-done.19.refs_7_), channel_id=1, source_target_pairs={{0,4},{4,0},{8,12},{12,8},{16,20},{20,16},{24,28},{28,24},{1,5},{5... | collective-permute-start | bytes 196616 | tf_op jit(solution)/shard_map/ppermute | solution.py:487
  76.2 4.1 %collective-permute-start.22 = (bf16[256,128]{1,0:T(8,128)(2,1)S(1)}, bf16[256,128]{1,0:T(8,128)(2,1)S(1)}, u32[]{:S(2)}, u32[]{:S(2)}) collective-permute-start(bf16[256,128]{1,0:T(8,128)(2,1)S(1)} %collective-permute-done.18.refs_6_), channel_id=1, source_target_pairs={{0,4},{4,0},{8,12},{12,8},{16,20},{20,16},{24,28},{28,24},{1,5},{5... | collective-permute-start | bytes 196616 | tf_op jit(solution)/shard_map/ppermute | solution.py:487
  76.7 3.6 %collective-permute-start.21 = (bf16[256,128]{1,0:T(8,128)(2,1)S(1)}, bf16[256,128]{1,0:T(8,128)(2,1)S(1)}, u32[]{:S(2)}, u32[]{:S(2)}) collective-permute-start(bf16[256,128]{1,0:T(8,128)(2,1)S(1)} %collective-permute-done.17.refs_5_), channel_id=1, source_target_pairs={{0,4},{4,0},{8,12},{12,8},{16,20},{20,16},{24,28},{28,24},{1,5},{5... | collective-permute-start | bytes 196616 | tf_op jit(solution)/shard_map/ppermute | solution.py:487
  76.7 7.0 %collective-permute-start.31 = (bf16[128,256]{1,0:T(8,128)(2,1)S(1)}, bf16[128,256]{1,0:T(8,128)(2,1)S(1)}, u32[]{:S(2)}, u32[]{:S(2)}) collective-permute-start(bf16[128,256]{1,0:T(8,128)(2,1)S(1)} %get-tuple-element.67), channel_id=1, source_target_pairs={{0,8},{4,12},{8,0},{12,4},{16,24},{20,28},{24,16},{28,20},{1,9},{5... | collective-permute-start | bytes 196616 | tf_op jit(solution)/shard_map/ppermute | solution.py:482
  77.6 8.5 %collective-permute-start.32 = (bf16[128,256]{1,0:T(8,128)(2,1)S(1)}, bf16[128,256]{1,0:T(8,128)(2,1)S(1)}, u32[]{:S(2)}, u32[]{:S(2)}) collective-permute-start(bf16[128,256]{1,0:T(8,128)(2,1)S(1)} %get-tuple-element.68), channel_id=1, source_target_pairs={{0,16},{4,20},{8,24},{12,28},{16,0},{20,4},{24,8},{28,12},{1,17},{... | collective-permute-start | bytes 196616 | tf_op jit(solution)/shard_map/ppermute | solution.py:482
  78.5 7.5 %collective-permute-start.33 = (bf16[128,256]{1,0:T(8,128)(2,1)S(1)}, bf16[128,256]{1,0:T(8,128)(2,1)S(1)}, u32[]{:S(2)}, u32[]{:S(2)}) collective-permute-start(bf16[128,256]{1,0:T(8,128)(2,1)S(1)} %get-tuple-element.69), channel_id=1, source_target_pairs={{0,24},{4,28},{8,16},{12,20},{16,8},{20,12},{24,0},{28,4},{1,25},{... | collective-permute-start | bytes 196616 | tf_op jit(solution)/shard_map/ppermute | solution.py:482
  81.6 5.3 %collective-permute-start.24 = (bf16[256,128]{1,0:T(8,128)(2,1)S(1)}, bf16[256,128]{1,0:T(8,128)(2,1)S(1)}, u32[]{:S(2)}, u32[]{:S(2)}) collective-permute-start(bf16[256,128]{1,0:T(8,128)(2,1)S(1)} %get-tuple-element.59), channel_id=1, source_target_pairs={{0,1},{1,0},{2,3},{3,2},{4,5},{5,4},{6,7},{7,6},{8,9},{9,8},{10,11... | collective-permute-start | bytes 196616 | tf_op jit(solution)/shard_map/ppermute | solution.py:482
  81.6 7.4 %collective-permute-start.25 = (bf16[256,128]{1,0:T(8,128)(2,1)S(1)}, bf16[256,128]{1,0:T(8,128)(2,1)S(1)}, u32[]{:S(2)}, u32[]{:S(2)}) collective-permute-start(bf16[256,128]{1,0:T(8,128)(2,1)S(1)} %get-tuple-element.60), channel_id=1, source_target_pairs={{0,2},{1,3},{2,0},{3,1},{4,6},{5,7},{6,4},{7,5},{8,10},{9,11},{10,... | collective-permute-start | bytes 196616 | tf_op jit(solution)/shard_map/ppermute | solution.py:482
  83.7 6.1 %collective-permute-start.26 = (bf16[256,128]{1,0:T(8,128)(2,1)S(1)}, bf16[256,128]{1,0:T(8,128)(2,1)S(1)}, u32[]{:S(2)}, u32[]{:S(2)}) collective-permute-start(bf16[256,128]{1,0:T(8,128)(2,1)S(1)} %get-tuple-element.61), channel_id=1, source_target_pairs={{0,3},{1,2},{2,1},{3,0},{4,7},{5,6},{6,5},{7,4},{8,11},{9,10},{10,... | collective-permute-start | bytes 196616 | tf_op jit(solution)/shard_map/ppermute | solution.py:482

commit v3 on v2

--- a/solution.py
+++ b/solution.py
@@ -12,6 +12,7 @@
 LANES = 128
 CODE_ROWS = 8
 GROUP = 8
+KEPT = 1
 F32 = jnp.float32
 BF16 = jnp.bfloat16
 NT = (((1,), (1,)), ((), ()))
@@ -210,15 +211,29 @@
     )(me, raw, dest, slot, wide)
 
 
-def segment_kernel(capacity, upd, cols, recv_ref, proj_narrow_ref, proj_wide_ref, *refs):
-    adj_refs, (user_ref, user_t_ref, item_ref) = refs[:cols], refs[cols : cols + 3]
-    held_refs, sems = refs[cols + 3 : -1], refs[-1]
+def segment_kernel(
+    capacity, upd, moved, me_ref, recv_ref, proj_narrow_ref, proj_wide_ref, *refs
+):
+    adj_refs, outs = refs[:moved], refs[moved : moved + 3]
+    held_refs, sems = refs[moved + 3 : -1], refs[-1]
     copies = [
         pltpu.make_async_copy(adj_ref, held_ref, sems.at[k])
         for k, (adj_ref, held_ref) in enumerate(zip(adj_refs, held_refs, strict=True))
     ]
     for copy in copies:
         copy.start()
+
+    @pl.when(me_ref[0] >= 0)
+    def _():
+        initial_rows(capacity, upd, recv_ref, proj_narrow_ref, proj_wide_ref, *outs)
+
+    for copy in copies:
+        copy.wait()
+
+
+def initial_rows(
+    capacity, upd, recv_ref, proj_narrow_ref, proj_wide_ref, user_ref, user_t_ref, item_ref
+):
     devices = recv_ref.shape[0]
     narrow, features = proj_narrow_ref.shape[0], proj_wide_ref.shape[0]
     nodes = user_ref.shape[0] + item_ref.shape[0]
@@ -247,11 +262,9 @@
     user_ref[...] = users.astype(BF16)
     user_t_ref[...] = users.T.astype(BF16)
     item_ref[...] = items
-    for copy in copies:
-        copy.wait()
-
-
-def segment(recv, proj_narrow, proj_wide, adjacency, upd, ipd, capacity):
+
+
+def segment(me, recv, proj_narrow, proj_wide, adjacency, upd, ipd, capacity):
     cols = len(adjacency)
     d = proj_wide.shape[1]
     return pl.pallas_call(
@@ -262,12 +275,15 @@
             jax.ShapeDtypeStruct((ipd, d), BF16),
             *[jax.ShapeDtypeStruct(block.shape, BF16) for block in adjacency],
         ),
-        in_specs=[vmem_spec()] * 3 + [pl.BlockSpec(memory_space=pltpu.HBM)] * cols,
+        in_specs=[pl.BlockSpec(memory_space=pltpu.SMEM)]
+        + [vmem_spec()] * 3
+        + [pl.BlockSpec(memory_space=pltpu.HBM)] * cols,
         out_specs=(vmem_spec(),) * (3 + cols),
         scratch_shapes=[pltpu.SemaphoreType.DMA((cols,))],
         compiler_params=params(),
         name="segment",
     )(
+        me,
         recv,
         proj_narrow,
         proj_wide,
@@ -529,9 +545,10 @@
     adjacency = dequantize(
         me, adj_values, tile_mask, tile_scale, (sides, chips, cols)
     )
-    users, users_t, items, *adjacency = segment(
-        recv, proj_narrow, proj_wide, adjacency, upd, ipd, capacity
-    )
+    users, users_t, items, *moved = segment(
+        me, recv, proj_narrow, proj_wide, adjacency[KEPT:], upd, ipd, capacity
+    )
+    adjacency = [*adjacency[:KEPT], *moved]
     for n in range(layers):
         all_users_t = exchange([users_t] * cols, "col", cols)
         own_swapped = [swap(items, "row", rows)]

time: 91 us -> 89.6 us (0.985)
  Pallas kernels: 18.1 us -> 16.6 us
  waiting for transfers between devices: 26.7 us -> 27.7 us
  local copies, waits for them, and re-layouts: 2.35 us -> 1.39 us
    pallas_call x1, Pallas kernels: 3.3 us -> 1.88 us  [segment(): pl.pallas_call(functools.partial(segment_kernel, capacity, upd, cols), ou...]
    all_to_all x1, waiting for transfers between devices: 5.57 us -> 6.56 us  [per_device(): lax.all_to_all(send, ('row', 'col'), split_axis=0, concat_axis=0, tiled=T...]
    unnamed x14 -> x12, local copies, waits for them, and re-layouts: 2.35 us -> 1.39 us
where the time goes in v3:
time: 89.6 us; the launch traced here: 89.2 us
  starting transfers between devices  42.8 us (48%)
  waiting for transfers between devices  27.7 us (31%)
  Pallas kernels  16.6 us (19%)
  local copies, waits for them, and re-layouts  1.39 us (2%)
    ppermute x24, starting transfers between devices, exchange(): received.append(lax.ppermute(blocks[k], axis, pairs))  34.3 us
    ppermute x24, waiting for transfers between devices, exchange(): received.append(lax.ppermute(blocks[k], axis, pairs))  21.1 us
    all_to_all x1, starting transfers between devices, per_device(): lax.all_to_all(send, ('row', 'col'), split_axis=0, concat_axis=0, tiled=T...  7.33 us
    all_to_all x1, waiting for transfers between devices, per_device(): lax.all_to_all(send, ('row', 'col'), split_axis=0, concat_axis=0, tiled=T...  6.56 us
    pallas_call x1, Pallas kernels, dequantize(): pl.pallas_call(functools.partial(dequantize_kernel, shape), out_shape=(ja...  5.03 us
    pallas_call x1, Pallas kernels, dispatch(): pl.pallas_call(functools.partial(dispatch_kernel, devices, capacity), out...  3.35 us
    pallas_call x2, Pallas kernels, user_sums(): pl.pallas_call(functools.partial(user_sum_kernel, cols), out_shape=(jax.S...  2.49 us
    pallas_call x1, Pallas kernels, segment(): pl.pallas_call(functools.partial(segment_kernel, capacity, upd, cols), ou...  1.88 us
  transfers between devices with their start and end apart: 35, of which 14 were waited for; matrix products, arithmetic and copies ran while one was open for 0% of the time, Pallas kernels for 12%

profile of v3, /device:TPU:0, one launch (start us, length us, event | category | flops | bytes accessed | tf_op | source)
XLA Modules:
  0.0 89.2 jit_solution(16919111160847115100)
XLA Ops:
  0.6 3.4 %dispatch.1 = bf16[32,56,128]{2,1,0:T(8,128)(2,1)} custom-call(s32[1]{0:T(128)} %bitcast.me_ref, bf16[64,1024]{1,0:T(8,128)(2,1)} %bitcast.6, s32[1,1024]{1,0:T(1,128)} %bitcast.8, s32[1,1024]{1,0:T(1,128)} %bitcast.9, s32[1,1024]{1,0:T(1,128)} %bitcast.10), custom_call_target="tpu_custom_call" | custom-call | tf_op jit(solution)/shard_map/dispatch/pallas_call | solution.py:196
  4.0 7.3 %all-to-all-start = ((bf16[32,56,128]{2,1,0:T(8,128)(2,1)}), bf16[32,56,128]{2,1,0:T(8,128)(2,1)S(1)}, u32[]{:S(2)}, u32[]{:S(2)}) async-start(bf16[32,56,128]{2,1,0:T(8,128)(2,1)} %dispatch.1), calls=%async_computation | async-start | bytes 917504 | tf_op jit(solution)/shard_map/all_to_all | solution.py:544
  11.4 0.7 copy-done.4
  12.1 0.7 copy-done.5
  12.7 5.0 %dequantize.1 = (bf16[256,2048]{1,0:T(8,128)(2,1)S(1)}, bf16[256,2048]{1,0:T(8,128)(2,1)}, bf16[256,2048]{1,0:T(8,128)(2,1)}, bf16[256,2048]{1,0:T(8,128)(2,1)}) custom-call(s32[1]{0:T(128)} %bitcast.me_ref, s32[8,16]{1,0:T(8,128)S(1)} %copy-done.4, f32[8,16]{1,0:T(8,128)S(1)} %copy-done.5, bf16[1024,2048]{1,0:T(8,128)(2,1)} %values_ref.1), custom_call_target="tpu_custom_call" | custom-call | flops 2097152 | bytes 8388608 | tf_op jit(solution)/shard_map/dequantize/pallas_call | solution.py:339
  17.8 6.6 %all-to-all-done.recv_ref = bf16[32,56,128]{2,1,0:T(8,128)(2,1)S(1)} async-done(((bf16[32,56,128]{2,1,0:T(8,128)(2,1)}), bf16[32,56,128]{2,1,0:T(8,128)(2,1)S(1)}, u32[]{:S(2)}, u32[]{:S(2)}) %all-to-all-start) | async-done | bytes 458784 | tf_op jit(solution)/shard_map/all_to_all | solution.py:544
  24.3 1.9 %segment.1 = (bf16[256,128]{1,0:T(8,128)(2,1)S(1)}, bf16[128,256]{1,0:T(8,128)(2,1)S(1)}, bf16[256,128]{1,0:T(8,128)(2,1)S(1)}, bf16[256,2048]{1,0:T(8,128)(2,1)...) custom-call(s32[1]{0:T(128)} %bitcast.me_ref, bf16[32,56,128]{2,1,0:T(8,128)(2,1)S(1)} %all-to-all-done.recv_ref, ...), custom_call_target="tpu_custom_call" | custom-call | tf_op jit(solution)/shard_map/segment/pallas_call | solution.py:270
  26.2 2.9 %collective-permute-start.12 = (bf16[128,256]{1,0:T(8,128)(2,1)S(1)}, bf16[128,256]{1,0:T(8,128)(2,1)S(1)}, u32[]{:S(2)}, u32[]{:S(2)}) collective-permute-start(bf16[128,256]{1,0:T(8,128)(2,1)S(1)} %get-tuple-element.49.refs_4_), channel_id=1, source_target_pairs={{0,3},{1,2},{2,1},{3,0},{4,7},{5,6},{6,5},{7,4},{8,11},{9,10},{10,... | collective-permute-start | bytes 196616 | tf_op jit(solution)/shard_map/ppermute | solution.py:498
  29.1 1.1 %collective-permute-start.11 = (bf16[128,256]{1,0:T(8,128)(2,1)S(1)}, bf16[128,256]{1,0:T(8,128)(2,1)S(1)}, u32[]{:S(2)}, u32[]{:S(2)}) collective-permute-start(bf16[128,256]{1,0:T(8,128)(2,1)S(1)} %get-tuple-element.49.refs_4_), channel_id=1, source_target_pairs={{0,2},{1,3},{2,0},{3,1},{4,6},{5,7},{6,4},{7,5},{8,10},{9,11},{10,... | collective-permute-start | bytes 196616 | tf_op jit(solution)/shard_map/ppermute | solution.py:498
  30.2 0.8 collective-permute-start.2
  31.0 1.1 %collective-permute-start.1 = (bf16[256,128]{1,0:T(8,128)(2,1)S(1)}, bf16[256,128]{1,0:T(8,128)(2,1)S(1)}, u32[]{:S(2)}, u32[]{:S(2)}) collective-permute-start(bf16[256,128]{1,0:T(8,128)(2,1)S(1)} %get-tuple-element.43.refs_4_.own_ref), channel_id=1, source_target_pairs={{0,16},{4,20},{8,24},{12,28},{16,0},{20,4},{24,8},{28,12},{1,17},{... | collective-permute-start | bytes 196616 | tf_op jit(solution)/shard_map/ppermute | solution.py:498
  32.1 1.6 %collective-permute-start = (bf16[256,128]{1,0:T(8,128)(2,1)S(1)}, bf16[256,128]{1,0:T(8,128)(2,1)S(1)}, u32[]{:S(2)}, u32[]{:S(2)}) collective-permute-start(bf16[256,128]{1,0:T(8,128)(2,1)S(1)} %get-tuple-element.43.refs_4_.own_ref), channel_id=1, source_target_pairs={{0,8},{4,12},{8,0},{12,4},{16,24},{20,28},{24,16},{28,20},{1,9},{5... | collective-permute-start | bytes 196616 | tf_op jit(solution)/shard_map/ppermute | solution.py:498
  33.7 2.7 %collective-permute-start.10 = (bf16[128,256]{1,0:T(8,128)(2,1)S(1)}, bf16[128,256]{1,0:T(8,128)(2,1)S(1)}, u32[]{:S(2)}, u32[]{:S(2)}) collective-permute-start(bf16[128,256]{1,0:T(8,128)(2,1)S(1)} %get-tuple-element.49.refs_4_), channel_id=1, source_target_pairs={{0,1},{1,0},{2,3},{3,2},{4,5},{5,4},{6,7},{7,6},{8,9},{9,8},{10,11... | collective-permute-start | bytes 196616 | tf_op jit(solution)/shard_map/ppermute | solution.py:498
  36.6 0.5 collective-permute-start.6
  37.2 0.4 collective-permute-start.4
  37.7 1.0 %collective-permute-done.10.refs_5_ = bf16[128,256]{1,0:T(8,128)(2,1)S(1)} collective-permute-done((bf16[128,256]{1,0:T(8,128)(2,1)S(1)}, bf16[128,256]{1,0:T(8,128)(2,1)S(1)}, u32[]{:S(2)}, u32[]{:S(2)}) %collective-permute-start.10) | collective-permute-done | bytes 65568 | tf_op jit(solution)/shard_map/ppermute | solution.py:498
  38.6 0.7 item_sums.2
  39.5 1.2 %user_sums.2 = (bf16[256,128]{1,0:T(8,128)(2,1)S(1)}, bf16[256,128]{1,0:T(8,128)(2,1)S(1)}, bf16[256,128]{1,0:T(8,128)(2,1)S(1)}, bf16[256,128]{1,0:T(8,128)(2,1)S(1)}) custom-call(bf16[256,2048]{1,0:T(8,128)(2,1)S(1)} %get-tuple-element.39.refs_0_, bf16[256,2048]{1,0:T(8,128)(2,1)S(1)} %get-tuple-element.40.refs_1_, ...), custom_call_target="tpu_custom_call" | custom-call | flops 536870912 | bytes 4194304 | tf_op jit(solution)/shard_map/user_sums/pallas_call | solution.py:369
  40.8 2.1 %collective-permute-start.7 = (bf16[256,128]{1,0:T(8,128)(2,1)S(1)}, bf16[256,128]{1,0:T(8,128)(2,1)S(1)}, u32[]{:S(2)}, u32[]{:S(2)}) collective-permute-start(bf16[256,128]{1,0:T(8,128)(2,1)S(1)} %get-tuple-element.45), channel_id=1, source_target_pairs={{0,1},{1,0},{2,3},{3,2},{4,5},{5,4},{6,7},{7,6},{8,9},{9,8},{10,11... | collective-permute-start | bytes 196616 | tf_op jit(solution)/shard_map/ppermute | solution.py:498
  42.8 2.4 %collective-permute-start.9 = (bf16[256,128]{1,0:T(8,128)(2,1)S(1)}, bf16[256,128]{1,0:T(8,128)(2,1)S(1)}, u32[]{:S(2)}, u32[]{:S(2)}) collective-permute-start(bf16[256,128]{1,0:T(8,128)(2,1)S(1)} %get-tuple-element.47), channel_id=1, source_target_pairs={{0,3},{1,2},{2,1},{3,0},{4,7},{5,6},{6,5},{7,4},{8,11},{9,10},{10,... | collective-permute-start | bytes 196616 | tf_op jit(solution)/shard_map/ppermute | solution.py:498
  45.3 0.3 collective-permute-done.7.refs_1_
  45.6 5.0 %collective-permute-done.8.refs_2_ = bf16[256,128]{1,0:T(8,128)(2,1)S(1)} collective-permute-done((bf16[256,128]{1,0:T(8,128)(2,1)S(1)}, bf16[256,128]{1,0:T(8,128)(2,1)S(1)}, u32[]{:S(2)}, u32[]{:S(2)}) %collective-permute-start.8) | collective-permute-done | bytes 65568 | tf_op jit(solution)/shard_map/ppermute | solution.py:498
  50.6 0.3 user_update.2
  50.9 1.5 %collective-permute-start.29 = (bf16[128,256]{1,0:T(8,128)(2,1)S(1)}, bf16[128,256]{1,0:T(8,128)(2,1)S(1)}, u32[]{:S(2)}, u32[]{:S(2)}) collective-permute-start(bf16[128,256]{1,0:T(8,128)(2,1)S(1)} %get-tuple-element.61.refs_4_), channel_id=1, source_target_pairs={{0,3},{1,2},{2,1},{3,0},{4,7},{5,6},{6,5},{7,4},{8,11},{9,10},{10,... | collective-permute-start | bytes 196616 | tf_op jit(solution)/shard_map/ppermute | solution.py:498
  52.4 1.9 %collective-permute-start.28 = (bf16[128,256]{1,0:T(8,128)(2,1)S(1)}, bf16[128,256]{1,0:T(8,128)(2,1)S(1)}, u32[]{:S(2)}, u32[]{:S(2)}) collective-permute-start(bf16[128,256]{1,0:T(8,128)(2,1)S(1)} %get-tuple-element.61.refs_4_), channel_id=1, source_target_pairs={{0,2},{1,3},{2,0},{3,1},{4,6},{5,7},{6,4},{7,5},{8,10},{9,11},{10,... | collective-permute-start | bytes 196616 | tf_op jit(solution)/shard_map/ppermute | solution.py:498
  54.3 1.0 %collective-permute-start.27 = (bf16[128,256]{1,0:T(8,128)(2,1)S(1)}, bf16[128,256]{1,0:T(8,128)(2,1)S(1)}, u32[]{:S(2)}, u32[]{:S(2)}) collective-permute-start(bf16[128,256]{1,0:T(8,128)(2,1)S(1)} %get-tuple-element.61.refs_4_), channel_id=1, source_target_pairs={{0,1},{1,0},{2,3},{3,2},{4,5},{5,4},{6,7},{7,6},{8,9},{9,8},{10,11... | collective-permute-start | bytes 196616 | tf_op jit(solution)/shard_map/ppermute | solution.py:498
  55.4 2.4 %collective-permute-done.29.refs_7_ = bf16[128,256]{1,0:T(8,128)(2,1)S(1)} collective-permute-done((bf16[128,256]{1,0:T(8,128)(2,1)S(1)}, bf16[128,256]{1,0:T(8,128)(2,1)S(1)}, u32[]{:S(2)}, u32[]{:S(2)}) %collective-permute-start.29) | collective-permute-done | bytes 65568 | tf_op jit(solution)/shard_map/ppermute | solution.py:498
  57.7 2.8 %collective-permute-done.28.refs_6_ = bf16[128,256]{1,0:T(8,128)(2,1)S(1)} collective-permute-done((bf16[128,256]{1,0:T(8,128)(2,1)S(1)}, bf16[128,256]{1,0:T(8,128)(2,1)S(1)}, u32[]{:S(2)}, u32[]{:S(2)}) %collective-permute-start.28) | collective-permute-done | bytes 65568 | tf_op jit(solution)/shard_map/ppermute | solution.py:498
  60.5 0.7 item_sums.3
  61.7 3.3 %collective-permute-start.16 = (bf16[128,256]{1,0:T(8,128)(2,1)S(1)}, bf16[128,256]{1,0:T(8,128)(2,1)S(1)}, u32[]{:S(2)}, u32[]{:S(2)}) collective-permute-start(bf16[128,256]{1,0:T(8,128)(2,1)S(1)} %get-tuple-element.55), channel_id=1, source_target_pairs={{0,24},{4,28},{8,16},{12,20},{16,8},{20,12},{24,0},{28,4},{1,25},{... | collective-permute-start | bytes 196616 | tf_op jit(solution)/shard_map/ppermute | solution.py:498
  65.0 1.1 %collective-permute-done.14.refs_1_ = bf16[128,256]{1,0:T(8,128)(2,1)S(1)} collective-permute-done((bf16[128,256]{1,0:T(8,128)(2,1)S(1)}, bf16[128,256]{1,0:T(8,128)(2,1)S(1)}, u32[]{:S(2)}, u32[]{:S(2)}) %collective-permute-start.14) | collective-permute-done | bytes 65568 | tf_op jit(solution)/shard_map/ppermute | solution.py:498
  66.1 1.3 %collective-permute-done.15.refs_2_ = bf16[128,256]{1,0:T(8,128)(2,1)S(1)} collective-permute-done((bf16[128,256]{1,0:T(8,128)(2,1)S(1)}, bf16[128,256]{1,0:T(8,128)(2,1)S(1)}, u32[]{:S(2)}, u32[]{:S(2)}) %collective-permute-start.15) | collective-permute-done | bytes 65568 | tf_op jit(solution)/shard_map/ppermute | solution.py:498
  67.7 2.8 %collective-permute-start.19 = (bf16[256,128]{1,0:T(8,128)(2,1)S(1)}, bf16[256,128]{1,0:T(8,128)(2,1)S(1)}, u32[]{:S(2)}, u32[]{:S(2)}) collective-permute-start(bf16[256,128]{1,0:T(8,128)(2,1)S(1)} %item_update.2.refs_4_.own_ref), channel_id=1, source_target_pairs={{0,24},{4,28},{8,16},{12,20},{16,8},{20,12},{24,0},{28,4},{1,25},{... | collective-permute-start | bytes 196616 | tf_op jit(solution)/shard_map/ppermute | solution.py:498
  70.5 0.5 collective-permute-start.18
  71.0 0.3 collective-permute-start.17
  71.3 1.9 %collective-permute-done.19.refs_7_ = bf16[256,128]{1,0:T(8,128)(2,1)S(1)} collective-permute-done((bf16[256,128]{1,0:T(8,128)(2,1)S(1)}, bf16[256,128]{1,0:T(8,128)(2,1)S(1)}, u32[]{:S(2)}, u32[]{:S(2)}) %collective-permute-start.19) | collective-permute-done | bytes 65568 | tf_op jit(solution)/shard_map/ppermute | solution.py:498
  73.1 1.6 %collective-permute-done.18.refs_6_ = bf16[256,128]{1,0:T(8,128)(2,1)S(1)} collective-permute-done((bf16[256,128]{1,0:T(8,128)(2,1)S(1)}, bf16[256,128]{1,0:T(8,128)(2,1)S(1)}, u32[]{:S(2)}, u32[]{:S(2)}) %collective-permute-start.18) | collective-permute-done | bytes 65568 | tf_op jit(solution)/shard_map/ppermute | solution.py:498
  74.7 0.5 collective-permute-done.17.refs_5_
  75.3 0.8 collective-permute-start.31
  76.1 0.9 %collective-permute-start.32 = (bf16[128,256]{1,0:T(8,128)(2,1)S(1)}, bf16[128,256]{1,0:T(8,128)(2,1)S(1)}, u32[]{:S(2)}, u32[]{:S(2)}) collective-permute-start(bf16[128,256]{1,0:T(8,128)(2,1)S(1)} %get-tuple-element.66), channel_id=1, source_target_pairs={{0,16},{4,20},{8,24},{12,28},{16,0},{20,4},{24,8},{28,12},{1,17},{... | collective-permute-start | bytes 196616 | tf_op jit(solution)/shard_map/ppermute | solution.py:498
  77.0 1.8 %collective-permute-start.33 = (bf16[128,256]{1,0:T(8,128)(2,1)S(1)}, bf16[128,256]{1,0:T(8,128)(2,1)S(1)}, u32[]{:S(2)}, u32[]{:S(2)}) collective-permute-start(bf16[128,256]{1,0:T(8,128)(2,1)S(1)} %get-tuple-element.67), channel_id=1, source_target_pairs={{0,24},{4,28},{8,16},{12,20},{16,8},{20,12},{24,0},{28,4},{1,25},{... | collective-permute-start | bytes 196616 | tf_op jit(solution)/shard_map/ppermute | solution.py:498
  78.9 1.2 %user_sums.3 = (bf16[256,128]{1,0:T(8,128)(2,1)S(1)}, bf16[256,128]{1,0:T(8,128)(2,1)S(1)}, bf16[256,128]{1,0:T(8,128)(2,1)S(1)}, bf16[256,128]{1,0:T(8,128)(2,1)S(1)}) custom-call(bf16[256,2048]{1,0:T(8,128)(2,1)S(1)} %get-tuple-element.39.refs_0_, bf16[256,2048]{1,0:T(8,128)(2,1)S(1)} %get-tuple-element.40.refs_1_, ...), custom_call_target="tpu_custom_call" | custom-call | flops 536870912 | bytes 4194304 | tf_op jit(solution)/shard_map/user_sums/pallas_call | solution.py:369
  80.2 2.1 %collective-permute-start.25 = (bf16[256,128]{1,0:T(8,128)(2,1)S(1)}, bf16[256,128]{1,0:T(8,128)(2,1)S(1)}, u32[]{:S(2)}, u32[]{:S(2)}) collective-permute-start(bf16[256,128]{1,0:T(8,128)(2,1)S(1)} %get-tuple-element.58), channel_id=1, source_target_pairs={{0,2},{1,3},{2,0},{3,1},{4,6},{5,7},{6,4},{7,5},{8,10},{9,11},{10,... | collective-permute-start | bytes 196616 | tf_op jit(solution)/shard_map/ppermute | solution.py:498
  82.3 2.3 %collective-permute-start.26 = (bf16[256,128]{1,0:T(8,128)(2,1)S(1)}, bf16[256,128]{1,0:T(8,128)(2,1)S(1)}, u32[]{:S(2)}, u32[]{:S(2)}) collective-permute-start(bf16[256,128]{1,0:T(8,128)(2,1)S(1)} %get-tuple-element.59), channel_id=1, source_target_pairs={{0,3},{1,2},{2,1},{3,0},{4,7},{5,6},{6,5},{7,4},{8,11},{9,10},{10,... | collective-permute-start | bytes 196616 | tf_op jit(solution)/shard_map/ppermute | solution.py:498
  84.6 0.9 item_update.3
  85.5 2.2 %collective-permute-done.25.refs_2_ = bf16[256,128]{1,0:T(8,128)(2,1)S(1)} collective-permute-done((bf16[256,128]{1,0:T(8,128)(2,1)S(1)}, bf16[256,128]{1,0:T(8,128)(2,1)S(1)}, u32[]{:S(2)}, u32[]{:S(2)}) %collective-permute-start.25) | collective-permute-done | bytes 65568 | tf_op jit(solution)/shard_map/ppermute | solution.py:498
  87.6 0.7 collective-permute-done.26.refs_3_
  88.4 0.9 %user_update.3 = (bf16[256,128]{1,0:T(8,128)(2,1)}, bf16[128,256]{1,0:T(8,128)(2,1)}) custom-call(bf16[256,128]{1,0:T(8,128)(2,1)S(1)} %get-tuple-element.48.own_ref, bf16[2,128,128]{2,1,0:T(8,128)(2,1)S(1)} %copy-done, bf16[2,128,128]{2,1,0:T(8,128)(2,1)S(1)} %copy-done.1, bf16[256,128]{1,0:T(8,128)(2,1)S(1)} %get-tuple-element.56.refs_0_, ...), custom_call_target="tpu_custom_call" | custom-call | tf_op jit(solution)/shard_map/user_update/pallas_call | solution.py:462
  (47 shorter events, 1.2 us)
Async XLA Ops:
  4.0 20.3 %copy-start.2 = (bf16[64,128]{1,0:T(8,128)(2,1)S(1)}, bf16[64,128]{1,0:T(8,128)(2,1)}, u32[]{:S(2)}) copy-start(bf16[64,128]{1,0:T(8,128)(2,1)} %proj_wide_ref.1) | copy-start | bytes 49156
  4.0 20.3 %copy-start.3 = (bf16[32,128]{1,0:T(8,128)(2,1)S(1)}, bf16[32,128]{1,0:T(8,128)(2,1)}, u32[]{:S(2)}) copy-start(bf16[32,128]{1,0:T(8,128)(2,1)} %proj_narrow_ref.1) | copy-start | bytes 24580
  4.0 20.3 %all-to-all-start = ((bf16[32,56,128]{2,1,0:T(8,128)(2,1)}), bf16[32,56,128]{2,1,0:T(8,128)(2,1)S(1)}, u32[]{:S(2)}, u32[]{:S(2)}) async-start(bf16[32,56,128]{2,1,0:T(8,128)(2,1)} %dispatch.1), calls=%async_computation | async-start | bytes 917504 | tf_op jit(solution)/shard_map/all_to_all | solution.py:544
  11.4 0.7 copy-start.4
  12.0 0.7 copy-start.5
  26.2 7.4 %collective-permute-start.12 = (bf16[128,256]{1,0:T(8,128)(2,1)S(1)}, bf16[128,256]{1,0:T(8,128)(2,1)S(1)}, u32[]{:S(2)}, u32[]{:S(2)}) collective-permute-start(bf16[128,256]{1,0:T(8,128)(2,1)S(1)} %get-tuple-element.49.refs_4_), channel_id=1, source_target_pairs={{0,3},{1,2},{2,1},{3,0},{4,7},{5,6},{6,5},{7,4},{8,11},{9,10},{10,... | collective-permute-start | bytes 196616 | tf_op jit(solution)/shard_map/ppermute | solution.py:498
  29.1 7.5 %collective-permute-start.11 = (bf16[128,256]{1,0:T(8,128)(2,1)S(1)}, bf16[128,256]{1,0:T(8,128)(2,1)S(1)}, u32[]{:S(2)}, u32[]{:S(2)}) collective-permute-start(bf16[128,256]{1,0:T(8,128)(2,1)S(1)} %get-tuple-element.49.refs_4_), channel_id=1, source_target_pairs={{0,2},{1,3},{2,0},{3,1},{4,6},{5,7},{6,4},{7,5},{8,10},{9,11},{10,... | collective-permute-start | bytes 196616 | tf_op jit(solution)/shard_map/ppermute | solution.py:498
  30.2 6.5 %collective-permute-start.2 = (bf16[256,128]{1,0:T(8,128)(2,1)S(1)}, bf16[256,128]{1,0:T(8,128)(2,1)S(1)}, u32[]{:S(2)}, u32[]{:S(2)}) collective-permute-start(bf16[256,128]{1,0:T(8,128)(2,1)S(1)} %get-tuple-element.43.refs_4_.own_ref), channel_id=1, source_target_pairs={{0,24},{4,28},{8,16},{12,20},{16,8},{20,12},{24,0},{28,4},{1,25},{... | collective-permute-start | bytes 196616 | tf_op jit(solution)/shard_map/ppermute | solution.py:498
  31.0 6.2 %collective-permute-start.1 = (bf16[256,128]{1,0:T(8,128)(2,1)S(1)}, bf16[256,128]{1,0:T(8,128)(2,1)S(1)}, u32[]{:S(2)}, u32[]{:S(2)}) collective-permute-start(bf16[256,128]{1,0:T(8,128)(2,1)S(1)} %get-tuple-element.43.refs_4_.own_ref), channel_id=1, source_target_pairs={{0,16},{4,20},{8,24},{12,28},{16,0},{20,4},{24,8},{28,12},{1,17},{... | collective-permute-start | bytes 196616 | tf_op jit(solution)/shard_map/ppermute | solution.py:498
  32.1 5.1 %collective-permute-start = (bf16[256,128]{1,0:T(8,128)(2,1)S(1)}, bf16[256,128]{1,0:T(8,128)(2,1)S(1)}, u32[]{:S(2)}, u32[]{:S(2)}) collective-permute-start(bf16[256,128]{1,0:T(8,128)(2,1)S(1)} %get-tuple-element.43.refs_4_.own_ref), channel_id=1, source_target_pairs={{0,8},{4,12},{8,0},{12,4},{16,24},{20,28},{24,16},{28,20},{1,9},{5... | collective-permute-start | bytes 196616 | tf_op jit(solution)/shard_map/ppermute | solution.py:498
  33.7 5.0 %collective-permute-start.10 = (bf16[128,256]{1,0:T(8,128)(2,1)S(1)}, bf16[128,256]{1,0:T(8,128)(2,1)S(1)}, u32[]{:S(2)}, u32[]{:S(2)}) collective-permute-start(bf16[128,256]{1,0:T(8,128)(2,1)S(1)} %get-tuple-element.49.refs_4_), channel_id=1, source_target_pairs={{0,1},{1,0},{2,3},{3,2},{4,5},{5,4},{6,7},{7,6},{8,9},{9,8},{10,11... | collective-permute-start | bytes 196616 | tf_op jit(solution)/shard_map/ppermute | solution.py:498
  36.6 2.8 %collective-permute-start.3 = (bf16[256,128]{1,0:T(8,128)(2,1)S(1)}, bf16[256,128]{1,0:T(8,128)(2,1)S(1)}, u32[]{:S(2)}, u32[]{:S(2)}) collective-permute-start(bf16[256,128]{1,0:T(8,128)(2,1)S(1)} %get-tuple-element.43.refs_4_.own_ref), channel_id=1, source_target_pairs={{0,4},{4,0},{8,12},{12,8},{16,20},{20,16},{24,28},{28,24},{1,5},{5... | collective-permute-start | bytes 196616 | tf_op jit(solution)/shard_map/ppermute | solution.py:503
  36.6 2.8 %collective-permute-start.6 = (bf16[256,128]{1,0:T(8,128)(2,1)S(1)}, bf16[256,128]{1,0:T(8,128)(2,1)S(1)}, u32[]{:S(2)}, u32[]{:S(2)}) collective-permute-start(bf16[256,128]{1,0:T(8,128)(2,1)S(1)} %collective-permute-done.2.refs_7_), channel_id=1, source_target_pairs={{0,4},{4,0},{8,12},{12,8},{16,20},{20,16},{24,28},{28,24},{1,5},{5... | collective-permute-start | bytes 196616 | tf_op jit(solution)/shard_map/ppermute | solution.py:503
  37.2 2.3 %collective-permute-start.5 = (bf16[256,128]{1,0:T(8,128)(2,1)S(1)}, bf16[256,128]{1,0:T(8,128)(2,1)S(1)}, u32[]{:S(2)}, u32[]{:S(2)}) collective-permute-start(bf16[256,128]{1,0:T(8,128)(2,1)S(1)} %collective-permute-done.1.refs_6_), channel_id=1, source_target_pairs={{0,4},{4,0},{8,12},{12,8},{16,20},{20,16},{24,28},{28,24},{1,5},{5... | collective-permute-start | bytes 196616 | tf_op jit(solution)/shard_map/ppermute | solution.py:503
  37.2 2.3 %collective-permute-start.4 = (bf16[256,128]{1,0:T(8,128)(2,1)S(1)}, bf16[256,128]{1,0:T(8,128)(2,1)S(1)}, u32[]{:S(2)}, u32[]{:S(2)}) collective-permute-start(bf16[256,128]{1,0:T(8,128)(2,1)S(1)} %collective-permute-done.refs_5_), channel_id=1, source_target_pairs={{0,4},{4,0},{8,12},{12,8},{16,20},{20,16},{24,28},{28,24},{1,5},{5... | collective-permute-start | bytes 196616 | tf_op jit(solution)/shard_map/ppermute | solution.py:503
  38.6 12.0 %copy-start = (bf16[2,128,128]{2,1,0:T(8,128)(2,1)S(1)}, bf16[2,128,128]{2,1,0:T(8,128)(2,1)}, u32[]{:S(2)}) copy-start(bf16[2,128,128]{2,1,0:T(8,128)(2,1)} %sum_ref.7) | copy-start | bytes 196612
  38.6 12.0 %copy-start.1 = (bf16[2,128,128]{2,1,0:T(8,128)(2,1)S(1)}, bf16[2,128,128]{2,1,0:T(8,128)(2,1)}, u32[]{:S(2)}) copy-start(bf16[2,128,128]{2,1,0:T(8,128)(2,1)} %product_ref.7) | copy-start | bytes 196612
  39.4 22.0 %collective-permute-start.13 = (bf16[4,128,256]{2,1,0:T(8,128)(2,1)S(1)}, bf16[4,128,256]{2,1,0:T(8,128)(2,1)S(1)}, u32[]{:S(2)}, u32[]{:S(2)}) collective-permute-start(bf16[4,128,256]{2,1,0:T(8,128)(2,1)S(1)} %get-tuple-element.51), channel_id=1, source_target_pairs={{0,4},{4,0},{8,12},{12,8},{16,20},{20,16},{24,28},{28,24},{1,5},{5... | collective-permute-start | bytes 786440 | tf_op jit(solution)/shard_map/ppermute | solution.py:503
  40.8 4.8 %collective-permute-start.7 = (bf16[256,128]{1,0:T(8,128)(2,1)S(1)}, bf16[256,128]{1,0:T(8,128)(2,1)S(1)}, u32[]{:S(2)}, u32[]{:S(2)}) collective-permute-start(bf16[256,128]{1,0:T(8,128)(2,1)S(1)} %get-tuple-element.45), channel_id=1, source_target_pairs={{0,1},{1,0},{2,3},{3,2},{4,5},{5,4},{6,7},{7,6},{8,9},{9,8},{10,11... | collective-permute-start | bytes 196616 | tf_op jit(solution)/shard_map/ppermute | solution.py:498
  42.8 7.8 %collective-permute-start.8 = (bf16[256,128]{1,0:T(8,128)(2,1)S(1)}, bf16[256,128]{1,0:T(8,128)(2,1)S(1)}, u32[]{:S(2)}, u32[]{:S(2)}) collective-permute-start(bf16[256,128]{1,0:T(8,128)(2,1)S(1)} %get-tuple-element.46), channel_id=1, source_target_pairs={{0,2},{1,3},{2,0},{3,1},{4,6},{5,7},{6,4},{7,5},{8,10},{9,11},{10,... | collective-permute-start | bytes 196616 | tf_op jit(solution)/shard_map/ppermute | solution.py:498
  42.8 7.8 %collective-permute-start.9 = (bf16[256,128]{1,0:T(8,128)(2,1)S(1)}, bf16[256,128]{1,0:T(8,128)(2,1)S(1)}, u32[]{:S(2)}, u32[]{:S(2)}) collective-permute-start(bf16[256,128]{1,0:T(8,128)(2,1)S(1)} %get-tuple-element.47), channel_id=1, source_target_pairs={{0,3},{1,2},{2,1},{3,0},{4,7},{5,6},{6,5},{7,4},{8,11},{9,10},{10,... | collective-permute-start | bytes 196616 | tf_op jit(solution)/shard_map/ppermute | solution.py:498
  50.9 6.8 %collective-permute-start.29 = (bf16[128,256]{1,0:T(8,128)(2,1)S(1)}, bf16[128,256]{1,0:T(8,128)(2,1)S(1)}, u32[]{:S(2)}, u32[]{:S(2)}) collective-permute-start(bf16[128,256]{1,0:T(8,128)(2,1)S(1)} %get-tuple-element.61.refs_4_), channel_id=1, source_target_pairs={{0,3},{1,2},{2,1},{3,0},{4,7},{5,6},{6,5},{7,4},{8,11},{9,10},{10,... | collective-permute-start | bytes 196616 | tf_op jit(solution)/shard_map/ppermute | solution.py:498
  52.4 8.2 %collective-permute-start.28 = (bf16[128,256]{1,0:T(8,128)(2,1)S(1)}, bf16[128,256]{1,0:T(8,128)(2,1)S(1)}, u32[]{:S(2)}, u32[]{:S(2)}) collective-permute-start(bf16[128,256]{1,0:T(8,128)(2,1)S(1)} %get-tuple-element.61.refs_4_), channel_id=1, source_target_pairs={{0,2},{1,3},{2,0},{3,1},{4,6},{5,7},{6,4},{7,5},{8,10},{9,11},{10,... | collective-permute-start | bytes 196616 | tf_op jit(solution)/shard_map/ppermute | solution.py:498
  54.3 6.2 %collective-permute-start.27 = (bf16[128,256]{1,0:T(8,128)(2,1)S(1)}, bf16[128,256]{1,0:T(8,128)(2,1)S(1)}, u32[]{:S(2)}, u32[]{:S(2)}) collective-permute-start(bf16[128,256]{1,0:T(8,128)(2,1)S(1)} %get-tuple-element.61.refs_4_), channel_id=1, source_target_pairs={{0,1},{1,0},{2,3},{3,2},{4,5},{5,4},{6,7},{7,6},{8,9},{9,8},{10,11... | collective-permute-start | bytes 196616 | tf_op jit(solution)/shard_map/ppermute | solution.py:498
  61.3 14.0 %collective-permute-start.30 = (bf16[4,128,256]{2,1,0:T(8,128)(2,1)S(1)}, bf16[4,128,256]{2,1,0:T(8,128)(2,1)S(1)}, u32[]{:S(2)}, u32[]{:S(2)}) collective-permute-start(bf16[4,128,256]{2,1,0:T(8,128)(2,1)S(1)} %get-tuple-element.63), channel_id=1, source_target_pairs={{0,4},{4,0},{8,12},{12,8},{16,20},{20,16},{24,28},{28,24},{1,5},{5... | collective-permute-start | bytes 786440 | tf_op jit(solution)/shard_map/ppermute | solution.py:503
  61.4 4.7 %collective-permute-start.14 = (bf16[128,256]{1,0:T(8,128)(2,1)S(1)}, bf16[128,256]{1,0:T(8,128)(2,1)S(1)}, u32[]{:S(2)}, u32[]{:S(2)}) collective-permute-start(bf16[128,256]{1,0:T(8,128)(2,1)S(1)} %get-tuple-element.53), channel_id=1, source_target_pairs={{0,8},{4,12},{8,0},{12,4},{16,24},{20,28},{24,16},{28,20},{1,9},{5... | collective-permute-start | bytes 196616 | tf_op jit(solution)/shard_map/ppermute | solution.py:498
  61.5 6.0 %collective-permute-start.15 = (bf16[128,256]{1,0:T(8,128)(2,1)S(1)}, bf16[128,256]{1,0:T(8,128)(2,1)S(1)}, u32[]{:S(2)}, u32[]{:S(2)}) collective-permute-start(bf16[128,256]{1,0:T(8,128)(2,1)S(1)} %get-tuple-element.54), channel_id=1, source_target_pairs={{0,16},{4,20},{8,24},{12,28},{16,0},{20,4},{24,8},{28,12},{1,17},{... | collective-permute-start | bytes 196616 | tf_op jit(solution)/shard_map/ppermute | solution.py:498
  61.7 5.8 %collective-permute-start.16 = (bf16[128,256]{1,0:T(8,128)(2,1)S(1)}, bf16[128,256]{1,0:T(8,128)(2,1)S(1)}, u32[]{:S(2)}, u32[]{:S(2)}) collective-permute-start(bf16[128,256]{1,0:T(8,128)(2,1)S(1)} %get-tuple-element.55), channel_id=1, source_target_pairs={{0,24},{4,28},{8,16},{12,20},{16,8},{20,12},{24,0},{28,4},{1,25},{... | collective-permute-start | bytes 196616 | tf_op jit(solution)/shard_map/ppermute | solution.py:498
  67.7 5.4 %collective-permute-start.19 = (bf16[256,128]{1,0:T(8,128)(2,1)S(1)}, bf16[256,128]{1,0:T(8,128)(2,1)S(1)}, u32[]{:S(2)}, u32[]{:S(2)}) collective-permute-start(bf16[256,128]{1,0:T(8,128)(2,1)S(1)} %item_update.2.refs_4_.own_ref), channel_id=1, source_target_pairs={{0,24},{4,28},{8,16},{12,20},{16,8},{20,12},{24,0},{28,4},{1,25},{... | collective-permute-start | bytes 196616 | tf_op jit(solution)/shard_map/ppermute | solution.py:498
  70.5 4.3 %collective-permute-start.18 = (bf16[256,128]{1,0:T(8,128)(2,1)S(1)}, bf16[256,128]{1,0:T(8,128)(2,1)S(1)}, u32[]{:S(2)}, u32[]{:S(2)}) collective-permute-start(bf16[256,128]{1,0:T(8,128)(2,1)S(1)} %item_update.2.refs_4_.own_ref), channel_id=1, source_target_pairs={{0,16},{4,20},{8,24},{12,28},{16,0},{20,4},{24,8},{28,12},{1,17},{... | collective-permute-start | bytes 196616 | tf_op jit(solution)/shard_map/ppermute | solution.py:498
  71.0 4.3 %collective-permute-start.17 = (bf16[256,128]{1,0:T(8,128)(2,1)S(1)}, bf16[256,128]{1,0:T(8,128)(2,1)S(1)}, u32[]{:S(2)}, u32[]{:S(2)}) collective-permute-start(bf16[256,128]{1,0:T(8,128)(2,1)S(1)} %item_update.2.refs_4_.own_ref), channel_id=1, source_target_pairs={{0,8},{4,12},{8,0},{12,4},{16,24},{20,28},{24,16},{28,20},{1,9},{5... | collective-permute-start | bytes 196616 | tf_op jit(solution)/shard_map/ppermute | solution.py:498
  71.3 4.9 %collective-permute-start.20 = (bf16[256,128]{1,0:T(8,128)(2,1)S(1)}, bf16[256,128]{1,0:T(8,128)(2,1)S(1)}, u32[]{:S(2)}, u32[]{:S(2)}) collective-permute-start(bf16[256,128]{1,0:T(8,128)(2,1)S(1)} %item_update.2.refs_4_.own_ref), channel_id=1, source_target_pairs={{0,4},{4,0},{8,12},{12,8},{16,20},{20,16},{24,28},{28,24},{1,5},{5... | collective-permute-start | bytes 196616 | tf_op jit(solution)/shard_map/ppermute | solution.py:503
  73.1 3.9 %collective-permute-start.23 = (bf16[256,128]{1,0:T(8,128)(2,1)S(1)}, bf16[256,128]{1,0:T(8,128)(2,1)S(1)}, u32[]{:S(2)}, u32[]{:S(2)}) collective-permute-start(bf16[256,128]{1,0:T(8,128)(2,1)S(1)} %collective-permute-done.19.refs_7_), channel_id=1, source_target_pairs={{0,4},{4,0},{8,12},{12,8},{16,20},{20,16},{24,28},{28,24},{1,5},{5... | collective-permute-start | bytes 196616 | tf_op jit(solution)/shard_map/ppermute | solution.py:503
  74.7 4.1 %collective-permute-start.22 = (bf16[256,128]{1,0:T(8,128)(2,1)S(1)}, bf16[256,128]{1,0:T(8,128)(2,1)S(1)}, u32[]{:S(2)}, u32[]{:S(2)}) collective-permute-start(bf16[256,128]{1,0:T(8,128)(2,1)S(1)} %collective-permute-done.18.refs_6_), channel_id=1, source_target_pairs={{0,4},{4,0},{8,12},{12,8},{16,20},{20,16},{24,28},{28,24},{1,5},{5... | collective-permute-start | bytes 196616 | tf_op jit(solution)/shard_map/ppermute | solution.py:503
  75.2 3.6 %collective-permute-start.21 = (bf16[256,128]{1,0:T(8,128)(2,1)S(1)}, bf16[256,128]{1,0:T(8,128)(2,1)S(1)}, u32[]{:S(2)}, u32[]{:S(2)}) collective-permute-start(bf16[256,128]{1,0:T(8,128)(2,1)S(1)} %collective-permute-done.17.refs_5_), channel_id=1, source_target_pairs={{0,4},{4,0},{8,12},{12,8},{16,20},{20,16},{24,28},{28,24},{1,5},{5... | collective-permute-start | bytes 196616 | tf_op jit(solution)/shard_map/ppermute | solution.py:503
  75.3 7.0 %collective-permute-start.31 = (bf16[128,256]{1,0:T(8,128)(2,1)S(1)}, bf16[128,256]{1,0:T(8,128)(2,1)S(1)}, u32[]{:S(2)}, u32[]{:S(2)}) collective-permute-start(bf16[128,256]{1,0:T(8,128)(2,1)S(1)} %get-tuple-element.65), channel_id=1, source_target_pairs={{0,8},{4,12},{8,0},{12,4},{16,24},{20,28},{24,16},{28,20},{1,9},{5... | collective-permute-start | bytes 196616 | tf_op jit(solution)/shard_map/ppermute | solution.py:498
  76.1 8.5 %collective-permute-start.32 = (bf16[128,256]{1,0:T(8,128)(2,1)S(1)}, bf16[128,256]{1,0:T(8,128)(2,1)S(1)}, u32[]{:S(2)}, u32[]{:S(2)}) collective-permute-start(bf16[128,256]{1,0:T(8,128)(2,1)S(1)} %get-tuple-element.66), channel_id=1, source_target_pairs={{0,16},{4,20},{8,24},{12,28},{16,0},{20,4},{24,8},{28,12},{1,17},{... | collective-permute-start | bytes 196616 | tf_op jit(solution)/shard_map/ppermute | solution.py:498
  77.0 7.5 %collective-permute-start.33 = (bf16[128,256]{1,0:T(8,128)(2,1)S(1)}, bf16[128,256]{1,0:T(8,128)(2,1)S(1)}, u32[]{:S(2)}, u32[]{:S(2)}) collective-permute-start(bf16[128,256]{1,0:T(8,128)(2,1)S(1)} %get-tuple-element.67), channel_id=1, source_target_pairs={{0,24},{4,28},{8,16},{12,20},{16,8},{20,12},{24,0},{28,4},{1,25},{... | collective-permute-start | bytes 196616 | tf_op jit(solution)/shard_map/ppermute | solution.py:498
  80.1 5.3 %collective-permute-start.24 = (bf16[256,128]{1,0:T(8,128)(2,1)S(1)}, bf16[256,128]{1,0:T(8,128)(2,1)S(1)}, u32[]{:S(2)}, u32[]{:S(2)}) collective-permute-start(bf16[256,128]{1,0:T(8,128)(2,1)S(1)} %get-tuple-element.57), channel_id=1, source_target_pairs={{0,1},{1,0},{2,3},{3,2},{4,5},{5,4},{6,7},{7,6},{8,9},{9,8},{10,11... | collective-permute-start | bytes 196616 | tf_op jit(solution)/shard_map/ppermute | solution.py:498
  80.2 7.4 %collective-permute-start.25 = (bf16[256,128]{1,0:T(8,128)(2,1)S(1)}, bf16[256,128]{1,0:T(8,128)(2,1)S(1)}, u32[]{:S(2)}, u32[]{:S(2)}) collective-permute-start(bf16[256,128]{1,0:T(8,128)(2,1)S(1)} %get-tuple-element.58), channel_id=1, source_target_pairs={{0,2},{1,3},{2,0},{3,1},{4,6},{5,7},{6,4},{7,5},{8,10},{9,11},{10,... | collective-permute-start | bytes 196616 | tf_op jit(solution)/shard_map/ppermute | solution.py:498
  82.3 6.1 %collective-permute-start.26 = (bf16[256,128]{1,0:T(8,128)(2,1)S(1)}, bf16[256,128]{1,0:T(8,128)(2,1)S(1)}, u32[]{:S(2)}, u32[]{:S(2)}) collective-permute-start(bf16[256,128]{1,0:T(8,128)(2,1)S(1)} %get-tuple-element.59), channel_id=1, source_target_pairs={{0,3},{1,2},{2,1},{3,0},{4,7},{5,6},{6,5},{7,4},{8,11},{9,10},{10,... | collective-permute-start | bytes 196616 | tf_op jit(solution)/shard_map/ppermute | solution.py:498

commit v4 on v3

--- a/solution.py
+++ b/solution.py
@@ -357,15 +357,31 @@
 
 def user_sum_kernel(cols, *refs):
     adj_refs, items_refs, out_refs = refs[:cols], refs[cols:-cols], refs[-cols:]
-    items = jnp.concatenate([ref[...] for ref in items_refs], axis=0)
+    items = jnp.concatenate([ref[...].reshape(-1, ref.shape[-1]) for ref in items_refs], axis=0)
     for adj_ref, out_ref in zip(adj_refs, out_refs, strict=True):
         out_ref[...] = jnp.dot(adj_ref[...], items, preferred_element_type=F32).astype(BF16)
+
+
+def merge_kernel(*refs):
+    for k, ref in enumerate(refs[:-1]):
+        refs[-1][k] = ref[...]
+
+
+def merge(blocks):
+    return pl.pallas_call(
+        merge_kernel,
+        out_shape=jax.ShapeDtypeStruct((len(blocks), *blocks[0].shape), blocks[0].dtype),
+        in_specs=[vmem_spec()] * len(blocks),
+        out_specs=vmem_spec(),
+        compiler_params=params(),
+        name="merge",
+    )(*blocks)
 
 
 def user_sums(adjacency, items):
     cols = len(adjacency)
     upd, n = adjacency[0].shape
-    d = items[0].shape[1]
+    d = items[0].shape[-1]
     return pl.pallas_call(
         functools.partial(user_sum_kernel, cols),
         out_shape=(jax.ShapeDtypeStruct((upd, d), BF16),) * cols,
@@ -551,11 +567,10 @@
     adjacency = [*adjacency[:KEPT], *moved]
     for n in range(layers):
         all_users_t = exchange([users_t] * cols, "col", cols)
-        own_swapped = [swap(items, "row", rows)]
         all_items = ordered(exchange([items] * chips, "row", chips, sides))
-        swapped = [swap(block, "row", rows) for block in all_items[1:]]
         if sides > 1:
-            all_items = [*all_items, *own_swapped, *swapped]
+            merged = merge(all_items)
+            all_items = [*all_items, swap(merged, "row", rows)]
         *away, kept = item_sums(adjacency, all_users_t, sides, chips)
         came = [swap(part, "row", rows) for part in away]
         user_parts = user_sums(adjacency, all_items)

time: 89.6 us -> 77.6 us (0.87)
  waiting for transfers between devices: 27.7 us -> 18.4 us
  starting transfers between devices: 42.8 us -> 40 us
    ppermute x24, waiting for transfers between devices: 21.1 us -> 11.9 us  [exchange(): received.append(lax.ppermute(blocks[k], axis, pairs))]
    ppermute x24, starting transfers between devices: 34.3 us -> 32.4 us  [exchange(): received.append(lax.ppermute(blocks[k], axis, pairs))]
  transfers between devices with their start and end apart: 35 -> 29, of which waited for: 14 -> 9; matrix products, arithmetic and copies ran while one was open for 0% -> 0% of each run, Pallas kernels for 12% -> 14%
where the time goes in v4:
time: 77.6 us; the launch traced here: 77.2 us
  starting transfers between devices  40 us (52%)
  waiting for transfers between devices  18.4 us (24%)
  Pallas kernels  16.6 us (21%)
  local copies, waits for them, and re-layouts  1.39 us (2%)
  between operations  0.84 us (1%)
    ppermute x24, starting transfers between devices, exchange(): received.append(lax.ppermute(blocks[k], axis, pairs))  32.4 us
    ppermute x24, waiting for transfers between devices, exchange(): received.append(lax.ppermute(blocks[k], axis, pairs))  11.9 us
    all_to_all x1, starting transfers between devices, per_device(): lax.all_to_all(send, ('row', 'col'), split_axis=0, concat_axis=0, tiled=T...  7.33 us
    all_to_all x1, waiting for transfers between devices, per_device(): lax.all_to_all(send, ('row', 'col'), split_axis=0, concat_axis=0, tiled=T...  6.58 us
    pallas_call x1, Pallas kernels, dequantize(): pl.pallas_call(functools.partial(dequantize_kernel, shape), out_shape=(ja...  5.01 us
    pallas_call x1, Pallas kernels, dispatch(): pl.pallas_call(functools.partial(dispatch_kernel, devices, capacity), out...  3.35 us
    pallas_call x2, Pallas kernels, user_sums(): pl.pallas_call(functools.partial(user_sum_kernel, cols), out_shape=(jax.S...  2.49 us
    pallas_call x1, Pallas kernels, segment(): pl.pallas_call(functools.partial(segment_kernel, capacity, upd, cols), ou...  1.88 us
  transfers between devices with their start and end apart: 29, of which 9 were waited for; matrix products, arithmetic and copies ran while one was open for 0% of the time, Pallas kernels for 14%

profile of v4, /device:TPU:0, one launch (start us, length us, event | category | flops | bytes accessed | tf_op | source)
XLA Modules:
  0.0 77.2 jit_solution(10316136954947855339)
XLA Ops:
  0.6 3.4 %dispatch.1 = bf16[32,56,128]{2,1,0:T(8,128)(2,1)} custom-call(s32[1]{0:T(128)} %bitcast.me_ref, bf16[64,1024]{1,0:T(8,128)(2,1)} %bitcast.6, s32[1,1024]{1,0:T(1,128)} %bitcast.8, s32[1,1024]{1,0:T(1,128)} %bitcast.9, s32[1,1024]{1,0:T(1,128)} %bitcast.10), custom_call_target="tpu_custom_call" | custom-call | tf_op jit(solution)/shard_map/dispatch/pallas_call | solution.py:196
  4.0 7.3 %all-to-all-start = ((bf16[32,56,128]{2,1,0:T(8,128)(2,1)}), bf16[32,56,128]{2,1,0:T(8,128)(2,1)S(1)}, u32[]{:S(2)}, u32[]{:S(2)}) async-start(bf16[32,56,128]{2,1,0:T(8,128)(2,1)} %dispatch.1), calls=%async_computation | async-start | bytes 917504 | tf_op jit(solution)/shard_map/all_to_all | solution.py:560
  11.4 0.7 copy-done.4
  12.0 0.7 copy-done.5
  12.7 5.0 %dequantize.1 = (bf16[256,2048]{1,0:T(8,128)(2,1)S(1)}, bf16[256,2048]{1,0:T(8,128)(2,1)}, bf16[256,2048]{1,0:T(8,128)(2,1)}, bf16[256,2048]{1,0:T(8,128)(2,1)}) custom-call(s32[1]{0:T(128)} %bitcast.me_ref, s32[8,16]{1,0:T(8,128)S(1)} %copy-done.4, f32[8,16]{1,0:T(8,128)S(1)} %copy-done.5, bf16[1024,2048]{1,0:T(8,128)(2,1)} %values_ref.1), custom_call_target="tpu_custom_call" | custom-call | flops 2097152 | bytes 8388608 | tf_op jit(solution)/shard_map/dequantize/pallas_call | solution.py:339
  17.7 6.6 %all-to-all-done.recv_ref = bf16[32,56,128]{2,1,0:T(8,128)(2,1)S(1)} async-done(((bf16[32,56,128]{2,1,0:T(8,128)(2,1)}), bf16[32,56,128]{2,1,0:T(8,128)(2,1)S(1)}, u32[]{:S(2)}, u32[]{:S(2)}) %all-to-all-start) | async-done | bytes 458784 | tf_op jit(solution)/shard_map/all_to_all | solution.py:560
  24.3 1.9 %segment.1 = (bf16[256,128]{1,0:T(8,128)(2,1)S(1)}, bf16[128,256]{1,0:T(8,128)(2,1)S(1)}, bf16[256,128]{1,0:T(8,128)(2,1)S(1)}, bf16[256,2048]{1,0:T(8,128)(2,1)...) custom-call(s32[1]{0:T(128)} %bitcast.me_ref, bf16[32,56,128]{2,1,0:T(8,128)(2,1)S(1)} %all-to-all-done.recv_ref, ...), custom_call_target="tpu_custom_call" | custom-call | tf_op jit(solution)/shard_map/segment/pallas_call | solution.py:270
  26.2 2.2 %collective-permute-start.2 = (bf16[256,128]{1,0:T(8,128)(2,1)S(1)}, bf16[256,128]{1,0:T(8,128)(2,1)S(1)}, u32[]{:S(2)}, u32[]{:S(2)}) collective-permute-start(bf16[256,128]{1,0:T(8,128)(2,1)S(1)} %get-tuple-element.43.refs_0_.refs_4_.own_ref), channel_id=1, source_target_pairs={{0,24},{4,28},{8,16},{12,20},{16,8},{20,12},{24,0},{28,4},{1,25},{... | collective-permute-start | bytes 196616 | tf_op jit(solution)/shard_map/ppermute | solution.py:514
  28.4 0.8 %collective-permute-start.1 = (bf16[256,128]{1,0:T(8,128)(2,1)S(1)}, bf16[256,128]{1,0:T(8,128)(2,1)S(1)}, u32[]{:S(2)}, u32[]{:S(2)}) collective-permute-start(bf16[256,128]{1,0:T(8,128)(2,1)S(1)} %get-tuple-element.43.refs_0_.refs_4_.own_ref), channel_id=1, source_target_pairs={{0,16},{4,20},{8,24},{12,28},{16,0},{20,4},{24,8},{28,12},{1,17},{... | collective-permute-start | bytes 196616 | tf_op jit(solution)/shard_map/ppermute | solution.py:514
  29.2 0.5 collective-permute-start
  29.8 2.8 %collective-permute-start.9 = (bf16[128,256]{1,0:T(8,128)(2,1)S(1)}, bf16[128,256]{1,0:T(8,128)(2,1)S(1)}, u32[]{:S(2)}, u32[]{:S(2)}) collective-permute-start(bf16[128,256]{1,0:T(8,128)(2,1)S(1)} %get-tuple-element.49.refs_4_), channel_id=1, source_target_pairs={{0,3},{1,2},{2,1},{3,0},{4,7},{5,6},{6,5},{7,4},{8,11},{9,10},{10,... | collective-permute-start | bytes 196616 | tf_op jit(solution)/shard_map/ppermute | solution.py:514
  32.6 1.1 %collective-permute-start.8 = (bf16[128,256]{1,0:T(8,128)(2,1)S(1)}, bf16[128,256]{1,0:T(8,128)(2,1)S(1)}, u32[]{:S(2)}, u32[]{:S(2)}) collective-permute-start(bf16[128,256]{1,0:T(8,128)(2,1)S(1)} %get-tuple-element.49.refs_4_), channel_id=1, source_target_pairs={{0,2},{1,3},{2,0},{3,1},{4,6},{5,7},{6,4},{7,5},{8,10},{9,11},{10,... | collective-permute-start | bytes 196616 | tf_op jit(solution)/shard_map/ppermute | solution.py:514
  33.7 0.9 %collective-permute-start.7 = (bf16[128,256]{1,0:T(8,128)(2,1)S(1)}, bf16[128,256]{1,0:T(8,128)(2,1)S(1)}, u32[]{:S(2)}, u32[]{:S(2)}) collective-permute-start(bf16[128,256]{1,0:T(8,128)(2,1)S(1)} %get-tuple-element.49.refs_4_), channel_id=1, source_target_pairs={{0,1},{1,0},{2,3},{3,2},{4,5},{5,4},{6,7},{7,6},{8,9},{9,8},{10,11... | collective-permute-start | bytes 196616 | tf_op jit(solution)/shard_map/ppermute | solution.py:514
  34.6 0.1 collective-permute-start.3
  34.7 2.0 %collective-permute-done.9.refs_7_ = bf16[128,256]{1,0:T(8,128)(2,1)S(1)} collective-permute-done((bf16[128,256]{1,0:T(8,128)(2,1)S(1)}, bf16[128,256]{1,0:T(8,128)(2,1)S(1)}, u32[]{:S(2)}, u32[]{:S(2)}) %collective-permute-start.9) | collective-permute-done | bytes 65568 | tf_op jit(solution)/shard_map/ppermute | solution.py:514
  36.6 2.9 %collective-permute-done.8.refs_6_ = bf16[128,256]{1,0:T(8,128)(2,1)S(1)} collective-permute-done((bf16[128,256]{1,0:T(8,128)(2,1)S(1)}, bf16[128,256]{1,0:T(8,128)(2,1)S(1)}, u32[]{:S(2)}, u32[]{:S(2)}) %collective-permute-start.8) | collective-permute-done | bytes 65568 | tf_op jit(solution)/shard_map/ppermute | solution.py:514
  39.5 0.7 item_sums.2
  40.3 0.1 collective-permute-start.10
  40.4 1.2 %user_sums.2 = (bf16[256,128]{1,0:T(8,128)(2,1)S(1)}, bf16[256,128]{1,0:T(8,128)(2,1)S(1)}, bf16[256,128]{1,0:T(8,128)(2,1)S(1)}, bf16[256,128]{1,0:T(8,128)(2,1)S(1)}) custom-call(bf16[256,2048]{1,0:T(8,128)(2,1)S(1)} %get-tuple-element.39.refs_0_, bf16[256,2048]{1,0:T(8,128)(2,1)S(1)} %get-tuple-element.40.refs_1_, ...), custom_call_target="tpu_custom_call" | custom-call | flops 536870912 | bytes 4194304 | tf_op jit(solution)/shard_map/user_sums/pallas_call | solution.py:385
  41.7 1.8 %collective-permute-start.5 = (bf16[256,128]{1,0:T(8,128)(2,1)S(1)}, bf16[256,128]{1,0:T(8,128)(2,1)S(1)}, u32[]{:S(2)}, u32[]{:S(2)}) collective-permute-start(bf16[256,128]{1,0:T(8,128)(2,1)S(1)} %get-tuple-element.46), channel_id=1, source_target_pairs={{0,2},{1,3},{2,0},{3,1},{4,6},{5,7},{6,4},{7,5},{8,10},{9,11},{10,... | collective-permute-start | bytes 196616 | tf_op jit(solution)/shard_map/ppermute | solution.py:514
  43.5 2.6 %collective-permute-start.6 = (bf16[256,128]{1,0:T(8,128)(2,1)S(1)}, bf16[256,128]{1,0:T(8,128)(2,1)S(1)}, u32[]{:S(2)}, u32[]{:S(2)}) collective-permute-start(bf16[256,128]{1,0:T(8,128)(2,1)S(1)} %get-tuple-element.47), channel_id=1, source_target_pairs={{0,3},{1,2},{2,1},{3,0},{4,7},{5,6},{6,5},{7,4},{8,11},{9,10},{10,... | collective-permute-start | bytes 196616 | tf_op jit(solution)/shard_map/ppermute | solution.py:514
  46.1 1.1 %collective-permute-start.11 = (bf16[128,256]{1,0:T(8,128)(2,1)S(1)}, bf16[128,256]{1,0:T(8,128)(2,1)S(1)}, u32[]{:S(2)}, u32[]{:S(2)}) collective-permute-start(bf16[128,256]{1,0:T(8,128)(2,1)S(1)} %get-tuple-element.53), channel_id=1, source_target_pairs={{0,8},{4,12},{8,0},{12,4},{16,24},{20,28},{24,16},{28,20},{1,9},{5... | collective-permute-start | bytes 196616 | tf_op jit(solution)/shard_map/ppermute | solution.py:514
  47.2 0.8 %collective-permute-start.12 = (bf16[128,256]{1,0:T(8,128)(2,1)S(1)}, bf16[128,256]{1,0:T(8,128)(2,1)S(1)}, u32[]{:S(2)}, u32[]{:S(2)}) collective-permute-start(bf16[128,256]{1,0:T(8,128)(2,1)S(1)} %get-tuple-element.54), channel_id=1, source_target_pairs={{0,16},{4,20},{8,24},{12,28},{16,0},{20,4},{24,8},{28,12},{1,17},{... | collective-permute-start | bytes 196616 | tf_op jit(solution)/shard_map/ppermute | solution.py:514
  48.0 1.6 %collective-permute-start.13 = (bf16[128,256]{1,0:T(8,128)(2,1)S(1)}, bf16[128,256]{1,0:T(8,128)(2,1)S(1)}, u32[]{:S(2)}, u32[]{:S(2)}) collective-permute-start(bf16[128,256]{1,0:T(8,128)(2,1)S(1)} %get-tuple-element.55), channel_id=1, source_target_pairs={{0,24},{4,28},{8,16},{12,20},{16,8},{20,12},{24,0},{28,4},{1,25},{... | collective-permute-start | bytes 196616 | tf_op jit(solution)/shard_map/ppermute | solution.py:514
  49.7 0.8 collective-permute-done.5.refs_2_
  50.4 0.3 user_update.2
  50.7 1.8 %collective-permute-start.23 = (bf16[128,256]{1,0:T(8,128)(2,1)S(1)}, bf16[128,256]{1,0:T(8,128)(2,1)S(1)}, u32[]{:S(2)}, u32[]{:S(2)}) collective-permute-start(bf16[128,256]{1,0:T(8,128)(2,1)S(1)} %get-tuple-element.61.refs_4_), channel_id=1, source_target_pairs={{0,3},{1,2},{2,1},{3,0},{4,7},{5,6},{6,5},{7,4},{8,11},{9,10},{10,... | collective-permute-start | bytes 196616 | tf_op jit(solution)/shard_map/ppermute | solution.py:514
  52.5 1.2 %collective-permute-start.22 = (bf16[128,256]{1,0:T(8,128)(2,1)S(1)}, bf16[128,256]{1,0:T(8,128)(2,1)S(1)}, u32[]{:S(2)}, u32[]{:S(2)}) collective-permute-start(bf16[128,256]{1,0:T(8,128)(2,1)S(1)} %get-tuple-element.61.refs_4_), channel_id=1, source_target_pairs={{0,2},{1,3},{2,0},{3,1},{4,6},{5,7},{6,4},{7,5},{8,10},{9,11},{10,... | collective-permute-start | bytes 196616 | tf_op jit(solution)/shard_map/ppermute | solution.py:514
  53.7 1.4 %collective-permute-start.21 = (bf16[128,256]{1,0:T(8,128)(2,1)S(1)}, bf16[128,256]{1,0:T(8,128)(2,1)S(1)}, u32[]{:S(2)}, u32[]{:S(2)}) collective-permute-start(bf16[128,256]{1,0:T(8,128)(2,1)S(1)} %get-tuple-element.61.refs_4_), channel_id=1, source_target_pairs={{0,1},{1,0},{2,3},{3,2},{4,5},{5,4},{6,7},{7,6},{8,9},{9,8},{10,11... | collective-permute-start | bytes 196616 | tf_op jit(solution)/shard_map/ppermute | solution.py:514
  55.2 0.3 item_update.2.refs_0_.refs_4_.own_ref
  55.4 1.4 %collective-permute-start.16 = (bf16[256,128]{1,0:T(8,128)(2,1)S(1)}, bf16[256,128]{1,0:T(8,128)(2,1)S(1)}, u32[]{:S(2)}, u32[]{:S(2)}) collective-permute-start(bf16[256,128]{1,0:T(8,128)(2,1)S(1)} %item_update.2.refs_0_.refs_4_.own_ref), channel_id=1, source_target_pairs={{0,24},{4,28},{8,16},{12,20},{16,8},{20,12},{24,0},{28,4},{1,25},{... | collective-permute-start | bytes 196616 | tf_op jit(solution)/shard_map/ppermute | solution.py:514
  56.8 1.2 %collective-permute-start.15 = (bf16[256,128]{1,0:T(8,128)(2,1)S(1)}, bf16[256,128]{1,0:T(8,128)(2,1)S(1)}, u32[]{:S(2)}, u32[]{:S(2)}) collective-permute-start(bf16[256,128]{1,0:T(8,128)(2,1)S(1)} %item_update.2.refs_0_.refs_4_.own_ref), channel_id=1, source_target_pairs={{0,16},{4,20},{8,24},{12,28},{16,0},{20,4},{24,8},{28,12},{1,17},{... | collective-permute-start | bytes 196616 | tf_op jit(solution)/shard_map/ppermute | solution.py:514
  58.0 1.0 %collective-permute-start.14 = (bf16[256,128]{1,0:T(8,128)(2,1)S(1)}, bf16[256,128]{1,0:T(8,128)(2,1)S(1)}, u32[]{:S(2)}, u32[]{:S(2)}) collective-permute-start(bf16[256,128]{1,0:T(8,128)(2,1)S(1)} %item_update.2.refs_0_.refs_4_.own_ref), channel_id=1, source_target_pairs={{0,8},{4,12},{8,0},{12,4},{16,24},{20,28},{24,16},{28,20},{1,9},{5... | collective-permute-start | bytes 196616 | tf_op jit(solution)/shard_map/ppermute | solution.py:514
  59.0 0.5 collective-permute-done.22.refs_6_
  59.5 0.7 item_sums.3
  60.3 0.4 collective-permute-done.16.refs_3_.refs_7_
  60.7 0.7 collective-permute-done.15.refs_2_.refs_6_
  61.4 0.9 %collective-permute-done.14.refs_1_.refs_5_ = bf16[256,128]{1,0:T(8,128)(2,1)S(1)} collective-permute-done((bf16[256,128]{1,0:T(8,128)(2,1)S(1)}, bf16[256,128]{1,0:T(8,128)(2,1)S(1)}, u32[]{:S(2)}, u32[]{:S(2)}) %collective-permute-start.14) | collective-permute-done | bytes 65568 | tf_op jit(solution)/shard_map/ppermute | solution.py:514
  62.4 1.1 %collective-permute-start.25 = (bf16[128,256]{1,0:T(8,128)(2,1)S(1)}, bf16[128,256]{1,0:T(8,128)(2,1)S(1)}, u32[]{:S(2)}, u32[]{:S(2)}) collective-permute-start(bf16[128,256]{1,0:T(8,128)(2,1)S(1)} %get-tuple-element.65), channel_id=1, source_target_pairs={{0,8},{4,12},{8,0},{12,4},{16,24},{20,28},{24,16},{28,20},{1,9},{5... | collective-permute-start | bytes 196616 | tf_op jit(solution)/shard_map/ppermute | solution.py:514
  63.5 1.1 %collective-permute-start.26 = (bf16[128,256]{1,0:T(8,128)(2,1)S(1)}, bf16[128,256]{1,0:T(8,128)(2,1)S(1)}, u32[]{:S(2)}, u32[]{:S(2)}) collective-permute-start(bf16[128,256]{1,0:T(8,128)(2,1)S(1)} %get-tuple-element.66), channel_id=1, source_target_pairs={{0,16},{4,20},{8,24},{12,28},{16,0},{20,4},{24,8},{28,12},{1,17},{... | collective-permute-start | bytes 196616 | tf_op jit(solution)/shard_map/ppermute | solution.py:514
  64.6 1.4 %collective-permute-start.27 = (bf16[128,256]{1,0:T(8,128)(2,1)S(1)}, bf16[128,256]{1,0:T(8,128)(2,1)S(1)}, u32[]{:S(2)}, u32[]{:S(2)}) collective-permute-start(bf16[128,256]{1,0:T(8,128)(2,1)S(1)} %get-tuple-element.67), channel_id=1, source_target_pairs={{0,24},{4,28},{8,16},{12,20},{16,8},{20,12},{24,0},{28,4},{1,25},{... | collective-permute-start | bytes 196616 | tf_op jit(solution)/shard_map/ppermute | solution.py:514
  66.0 1.2 %user_sums.3 = (bf16[256,128]{1,0:T(8,128)(2,1)S(1)}, bf16[256,128]{1,0:T(8,128)(2,1)S(1)}, bf16[256,128]{1,0:T(8,128)(2,1)S(1)}, bf16[256,128]{1,0:T(8,128)(2,1)S(1)}) custom-call(bf16[256,2048]{1,0:T(8,128)(2,1)S(1)} %get-tuple-element.39.refs_0_, bf16[256,2048]{1,0:T(8,128)(2,1)S(1)} %get-tuple-element.40.refs_1_, ...), custom_call_target="tpu_custom_call" | custom-call | flops 536870912 | bytes 4194304 | tf_op jit(solution)/shard_map/user_sums/pallas_call | solution.py:385
  67.2 1.3 %collective-permute-start.18 = (bf16[256,128]{1,0:T(8,128)(2,1)S(1)}, bf16[256,128]{1,0:T(8,128)(2,1)S(1)}, u32[]{:S(2)}, u32[]{:S(2)}) collective-permute-start(bf16[256,128]{1,0:T(8,128)(2,1)S(1)} %get-tuple-element.57), channel_id=1, source_target_pairs={{0,1},{1,0},{2,3},{3,2},{4,5},{5,4},{6,7},{7,6},{8,9},{9,8},{10,11... | collective-permute-start | bytes 196616 | tf_op jit(solution)/shard_map/ppermute | solution.py:514
  68.6 1.2 %collective-permute-start.19 = (bf16[256,128]{1,0:T(8,128)(2,1)S(1)}, bf16[256,128]{1,0:T(8,128)(2,1)S(1)}, u32[]{:S(2)}, u32[]{:S(2)}) collective-permute-start(bf16[256,128]{1,0:T(8,128)(2,1)S(1)} %get-tuple-element.58), channel_id=1, source_target_pairs={{0,2},{1,3},{2,0},{3,1},{4,6},{5,7},{6,4},{7,5},{8,10},{9,11},{10,... | collective-permute-start | bytes 196616 | tf_op jit(solution)/shard_map/ppermute | solution.py:514
  69.8 1.9 %collective-permute-start.20 = (bf16[256,128]{1,0:T(8,128)(2,1)S(1)}, bf16[256,128]{1,0:T(8,128)(2,1)S(1)}, u32[]{:S(2)}, u32[]{:S(2)}) collective-permute-start(bf16[256,128]{1,0:T(8,128)(2,1)S(1)} %get-tuple-element.59), channel_id=1, source_target_pairs={{0,3},{1,2},{2,1},{3,0},{4,7},{5,6},{6,5},{7,4},{8,11},{9,10},{10,... | collective-permute-start | bytes 196616 | tf_op jit(solution)/shard_map/ppermute | solution.py:514
  71.7 0.9 %item_update.3 = bf16[256,128]{1,0:T(8,128)(2,1)} custom-call(bf16[256,128]{1,0:T(8,128)(2,1)S(1)} %item_update.2.refs_0_.refs_4_.own_ref, bf16[2,128,128]{2,1,0:T(8,128)(2,1)S(1)} %copy-done, bf16[2,128,128]{2,1,0:T(8,128)(2,1)S(1)} %copy-done.1, bf16[128,256]{1,0:T(8,128)(2,1)S(1)} %get-tuple-element.64.refs_0_, ...), custom_call_target="tpu_custom_call" | custom-call | tf_op jit(solution)/shard_map/item_update/pallas_call | solution.py:498
  72.6 3.8 %collective-permute-done.19.refs_2_ = bf16[256,128]{1,0:T(8,128)(2,1)S(1)} collective-permute-done((bf16[256,128]{1,0:T(8,128)(2,1)S(1)}, bf16[256,128]{1,0:T(8,128)(2,1)S(1)}, u32[]{:S(2)}, u32[]{:S(2)}) %collective-permute-start.19) | collective-permute-done | bytes 65568 | tf_op jit(solution)/shard_map/ppermute | solution.py:514
  76.3 0.9 %user_update.3 = (bf16[256,128]{1,0:T(8,128)(2,1)}, bf16[128,256]{1,0:T(8,128)(2,1)}) custom-call(bf16[256,128]{1,0:T(8,128)(2,1)S(1)} %get-tuple-element.48.own_ref, bf16[2,128,128]{2,1,0:T(8,128)(2,1)S(1)} %copy-done, bf16[2,128,128]{2,1,0:T(8,128)(2,1)S(1)} %copy-done.1, bf16[256,128]{1,0:T(8,128)(2,1)S(1)} %get-tuple-element.56.refs_0_, ...), custom_call_target="tpu_custom_call" | custom-call | tf_op jit(solution)/shard_map/user_update/pallas_call | solution.py:478
  (37 shorter events, 0.4 us)
Async XLA Ops:
  4.0 20.3 %copy-start.2 = (bf16[64,128]{1,0:T(8,128)(2,1)S(1)}, bf16[64,128]{1,0:T(8,128)(2,1)}, u32[]{:S(2)}) copy-start(bf16[64,128]{1,0:T(8,128)(2,1)} %proj_wide_ref.1) | copy-start | bytes 49156
  4.0 20.3 %copy-start.3 = (bf16[32,128]{1,0:T(8,128)(2,1)S(1)}, bf16[32,128]{1,0:T(8,128)(2,1)}, u32[]{:S(2)}) copy-start(bf16[32,128]{1,0:T(8,128)(2,1)} %proj_narrow_ref.1) | copy-start | bytes 24580
  4.0 20.3 %all-to-all-start = ((bf16[32,56,128]{2,1,0:T(8,128)(2,1)}), bf16[32,56,128]{2,1,0:T(8,128)(2,1)S(1)}, u32[]{:S(2)}, u32[]{:S(2)}) async-start(bf16[32,56,128]{2,1,0:T(8,128)(2,1)} %dispatch.1), calls=%async_computation | async-start | bytes 917504 | tf_op jit(solution)/shard_map/all_to_all | solution.py:560
  11.4 0.7 copy-start.4
  12.0 0.7 copy-start.5
  26.2 7.4 %collective-permute-start.2 = (bf16[256,128]{1,0:T(8,128)(2,1)S(1)}, bf16[256,128]{1,0:T(8,128)(2,1)S(1)}, u32[]{:S(2)}, u32[]{:S(2)}) collective-permute-start(bf16[256,128]{1,0:T(8,128)(2,1)S(1)} %get-tuple-element.43.refs_0_.refs_4_.own_ref), channel_id=1, source_target_pairs={{0,24},{4,28},{8,16},{12,20},{16,8},{20,12},{24,0},{28,4},{1,25},{... | collective-permute-start | bytes 196616 | tf_op jit(solution)/shard_map/ppermute | solution.py:514
  28.4 6.2 %collective-permute-start.1 = (bf16[256,128]{1,0:T(8,128)(2,1)S(1)}, bf16[256,128]{1,0:T(8,128)(2,1)S(1)}, u32[]{:S(2)}, u32[]{:S(2)}) collective-permute-start(bf16[256,128]{1,0:T(8,128)(2,1)S(1)} %get-tuple-element.43.refs_0_.refs_4_.own_ref), channel_id=1, source_target_pairs={{0,16},{4,20},{8,24},{12,28},{16,0},{20,4},{24,8},{28,12},{1,17},{... | collective-permute-start | bytes 196616 | tf_op jit(solution)/shard_map/ppermute | solution.py:514
  29.2 5.3 %collective-permute-start = (bf16[256,128]{1,0:T(8,128)(2,1)S(1)}, bf16[256,128]{1,0:T(8,128)(2,1)S(1)}, u32[]{:S(2)}, u32[]{:S(2)}) collective-permute-start(bf16[256,128]{1,0:T(8,128)(2,1)S(1)} %get-tuple-element.43.refs_0_.refs_4_.own_ref), channel_id=1, source_target_pairs={{0,8},{4,12},{8,0},{12,4},{16,24},{20,28},{24,16},{28,20},{1,9},{5... | collective-permute-start | bytes 196616 | tf_op jit(solution)/shard_map/ppermute | solution.py:514
  29.8 6.9 %collective-permute-start.9 = (bf16[128,256]{1,0:T(8,128)(2,1)S(1)}, bf16[128,256]{1,0:T(8,128)(2,1)S(1)}, u32[]{:S(2)}, u32[]{:S(2)}) collective-permute-start(bf16[128,256]{1,0:T(8,128)(2,1)S(1)} %get-tuple-element.49.refs_4_), channel_id=1, source_target_pairs={{0,3},{1,2},{2,1},{3,0},{4,7},{5,6},{6,5},{7,4},{8,11},{9,10},{10,... | collective-permute-start | bytes 196616 | tf_op jit(solution)/shard_map/ppermute | solution.py:514
  32.6 6.9 %collective-permute-start.8 = (bf16[128,256]{1,0:T(8,128)(2,1)S(1)}, bf16[128,256]{1,0:T(8,128)(2,1)S(1)}, u32[]{:S(2)}, u32[]{:S(2)}) collective-permute-start(bf16[128,256]{1,0:T(8,128)(2,1)S(1)} %get-tuple-element.49.refs_4_), channel_id=1, source_target_pairs={{0,2},{1,3},{2,0},{3,1},{4,6},{5,7},{6,4},{7,5},{8,10},{9,11},{10,... | collective-permute-start | bytes 196616 | tf_op jit(solution)/shard_map/ppermute | solution.py:514
  33.7 5.9 %collective-permute-start.7 = (bf16[128,256]{1,0:T(8,128)(2,1)S(1)}, bf16[128,256]{1,0:T(8,128)(2,1)S(1)}, u32[]{:S(2)}, u32[]{:S(2)}) collective-permute-start(bf16[128,256]{1,0:T(8,128)(2,1)S(1)} %get-tuple-element.49.refs_4_), channel_id=1, source_target_pairs={{0,1},{1,0},{2,3},{3,2},{4,5},{5,4},{6,7},{7,6},{8,9},{9,8},{10,11... | collective-permute-start | bytes 196616 | tf_op jit(solution)/shard_map/ppermute | solution.py:514
  34.6 5.8 %collective-permute-start.3 = (bf16[4,256,128]{2,1,0:T(8,128)(2,1)S(1)}, bf16[4,256,128]{2,1,0:T(8,128)(2,1)S(1)}, u32[]{:S(2)}, u32[]{:S(2)}) collective-permute-start(bf16[4,256,128]{2,1,0:T(8,128)(2,1)S(1)} %merge.2), channel_id=1, source_target_pairs={{0,4},{4,0},{8,12},{12,8},{16,20},{20,16},{24,28},{28,24},{1,5},{5... | collective-permute-start | bytes 786440 | tf_op jit(solution)/shard_map/ppermute | solution.py:519
  39.5 10.9 %copy-start = (bf16[2,128,128]{2,1,0:T(8,128)(2,1)S(1)}, bf16[2,128,128]{2,1,0:T(8,128)(2,1)}, u32[]{:S(2)}) copy-start(bf16[2,128,128]{2,1,0:T(8,128)(2,1)} %sum_ref.7) | copy-start | bytes 196612
  39.5 10.9 %copy-start.1 = (bf16[2,128,128]{2,1,0:T(8,128)(2,1)S(1)}, bf16[2,128,128]{2,1,0:T(8,128)(2,1)}, u32[]{:S(2)}) copy-start(bf16[2,128,128]{2,1,0:T(8,128)(2,1)} %product_ref.7) | copy-start | bytes 196612
  40.3 5.8 %collective-permute-start.10 = (bf16[4,128,256]{2,1,0:T(8,128)(2,1)S(1)}, bf16[4,128,256]{2,1,0:T(8,128)(2,1)S(1)}, u32[]{:S(2)}, u32[]{:S(2)}) collective-permute-start(bf16[4,128,256]{2,1,0:T(8,128)(2,1)S(1)} %get-tuple-element.51), channel_id=1, source_target_pairs={{0,4},{4,0},{8,12},{12,8},{16,20},{20,16},{24,28},{28,24},{1,5},{5... | collective-permute-start | bytes 786440 | tf_op jit(solution)/shard_map/ppermute | solution.py:519
  41.6 6.4 %collective-permute-start.4 = (bf16[256,128]{1,0:T(8,128)(2,1)S(1)}, bf16[256,128]{1,0:T(8,128)(2,1)S(1)}, u32[]{:S(2)}, u32[]{:S(2)}) collective-permute-start(bf16[256,128]{1,0:T(8,128)(2,1)S(1)} %get-tuple-element.45), channel_id=1, source_target_pairs={{0,1},{1,0},{2,3},{3,2},{4,5},{5,4},{6,7},{7,6},{8,9},{9,8},{10,11... | collective-permute-start | bytes 196616 | tf_op jit(solution)/shard_map/ppermute | solution.py:514
  41.7 8.7 %collective-permute-start.5 = (bf16[256,128]{1,0:T(8,128)(2,1)S(1)}, bf16[256,128]{1,0:T(8,128)(2,1)S(1)}, u32[]{:S(2)}, u32[]{:S(2)}) collective-permute-start(bf16[256,128]{1,0:T(8,128)(2,1)S(1)} %get-tuple-element.46), channel_id=1, source_target_pairs={{0,2},{1,3},{2,0},{3,1},{4,6},{5,7},{6,4},{7,5},{8,10},{9,11},{10,... | collective-permute-start | bytes 196616 | tf_op jit(solution)/shard_map/ppermute | solution.py:514
  43.5 7.0 %collective-permute-start.6 = (bf16[256,128]{1,0:T(8,128)(2,1)S(1)}, bf16[256,128]{1,0:T(8,128)(2,1)S(1)}, u32[]{:S(2)}, u32[]{:S(2)}) collective-permute-start(bf16[256,128]{1,0:T(8,128)(2,1)S(1)} %get-tuple-element.47), channel_id=1, source_target_pairs={{0,3},{1,2},{2,1},{3,0},{4,7},{5,6},{6,5},{7,4},{8,11},{9,10},{10,... | collective-permute-start | bytes 196616 | tf_op jit(solution)/shard_map/ppermute | solution.py:514
  46.1 7.6 %collective-permute-start.11 = (bf16[128,256]{1,0:T(8,128)(2,1)S(1)}, bf16[128,256]{1,0:T(8,128)(2,1)S(1)}, u32[]{:S(2)}, u32[]{:S(2)}) collective-permute-start(bf16[128,256]{1,0:T(8,128)(2,1)S(1)} %get-tuple-element.53), channel_id=1, source_target_pairs={{0,8},{4,12},{8,0},{12,4},{16,24},{20,28},{24,16},{28,20},{1,9},{5... | collective-permute-start | bytes 196616 | tf_op jit(solution)/shard_map/ppermute | solution.py:514
  47.2 8.0 %collective-permute-start.12 = (bf16[128,256]{1,0:T(8,128)(2,1)S(1)}, bf16[128,256]{1,0:T(8,128)(2,1)S(1)}, u32[]{:S(2)}, u32[]{:S(2)}) collective-permute-start(bf16[128,256]{1,0:T(8,128)(2,1)S(1)} %get-tuple-element.54), channel_id=1, source_target_pairs={{0,16},{4,20},{8,24},{12,28},{16,0},{20,4},{24,8},{28,12},{1,17},{... | collective-permute-start | bytes 196616 | tf_op jit(solution)/shard_map/ppermute | solution.py:514
  48.0 7.1 %collective-permute-start.13 = (bf16[128,256]{1,0:T(8,128)(2,1)S(1)}, bf16[128,256]{1,0:T(8,128)(2,1)S(1)}, u32[]{:S(2)}, u32[]{:S(2)}) collective-permute-start(bf16[128,256]{1,0:T(8,128)(2,1)S(1)} %get-tuple-element.55), channel_id=1, source_target_pairs={{0,24},{4,28},{8,16},{12,20},{16,8},{20,12},{24,0},{28,4},{1,25},{... | collective-permute-start | bytes 196616 | tf_op jit(solution)/shard_map/ppermute | solution.py:514
  50.7 7.3 %collective-permute-start.23 = (bf16[128,256]{1,0:T(8,128)(2,1)S(1)}, bf16[128,256]{1,0:T(8,128)(2,1)S(1)}, u32[]{:S(2)}, u32[]{:S(2)}) collective-permute-start(bf16[128,256]{1,0:T(8,128)(2,1)S(1)} %get-tuple-element.61.refs_4_), channel_id=1, source_target_pairs={{0,3},{1,2},{2,1},{3,0},{4,7},{5,6},{6,5},{7,4},{8,11},{9,10},{10,... | collective-permute-start | bytes 196616 | tf_op jit(solution)/shard_map/ppermute | solution.py:514
  52.5 7.1 %collective-permute-start.22 = (bf16[128,256]{1,0:T(8,128)(2,1)S(1)}, bf16[128,256]{1,0:T(8,128)(2,1)S(1)}, u32[]{:S(2)}, u32[]{:S(2)}) collective-permute-start(bf16[128,256]{1,0:T(8,128)(2,1)S(1)} %get-tuple-element.61.refs_4_), channel_id=1, source_target_pairs={{0,2},{1,3},{2,0},{3,1},{4,6},{5,7},{6,4},{7,5},{8,10},{9,11},{10,... | collective-permute-start | bytes 196616 | tf_op jit(solution)/shard_map/ppermute | solution.py:514
  53.7 5.8 %collective-permute-start.21 = (bf16[128,256]{1,0:T(8,128)(2,1)S(1)}, bf16[128,256]{1,0:T(8,128)(2,1)S(1)}, u32[]{:S(2)}, u32[]{:S(2)}) collective-permute-start(bf16[128,256]{1,0:T(8,128)(2,1)S(1)} %get-tuple-element.61.refs_4_), channel_id=1, source_target_pairs={{0,1},{1,0},{2,3},{3,2},{4,5},{5,4},{6,7},{7,6},{8,9},{9,8},{10,11... | collective-permute-start | bytes 196616 | tf_op jit(solution)/shard_map/ppermute | solution.py:514
  55.4 5.3 %collective-permute-start.16 = (bf16[256,128]{1,0:T(8,128)(2,1)S(1)}, bf16[256,128]{1,0:T(8,128)(2,1)S(1)}, u32[]{:S(2)}, u32[]{:S(2)}) collective-permute-start(bf16[256,128]{1,0:T(8,128)(2,1)S(1)} %item_update.2.refs_0_.refs_4_.own_ref), channel_id=1, source_target_pairs={{0,24},{4,28},{8,16},{12,20},{16,8},{20,12},{24,0},{28,4},{1,25},{... | collective-permute-start | bytes 196616 | tf_op jit(solution)/shard_map/ppermute | solution.py:514
  56.8 4.6 %collective-permute-start.15 = (bf16[256,128]{1,0:T(8,128)(2,1)S(1)}, bf16[256,128]{1,0:T(8,128)(2,1)S(1)}, u32[]{:S(2)}, u32[]{:S(2)}) collective-permute-start(bf16[256,128]{1,0:T(8,128)(2,1)S(1)} %item_update.2.refs_0_.refs_4_.own_ref), channel_id=1, source_target_pairs={{0,16},{4,20},{8,24},{12,28},{16,0},{20,4},{24,8},{28,12},{1,17},{... | collective-permute-start | bytes 196616 | tf_op jit(solution)/shard_map/ppermute | solution.py:514
  58.0 4.3 %collective-permute-start.14 = (bf16[256,128]{1,0:T(8,128)(2,1)S(1)}, bf16[256,128]{1,0:T(8,128)(2,1)S(1)}, u32[]{:S(2)}, u32[]{:S(2)}) collective-permute-start(bf16[256,128]{1,0:T(8,128)(2,1)S(1)} %item_update.2.refs_0_.refs_4_.own_ref), channel_id=1, source_target_pairs={{0,8},{4,12},{8,0},{12,4},{16,24},{20,28},{24,16},{28,20},{1,9},{5... | collective-permute-start | bytes 196616 | tf_op jit(solution)/shard_map/ppermute | solution.py:514
  60.3 2.1 %collective-permute-start.24 = (bf16[4,128,256]{2,1,0:T(8,128)(2,1)S(1)}, bf16[4,128,256]{2,1,0:T(8,128)(2,1)S(1)}, u32[]{:S(2)}, u32[]{:S(2)}) collective-permute-start(bf16[4,128,256]{2,1,0:T(8,128)(2,1)S(1)} %get-tuple-element.63), channel_id=1, source_target_pairs={{0,4},{4,0},{8,12},{12,8},{16,20},{20,16},{24,28},{28,24},{1,5},{5... | collective-permute-start | bytes 786440 | tf_op jit(solution)/shard_map/ppermute | solution.py:519
  62.3 3.7 %collective-permute-start.17 = (bf16[4,256,128]{2,1,0:T(8,128)(2,1)S(1)}, bf16[4,256,128]{2,1,0:T(8,128)(2,1)S(1)}, u32[]{:S(2)}, u32[]{:S(2)}) collective-permute-start(bf16[4,256,128]{2,1,0:T(8,128)(2,1)S(1)} %merge.3), channel_id=1, source_target_pairs={{0,4},{4,0},{8,12},{12,8},{16,20},{20,16},{24,28},{28,24},{1,5},{5... | collective-permute-start | bytes 786440 | tf_op jit(solution)/shard_map/ppermute | solution.py:519
  62.4 7.4 %collective-permute-start.25 = (bf16[128,256]{1,0:T(8,128)(2,1)S(1)}, bf16[128,256]{1,0:T(8,128)(2,1)S(1)}, u32[]{:S(2)}, u32[]{:S(2)}) collective-permute-start(bf16[128,256]{1,0:T(8,128)(2,1)S(1)} %get-tuple-element.65), channel_id=1, source_target_pairs={{0,8},{4,12},{8,0},{12,4},{16,24},{20,28},{24,16},{28,20},{1,9},{5... | collective-permute-start | bytes 196616 | tf_op jit(solution)/shard_map/ppermute | solution.py:514
  63.5 8.2 %collective-permute-start.26 = (bf16[128,256]{1,0:T(8,128)(2,1)S(1)}, bf16[128,256]{1,0:T(8,128)(2,1)S(1)}, u32[]{:S(2)}, u32[]{:S(2)}) collective-permute-start(bf16[128,256]{1,0:T(8,128)(2,1)S(1)} %get-tuple-element.66), channel_id=1, source_target_pairs={{0,16},{4,20},{8,24},{12,28},{16,0},{20,4},{24,8},{28,12},{1,17},{... | collective-permute-start | bytes 196616 | tf_op jit(solution)/shard_map/ppermute | solution.py:514
  64.6 7.1 %collective-permute-start.27 = (bf16[128,256]{1,0:T(8,128)(2,1)S(1)}, bf16[128,256]{1,0:T(8,128)(2,1)S(1)}, u32[]{:S(2)}, u32[]{:S(2)}) collective-permute-start(bf16[128,256]{1,0:T(8,128)(2,1)S(1)} %get-tuple-element.67), channel_id=1, source_target_pairs={{0,24},{4,28},{8,16},{12,20},{16,8},{20,12},{24,0},{28,4},{1,25},{... | collective-permute-start | bytes 196616 | tf_op jit(solution)/shard_map/ppermute | solution.py:514
  67.2 5.4 %collective-permute-start.18 = (bf16[256,128]{1,0:T(8,128)(2,1)S(1)}, bf16[256,128]{1,0:T(8,128)(2,1)S(1)}, u32[]{:S(2)}, u32[]{:S(2)}) collective-permute-start(bf16[256,128]{1,0:T(8,128)(2,1)S(1)} %get-tuple-element.57), channel_id=1, source_target_pairs={{0,1},{1,0},{2,3},{3,2},{4,5},{5,4},{6,7},{7,6},{8,9},{9,8},{10,11... | collective-permute-start | bytes 196616 | tf_op jit(solution)/shard_map/ppermute | solution.py:514
  68.6 7.8 %collective-permute-start.19 = (bf16[256,128]{1,0:T(8,128)(2,1)S(1)}, bf16[256,128]{1,0:T(8,128)(2,1)S(1)}, u32[]{:S(2)}, u32[]{:S(2)}) collective-permute-start(bf16[256,128]{1,0:T(8,128)(2,1)S(1)} %get-tuple-element.58), channel_id=1, source_target_pairs={{0,2},{1,3},{2,0},{3,1},{4,6},{5,7},{6,4},{7,5},{8,10},{9,11},{10,... | collective-permute-start | bytes 196616 | tf_op jit(solution)/shard_map/ppermute | solution.py:514
  69.8 6.5 %collective-permute-start.20 = (bf16[256,128]{1,0:T(8,128)(2,1)S(1)}, bf16[256,128]{1,0:T(8,128)(2,1)S(1)}, u32[]{:S(2)}, u32[]{:S(2)}) collective-permute-start(bf16[256,128]{1,0:T(8,128)(2,1)S(1)} %get-tuple-element.59), channel_id=1, source_target_pairs={{0,3},{1,2},{2,1},{3,0},{4,7},{5,6},{6,5},{7,4},{8,11},{9,10},{10,... | collective-permute-start | bytes 196616 | tf_op jit(solution)/shard_map/ppermute | solution.py:514

commit v5 on v4

--- a/solution.py
+++ b/solution.py
@@ -164,11 +164,28 @@
         jnp.where(code == 1, slot // 256 * 2 + wide_ref[...], 0),
     )
     ext = jnp.concatenate([raw_ref[...], codes.astype(F32).astype(BF16)], axis=0)
-    height = ext.shape[0]
+    height = features + CODE_ROWS
+    middle = jnp.concatenate(
+        [ext[features : features + CODE_ROWS].astype(F32), ext[:CODE_ROWS].astype(F32)], axis=0
+    ).astype(BF16)
+    rest = jnp.concatenate(
+        [ext[CODE_ROWS:features].astype(F32), ext[features : features + CODE_ROWS].astype(F32)],
+        axis=0,
+    ).astype(BF16)
+    upper = lax.broadcasted_iota(jnp.int32, (2 * CODE_ROWS, 1), 0) < CODE_ROWS
     writes = []
     for n, first in enumerate(range(0, devices, GROUP)):
         masked = jnp.concatenate(
-            [ext * hot_bf[d : d + 1, :] for d in range(first, first + GROUP)], axis=0
+            [
+                piece
+                for d in range(first, first + GROUP, 2)
+                for piece in (
+                    ext[:features] * hot_bf[d : d + 1],
+                    middle * jnp.where(upper, hot_bf[d : d + 1], hot_bf[d + 1 : d + 2]),
+                    rest * hot_bf[d + 1 : d + 2],
+                )
+            ],
+            axis=0,
         )
         placed = lax.dot_general(masked, place, NT, preferred_element_type=F32)
         for d in range(GROUP):

time: 77.6 us -> 77.4 us (level)
  no operation moved by 1% of the time
where the time goes in v5:
time: 77.4 us; the launch traced here: 77.1 us
  starting transfers between devices  40 us (52%)
  waiting for transfers between devices  18.4 us (24%)
  Pallas kernels  16.5 us (21%)
  local copies, waits for them, and re-layouts  1.39 us (2%)
  between operations  0.84 us (1%)
    ppermute x24, starting transfers between devices, exchange(): received.append(lax.ppermute(blocks[k], axis, pairs))  32.4 us
    ppermute x24, waiting for transfers between devices, exchange(): received.append(lax.ppermute(blocks[k], axis, pairs))  11.9 us
    all_to_all x1, starting transfers between devices, per_device(): lax.all_to_all(send, ('row', 'col'), split_axis=0, concat_axis=0, tiled=T...  7.33 us
    all_to_all x1, waiting for transfers between devices, per_device(): lax.all_to_all(send, ('row', 'col'), split_axis=0, concat_axis=0, tiled=T...  6.58 us
    pallas_call x1, Pallas kernels, dequantize(): pl.pallas_call(functools.partial(dequantize_kernel, shape), out_shape=(ja...  5.01 us
    pallas_call x1, Pallas kernels, dispatch(): pl.pallas_call(functools.partial(dispatch_kernel, devices, capacity), out...  3.22 us
    pallas_call x2, Pallas kernels, user_sums(): pl.pallas_call(functools.partial(user_sum_kernel, cols), out_shape=(jax.S...  2.49 us
    pallas_call x1, Pallas kernels, segment(): pl.pallas_call(functools.partial(segment_kernel, capacity, upd, cols), ou...  1.88 us
  transfers between devices with their start and end apart: 29, of which 9 were waited for; matrix products, arithmetic and copies ran while one was open for 0% of the time, Pallas kernels for 14%

profile of v5, /device:TPU:0, one launch (start us, length us, event | category | flops | bytes accessed | tf_op | source)
XLA Modules:
  0.0 77.1 jit_solution(4214015999233415568)
XLA Ops:
  0.6 3.2 %dispatch.1 = bf16[32,56,128]{2,1,0:T(8,128)(2,1)} custom-call(s32[1]{0:T(128)} %bitcast.me_ref, bf16[64,1024]{1,0:T(8,128)(2,1)} %bitcast.6, s32[1,1024]{1,0:T(1,128)} %bitcast.8, s32[1,1024]{1,0:T(1,128)} %bitcast.9, s32[1,1024]{1,0:T(1,128)} %bitcast.10), custom_call_target="tpu_custom_call" | custom-call | tf_op jit(solution)/shard_map/dispatch/pallas_call | solution.py:213
  3.9 7.3 %all-to-all-start = ((bf16[32,56,128]{2,1,0:T(8,128)(2,1)}), bf16[32,56,128]{2,1,0:T(8,128)(2,1)S(1)}, u32[]{:S(2)}, u32[]{:S(2)}) async-start(bf16[32,56,128]{2,1,0:T(8,128)(2,1)} %dispatch.1), calls=%async_computation | async-start | bytes 917504 | tf_op jit(solution)/shard_map/all_to_all | solution.py:577
  11.2 0.7 copy-done.4
  11.9 0.7 copy-done.5
  12.6 5.0 %dequantize.1 = (bf16[256,2048]{1,0:T(8,128)(2,1)S(1)}, bf16[256,2048]{1,0:T(8,128)(2,1)}, bf16[256,2048]{1,0:T(8,128)(2,1)}, bf16[256,2048]{1,0:T(8,128)(2,1)}) custom-call(s32[1]{0:T(128)} %bitcast.me_ref, s32[8,16]{1,0:T(8,128)S(1)} %copy-done.4, f32[8,16]{1,0:T(8,128)S(1)} %copy-done.5, bf16[1024,2048]{1,0:T(8,128)(2,1)} %values_ref.1), custom_call_target="tpu_custom_call" | custom-call | flops 2097152 | bytes 8388608 | tf_op jit(solution)/shard_map/dequantize/pallas_call | solution.py:356
  17.6 6.6 %all-to-all-done.recv_ref = bf16[32,56,128]{2,1,0:T(8,128)(2,1)S(1)} async-done(((bf16[32,56,128]{2,1,0:T(8,128)(2,1)}), bf16[32,56,128]{2,1,0:T(8,128)(2,1)S(1)}, u32[]{:S(2)}, u32[]{:S(2)}) %all-to-all-start) | async-done | bytes 458784 | tf_op jit(solution)/shard_map/all_to_all | solution.py:577
  24.2 1.9 %segment.1 = (bf16[256,128]{1,0:T(8,128)(2,1)S(1)}, bf16[128,256]{1,0:T(8,128)(2,1)S(1)}, bf16[256,128]{1,0:T(8,128)(2,1)S(1)}, bf16[256,2048]{1,0:T(8,128)(2,1)...) custom-call(s32[1]{0:T(128)} %bitcast.me_ref, bf16[32,56,128]{2,1,0:T(8,128)(2,1)S(1)} %all-to-all-done.recv_ref, ...), custom_call_target="tpu_custom_call" | custom-call | tf_op jit(solution)/shard_map/segment/pallas_call | solution.py:287
  26.1 2.2 %collective-permute-start.2 = (bf16[256,128]{1,0:T(8,128)(2,1)S(1)}, bf16[256,128]{1,0:T(8,128)(2,1)S(1)}, u32[]{:S(2)}, u32[]{:S(2)}) collective-permute-start(bf16[256,128]{1,0:T(8,128)(2,1)S(1)} %get-tuple-element.43.refs_0_.refs_4_.own_ref), channel_id=1, source_target_pairs={{0,24},{4,28},{8,16},{12,20},{16,8},{20,12},{24,0},{28,4},{1,25},{... | collective-permute-start | bytes 196616 | tf_op jit(solution)/shard_map/ppermute | solution.py:531
  28.3 0.8 %collective-permute-start.1 = (bf16[256,128]{1,0:T(8,128)(2,1)S(1)}, bf16[256,128]{1,0:T(8,128)(2,1)S(1)}, u32[]{:S(2)}, u32[]{:S(2)}) collective-permute-start(bf16[256,128]{1,0:T(8,128)(2,1)S(1)} %get-tuple-element.43.refs_0_.refs_4_.own_ref), channel_id=1, source_target_pairs={{0,16},{4,20},{8,24},{12,28},{16,0},{20,4},{24,8},{28,12},{1,17},{... | collective-permute-start | bytes 196616 | tf_op jit(solution)/shard_map/ppermute | solution.py:531
  29.1 0.5 collective-permute-start
  29.6 2.8 %collective-permute-start.9 = (bf16[128,256]{1,0:T(8,128)(2,1)S(1)}, bf16[128,256]{1,0:T(8,128)(2,1)S(1)}, u32[]{:S(2)}, u32[]{:S(2)}) collective-permute-start(bf16[128,256]{1,0:T(8,128)(2,1)S(1)} %get-tuple-element.49.refs_4_), channel_id=1, source_target_pairs={{0,3},{1,2},{2,1},{3,0},{4,7},{5,6},{6,5},{7,4},{8,11},{9,10},{10,... | collective-permute-start | bytes 196616 | tf_op jit(solution)/shard_map/ppermute | solution.py:531
  32.4 1.1 %collective-permute-start.8 = (bf16[128,256]{1,0:T(8,128)(2,1)S(1)}, bf16[128,256]{1,0:T(8,128)(2,1)S(1)}, u32[]{:S(2)}, u32[]{:S(2)}) collective-permute-start(bf16[128,256]{1,0:T(8,128)(2,1)S(1)} %get-tuple-element.49.refs_4_), channel_id=1, source_target_pairs={{0,2},{1,3},{2,0},{3,1},{4,6},{5,7},{6,4},{7,5},{8,10},{9,11},{10,... | collective-permute-start | bytes 196616 | tf_op jit(solution)/shard_map/ppermute | solution.py:531
  33.5 0.9 %collective-permute-start.7 = (bf16[128,256]{1,0:T(8,128)(2,1)S(1)}, bf16[128,256]{1,0:T(8,128)(2,1)S(1)}, u32[]{:S(2)}, u32[]{:S(2)}) collective-permute-start(bf16[128,256]{1,0:T(8,128)(2,1)S(1)} %get-tuple-element.49.refs_4_), channel_id=1, source_target_pairs={{0,1},{1,0},{2,3},{3,2},{4,5},{5,4},{6,7},{7,6},{8,9},{9,8},{10,11... | collective-permute-start | bytes 196616 | tf_op jit(solution)/shard_map/ppermute | solution.py:531
  34.5 2.0 %collective-permute-done.9.refs_7_ = bf16[128,256]{1,0:T(8,128)(2,1)S(1)} collective-permute-done((bf16[128,256]{1,0:T(8,128)(2,1)S(1)}, bf16[128,256]{1,0:T(8,128)(2,1)S(1)}, u32[]{:S(2)}, u32[]{:S(2)}) %collective-permute-start.9) | collective-permute-done | bytes 65568 | tf_op jit(solution)/shard_map/ppermute | solution.py:531
  36.5 2.9 %collective-permute-done.8.refs_6_ = bf16[128,256]{1,0:T(8,128)(2,1)S(1)} collective-permute-done((bf16[128,256]{1,0:T(8,128)(2,1)S(1)}, bf16[128,256]{1,0:T(8,128)(2,1)S(1)}, u32[]{:S(2)}, u32[]{:S(2)}) %collective-permute-start.8) | collective-permute-done | bytes 65568 | tf_op jit(solution)/shard_map/ppermute | solution.py:531
  39.4 0.7 item_sums.2
  40.2 1.2 %user_sums.2 = (bf16[256,128]{1,0:T(8,128)(2,1)S(1)}, bf16[256,128]{1,0:T(8,128)(2,1)S(1)}, bf16[256,128]{1,0:T(8,128)(2,1)S(1)}, bf16[256,128]{1,0:T(8,128)(2,1)S(1)}) custom-call(bf16[256,2048]{1,0:T(8,128)(2,1)S(1)} %get-tuple-element.39.refs_0_, bf16[256,2048]{1,0:T(8,128)(2,1)S(1)} %get-tuple-element.40.refs_1_, ...), custom_call_target="tpu_custom_call" | custom-call | flops 536870912 | bytes 4194304 | tf_op jit(solution)/shard_map/user_sums/pallas_call | solution.py:402
  41.5 0.1 collective-permute-start.4
  41.6 1.8 %collective-permute-start.5 = (bf16[256,128]{1,0:T(8,128)(2,1)S(1)}, bf16[256,128]{1,0:T(8,128)(2,1)S(1)}, u32[]{:S(2)}, u32[]{:S(2)}) collective-permute-start(bf16[256,128]{1,0:T(8,128)(2,1)S(1)} %get-tuple-element.46), channel_id=1, source_target_pairs={{0,2},{1,3},{2,0},{3,1},{4,6},{5,7},{6,4},{7,5},{8,10},{9,11},{10,... | collective-permute-start | bytes 196616 | tf_op jit(solution)/shard_map/ppermute | solution.py:531
  43.3 2.6 %collective-permute-start.6 = (bf16[256,128]{1,0:T(8,128)(2,1)S(1)}, bf16[256,128]{1,0:T(8,128)(2,1)S(1)}, u32[]{:S(2)}, u32[]{:S(2)}) collective-permute-start(bf16[256,128]{1,0:T(8,128)(2,1)S(1)} %get-tuple-element.47), channel_id=1, source_target_pairs={{0,3},{1,2},{2,1},{3,0},{4,7},{5,6},{6,5},{7,4},{8,11},{9,10},{10,... | collective-permute-start | bytes 196616 | tf_op jit(solution)/shard_map/ppermute | solution.py:531
  46.0 1.1 %collective-permute-start.11 = (bf16[128,256]{1,0:T(8,128)(2,1)S(1)}, bf16[128,256]{1,0:T(8,128)(2,1)S(1)}, u32[]{:S(2)}, u32[]{:S(2)}) collective-permute-start(bf16[128,256]{1,0:T(8,128)(2,1)S(1)} %get-tuple-element.53), channel_id=1, source_target_pairs={{0,8},{4,12},{8,0},{12,4},{16,24},{20,28},{24,16},{28,20},{1,9},{5... | collective-permute-start | bytes 196616 | tf_op jit(solution)/shard_map/ppermute | solution.py:531
  47.1 0.8 %collective-permute-start.12 = (bf16[128,256]{1,0:T(8,128)(2,1)S(1)}, bf16[128,256]{1,0:T(8,128)(2,1)S(1)}, u32[]{:S(2)}, u32[]{:S(2)}) collective-permute-start(bf16[128,256]{1,0:T(8,128)(2,1)S(1)} %get-tuple-element.54), channel_id=1, source_target_pairs={{0,16},{4,20},{8,24},{12,28},{16,0},{20,4},{24,8},{28,12},{1,17},{... | collective-permute-start | bytes 196616 | tf_op jit(solution)/shard_map/ppermute | solution.py:531
  47.9 1.6 %collective-permute-start.13 = (bf16[128,256]{1,0:T(8,128)(2,1)S(1)}, bf16[128,256]{1,0:T(8,128)(2,1)S(1)}, u32[]{:S(2)}, u32[]{:S(2)}) collective-permute-start(bf16[128,256]{1,0:T(8,128)(2,1)S(1)} %get-tuple-element.55), channel_id=1, source_target_pairs={{0,24},{4,28},{8,16},{12,20},{16,8},{20,12},{24,0},{28,4},{1,25},{... | collective-permute-start | bytes 196616 | tf_op jit(solution)/shard_map/ppermute | solution.py:531
  49.5 0.8 collective-permute-done.5.refs_2_
  50.3 0.3 user_update.2
  50.6 1.8 %collective-permute-start.23 = (bf16[128,256]{1,0:T(8,128)(2,1)S(1)}, bf16[128,256]{1,0:T(8,128)(2,1)S(1)}, u32[]{:S(2)}, u32[]{:S(2)}) collective-permute-start(bf16[128,256]{1,0:T(8,128)(2,1)S(1)} %get-tuple-element.61.refs_4_), channel_id=1, source_target_pairs={{0,3},{1,2},{2,1},{3,0},{4,7},{5,6},{6,5},{7,4},{8,11},{9,10},{10,... | collective-permute-start | bytes 196616 | tf_op jit(solution)/shard_map/ppermute | solution.py:531
  52.3 1.2 %collective-permute-start.22 = (bf16[128,256]{1,0:T(8,128)(2,1)S(1)}, bf16[128,256]{1,0:T(8,128)(2,1)S(1)}, u32[]{:S(2)}, u32[]{:S(2)}) collective-permute-start(bf16[128,256]{1,0:T(8,128)(2,1)S(1)} %get-tuple-element.61.refs_4_), channel_id=1, source_target_pairs={{0,2},{1,3},{2,0},{3,1},{4,6},{5,7},{6,4},{7,5},{8,10},{9,11},{10,... | collective-permute-start | bytes 196616 | tf_op jit(solution)/shard_map/ppermute | solution.py:531
  53.6 1.5 %collective-permute-start.21 = (bf16[128,256]{1,0:T(8,128)(2,1)S(1)}, bf16[128,256]{1,0:T(8,128)(2,1)S(1)}, u32[]{:S(2)}, u32[]{:S(2)}) collective-permute-start(bf16[128,256]{1,0:T(8,128)(2,1)S(1)} %get-tuple-element.61.refs_4_), channel_id=1, source_target_pairs={{0,1},{1,0},{2,3},{3,2},{4,5},{5,4},{6,7},{7,6},{8,9},{9,8},{10,11... | collective-permute-start | bytes 196616 | tf_op jit(solution)/shard_map/ppermute | solution.py:531
  55.0 0.3 item_update.2.refs_0_.refs_4_.own_ref
  55.3 1.4 %collective-permute-start.16 = (bf16[256,128]{1,0:T(8,128)(2,1)S(1)}, bf16[256,128]{1,0:T(8,128)(2,1)S(1)}, u32[]{:S(2)}, u32[]{:S(2)}) collective-permute-start(bf16[256,128]{1,0:T(8,128)(2,1)S(1)} %item_update.2.refs_0_.refs_4_.own_ref), channel_id=1, source_target_pairs={{0,24},{4,28},{8,16},{12,20},{16,8},{20,12},{24,0},{28,4},{1,25},{... | collective-permute-start | bytes 196616 | tf_op jit(solution)/shard_map/ppermute | solution.py:531
  56.7 1.2 %collective-permute-start.15 = (bf16[256,128]{1,0:T(8,128)(2,1)S(1)}, bf16[256,128]{1,0:T(8,128)(2,1)S(1)}, u32[]{:S(2)}, u32[]{:S(2)}) collective-permute-start(bf16[256,128]{1,0:T(8,128)(2,1)S(1)} %item_update.2.refs_0_.refs_4_.own_ref), channel_id=1, source_target_pairs={{0,16},{4,20},{8,24},{12,28},{16,0},{20,4},{24,8},{28,12},{1,17},{... | collective-permute-start | bytes 196616 | tf_op jit(solution)/shard_map/ppermute | solution.py:531
  57.9 1.0 %collective-permute-start.14 = (bf16[256,128]{1,0:T(8,128)(2,1)S(1)}, bf16[256,128]{1,0:T(8,128)(2,1)S(1)}, u32[]{:S(2)}, u32[]{:S(2)}) collective-permute-start(bf16[256,128]{1,0:T(8,128)(2,1)S(1)} %item_update.2.refs_0_.refs_4_.own_ref), channel_id=1, source_target_pairs={{0,8},{4,12},{8,0},{12,4},{16,24},{20,28},{24,16},{28,20},{1,9},{5... | collective-permute-start | bytes 196616 | tf_op jit(solution)/shard_map/ppermute | solution.py:531
  58.9 0.5 collective-permute-done.22.refs_6_
  59.4 0.7 item_sums.3
  60.1 0.1 collective-permute-start.24
  60.2 0.4 collective-permute-done.16.refs_3_.refs_7_
  60.6 0.7 collective-permute-done.15.refs_2_.refs_6_
  61.2 0.9 %collective-permute-done.14.refs_1_.refs_5_ = bf16[256,128]{1,0:T(8,128)(2,1)S(1)} collective-permute-done((bf16[256,128]{1,0:T(8,128)(2,1)S(1)}, bf16[256,128]{1,0:T(8,128)(2,1)S(1)}, u32[]{:S(2)}, u32[]{:S(2)}) %collective-permute-start.14) | collective-permute-done | bytes 65568 | tf_op jit(solution)/shard_map/ppermute | solution.py:531
  62.3 1.1 %collective-permute-start.25 = (bf16[128,256]{1,0:T(8,128)(2,1)S(1)}, bf16[128,256]{1,0:T(8,128)(2,1)S(1)}, u32[]{:S(2)}, u32[]{:S(2)}) collective-permute-start(bf16[128,256]{1,0:T(8,128)(2,1)S(1)} %get-tuple-element.65), channel_id=1, source_target_pairs={{0,8},{4,12},{8,0},{12,4},{16,24},{20,28},{24,16},{28,20},{1,9},{5... | collective-permute-start | bytes 196616 | tf_op jit(solution)/shard_map/ppermute | solution.py:531
  63.4 1.1 %collective-permute-start.26 = (bf16[128,256]{1,0:T(8,128)(2,1)S(1)}, bf16[128,256]{1,0:T(8,128)(2,1)S(1)}, u32[]{:S(2)}, u32[]{:S(2)}) collective-permute-start(bf16[128,256]{1,0:T(8,128)(2,1)S(1)} %get-tuple-element.66), channel_id=1, source_target_pairs={{0,16},{4,20},{8,24},{12,28},{16,0},{20,4},{24,8},{28,12},{1,17},{... | collective-permute-start | bytes 196616 | tf_op jit(solution)/shard_map/ppermute | solution.py:531
  64.5 1.4 %collective-permute-start.27 = (bf16[128,256]{1,0:T(8,128)(2,1)S(1)}, bf16[128,256]{1,0:T(8,128)(2,1)S(1)}, u32[]{:S(2)}, u32[]{:S(2)}) collective-permute-start(bf16[128,256]{1,0:T(8,128)(2,1)S(1)} %get-tuple-element.67), channel_id=1, source_target_pairs={{0,24},{4,28},{8,16},{12,20},{16,8},{20,12},{24,0},{28,4},{1,25},{... | collective-permute-start | bytes 196616 | tf_op jit(solution)/shard_map/ppermute | solution.py:531
  65.9 1.2 %user_sums.3 = (bf16[256,128]{1,0:T(8,128)(2,1)S(1)}, bf16[256,128]{1,0:T(8,128)(2,1)S(1)}, bf16[256,128]{1,0:T(8,128)(2,1)S(1)}, bf16[256,128]{1,0:T(8,128)(2,1)S(1)}) custom-call(bf16[256,2048]{1,0:T(8,128)(2,1)S(1)} %get-tuple-element.39.refs_0_, bf16[256,2048]{1,0:T(8,128)(2,1)S(1)} %get-tuple-element.40.refs_1_, ...), custom_call_target="tpu_custom_call" | custom-call | flops 536870912 | bytes 4194304 | tf_op jit(solution)/shard_map/user_sums/pallas_call | solution.py:402
  67.1 1.3 %collective-permute-start.18 = (bf16[256,128]{1,0:T(8,128)(2,1)S(1)}, bf16[256,128]{1,0:T(8,128)(2,1)S(1)}, u32[]{:S(2)}, u32[]{:S(2)}) collective-permute-start(bf16[256,128]{1,0:T(8,128)(2,1)S(1)} %get-tuple-element.57), channel_id=1, source_target_pairs={{0,1},{1,0},{2,3},{3,2},{4,5},{5,4},{6,7},{7,6},{8,9},{9,8},{10,11... | collective-permute-start | bytes 196616 | tf_op jit(solution)/shard_map/ppermute | solution.py:531
  68.4 1.2 %collective-permute-start.19 = (bf16[256,128]{1,0:T(8,128)(2,1)S(1)}, bf16[256,128]{1,0:T(8,128)(2,1)S(1)}, u32[]{:S(2)}, u32[]{:S(2)}) collective-permute-start(bf16[256,128]{1,0:T(8,128)(2,1)S(1)} %get-tuple-element.58), channel_id=1, source_target_pairs={{0,2},{1,3},{2,0},{3,1},{4,6},{5,7},{6,4},{7,5},{8,10},{9,11},{10,... | collective-permute-start | bytes 196616 | tf_op jit(solution)/shard_map/ppermute | solution.py:531
  69.7 1.9 %collective-permute-start.20 = (bf16[256,128]{1,0:T(8,128)(2,1)S(1)}, bf16[256,128]{1,0:T(8,128)(2,1)S(1)}, u32[]{:S(2)}, u32[]{:S(2)}) collective-permute-start(bf16[256,128]{1,0:T(8,128)(2,1)S(1)} %get-tuple-element.59), channel_id=1, source_target_pairs={{0,3},{1,2},{2,1},{3,0},{4,7},{5,6},{6,5},{7,4},{8,11},{9,10},{10,... | collective-permute-start | bytes 196616 | tf_op jit(solution)/shard_map/ppermute | solution.py:531
  71.6 0.9 %item_update.3 = bf16[256,128]{1,0:T(8,128)(2,1)} custom-call(bf16[256,128]{1,0:T(8,128)(2,1)S(1)} %item_update.2.refs_0_.refs_4_.own_ref, bf16[2,128,128]{2,1,0:T(8,128)(2,1)S(1)} %copy-done, bf16[2,128,128]{2,1,0:T(8,128)(2,1)S(1)} %copy-done.1, bf16[128,256]{1,0:T(8,128)(2,1)S(1)} %get-tuple-element.64.refs_0_, ...), custom_call_target="tpu_custom_call" | custom-call | tf_op jit(solution)/shard_map/item_update/pallas_call | solution.py:515
  72.5 3.8 %collective-permute-done.19.refs_2_ = bf16[256,128]{1,0:T(8,128)(2,1)S(1)} collective-permute-done((bf16[256,128]{1,0:T(8,128)(2,1)S(1)}, bf16[256,128]{1,0:T(8,128)(2,1)S(1)}, u32[]{:S(2)}, u32[]{:S(2)}) %collective-permute-start.19) | collective-permute-done | bytes 65568 | tf_op jit(solution)/shard_map/ppermute | solution.py:531
  76.2 0.9 %user_update.3 = (bf16[256,128]{1,0:T(8,128)(2,1)}, bf16[128,256]{1,0:T(8,128)(2,1)}) custom-call(bf16[256,128]{1,0:T(8,128)(2,1)S(1)} %get-tuple-element.48.own_ref, bf16[2,128,128]{2,1,0:T(8,128)(2,1)S(1)} %copy-done, bf16[2,128,128]{2,1,0:T(8,128)(2,1)S(1)} %copy-done.1, bf16[256,128]{1,0:T(8,128)(2,1)S(1)} %get-tuple-element.56.refs_0_, ...), custom_call_target="tpu_custom_call" | custom-call | tf_op jit(solution)/shard_map/user_update/pallas_call | solution.py:495
  (37 shorter events, 0.4 us)
Async XLA Ops:
  3.9 20.3 %copy-start.2 = (bf16[64,128]{1,0:T(8,128)(2,1)S(1)}, bf16[64,128]{1,0:T(8,128)(2,1)}, u32[]{:S(2)}) copy-start(bf16[64,128]{1,0:T(8,128)(2,1)} %proj_wide_ref.1) | copy-start | bytes 49156
  3.9 20.3 %copy-start.3 = (bf16[32,128]{1,0:T(8,128)(2,1)S(1)}, bf16[32,128]{1,0:T(8,128)(2,1)}, u32[]{:S(2)}) copy-start(bf16[32,128]{1,0:T(8,128)(2,1)} %proj_narrow_ref.1) | copy-start | bytes 24580
  3.9 20.3 %all-to-all-start = ((bf16[32,56,128]{2,1,0:T(8,128)(2,1)}), bf16[32,56,128]{2,1,0:T(8,128)(2,1)S(1)}, u32[]{:S(2)}, u32[]{:S(2)}) async-start(bf16[32,56,128]{2,1,0:T(8,128)(2,1)} %dispatch.1), calls=%async_computation | async-start | bytes 917504 | tf_op jit(solution)/shard_map/all_to_all | solution.py:577
  11.2 0.7 copy-start.4
  11.9 0.7 copy-start.5
  26.1 7.4 %collective-permute-start.2 = (bf16[256,128]{1,0:T(8,128)(2,1)S(1)}, bf16[256,128]{1,0:T(8,128)(2,1)S(1)}, u32[]{:S(2)}, u32[]{:S(2)}) collective-permute-start(bf16[256,128]{1,0:T(8,128)(2,1)S(1)} %get-tuple-element.43.refs_0_.refs_4_.own_ref), channel_id=1, source_target_pairs={{0,24},{4,28},{8,16},{12,20},{16,8},{20,12},{24,0},{28,4},{1,25},{... | collective-permute-start | bytes 196616 | tf_op jit(solution)/shard_map/ppermute | solution.py:531
  28.3 6.2 %collective-permute-start.1 = (bf16[256,128]{1,0:T(8,128)(2,1)S(1)}, bf16[256,128]{1,0:T(8,128)(2,1)S(1)}, u32[]{:S(2)}, u32[]{:S(2)}) collective-permute-start(bf16[256,128]{1,0:T(8,128)(2,1)S(1)} %get-tuple-element.43.refs_0_.refs_4_.own_ref), channel_id=1, source_target_pairs={{0,16},{4,20},{8,24},{12,28},{16,0},{20,4},{24,8},{28,12},{1,17},{... | collective-permute-start | bytes 196616 | tf_op jit(solution)/shard_map/ppermute | solution.py:531
  29.1 5.3 %collective-permute-start = (bf16[256,128]{1,0:T(8,128)(2,1)S(1)}, bf16[256,128]{1,0:T(8,128)(2,1)S(1)}, u32[]{:S(2)}, u32[]{:S(2)}) collective-permute-start(bf16[256,128]{1,0:T(8,128)(2,1)S(1)} %get-tuple-element.43.refs_0_.refs_4_.own_ref), channel_id=1, source_target_pairs={{0,8},{4,12},{8,0},{12,4},{16,24},{20,28},{24,16},{28,20},{1,9},{5... | collective-permute-start | bytes 196616 | tf_op jit(solution)/shard_map/ppermute | solution.py:531
  29.6 6.9 %collective-permute-start.9 = (bf16[128,256]{1,0:T(8,128)(2,1)S(1)}, bf16[128,256]{1,0:T(8,128)(2,1)S(1)}, u32[]{:S(2)}, u32[]{:S(2)}) collective-permute-start(bf16[128,256]{1,0:T(8,128)(2,1)S(1)} %get-tuple-element.49.refs_4_), channel_id=1, source_target_pairs={{0,3},{1,2},{2,1},{3,0},{4,7},{5,6},{6,5},{7,4},{8,11},{9,10},{10,... | collective-permute-start | bytes 196616 | tf_op jit(solution)/shard_map/ppermute | solution.py:531
  32.4 6.9 %collective-permute-start.8 = (bf16[128,256]{1,0:T(8,128)(2,1)S(1)}, bf16[128,256]{1,0:T(8,128)(2,1)S(1)}, u32[]{:S(2)}, u32[]{:S(2)}) collective-permute-start(bf16[128,256]{1,0:T(8,128)(2,1)S(1)} %get-tuple-element.49.refs_4_), channel_id=1, source_target_pairs={{0,2},{1,3},{2,0},{3,1},{4,6},{5,7},{6,4},{7,5},{8,10},{9,11},{10,... | collective-permute-start | bytes 196616 | tf_op jit(solution)/shard_map/ppermute | solution.py:531
  33.5 5.9 %collective-permute-start.7 = (bf16[128,256]{1,0:T(8,128)(2,1)S(1)}, bf16[128,256]{1,0:T(8,128)(2,1)S(1)}, u32[]{:S(2)}, u32[]{:S(2)}) collective-permute-start(bf16[128,256]{1,0:T(8,128)(2,1)S(1)} %get-tuple-element.49.refs_4_), channel_id=1, source_target_pairs={{0,1},{1,0},{2,3},{3,2},{4,5},{5,4},{6,7},{7,6},{8,9},{9,8},{10,11... | collective-permute-start | bytes 196616 | tf_op jit(solution)/shard_map/ppermute | solution.py:531
  34.5 5.8 %collective-permute-start.3 = (bf16[4,256,128]{2,1,0:T(8,128)(2,1)S(1)}, bf16[4,256,128]{2,1,0:T(8,128)(2,1)S(1)}, u32[]{:S(2)}, u32[]{:S(2)}) collective-permute-start(bf16[4,256,128]{2,1,0:T(8,128)(2,1)S(1)} %merge.2), channel_id=1, source_target_pairs={{0,4},{4,0},{8,12},{12,8},{16,20},{20,16},{24,28},{28,24},{1,5},{5... | collective-permute-start | bytes 786440 | tf_op jit(solution)/shard_map/ppermute | solution.py:536
  39.4 10.9 %copy-start = (bf16[2,128,128]{2,1,0:T(8,128)(2,1)S(1)}, bf16[2,128,128]{2,1,0:T(8,128)(2,1)}, u32[]{:S(2)}) copy-start(bf16[2,128,128]{2,1,0:T(8,128)(2,1)} %sum_ref.7) | copy-start | bytes 196612
  39.4 10.9 %copy-start.1 = (bf16[2,128,128]{2,1,0:T(8,128)(2,1)S(1)}, bf16[2,128,128]{2,1,0:T(8,128)(2,1)}, u32[]{:S(2)}) copy-start(bf16[2,128,128]{2,1,0:T(8,128)(2,1)} %product_ref.7) | copy-start | bytes 196612
  40.1 5.8 %collective-permute-start.10 = (bf16[4,128,256]{2,1,0:T(8,128)(2,1)S(1)}, bf16[4,128,256]{2,1,0:T(8,128)(2,1)S(1)}, u32[]{:S(2)}, u32[]{:S(2)}) collective-permute-start(bf16[4,128,256]{2,1,0:T(8,128)(2,1)S(1)} %get-tuple-element.51), channel_id=1, source_target_pairs={{0,4},{4,0},{8,12},{12,8},{16,20},{20,16},{24,28},{28,24},{1,5},{5... | collective-permute-start | bytes 786440 | tf_op jit(solution)/shard_map/ppermute | solution.py:536
  41.5 6.4 %collective-permute-start.4 = (bf16[256,128]{1,0:T(8,128)(2,1)S(1)}, bf16[256,128]{1,0:T(8,128)(2,1)S(1)}, u32[]{:S(2)}, u32[]{:S(2)}) collective-permute-start(bf16[256,128]{1,0:T(8,128)(2,1)S(1)} %get-tuple-element.45), channel_id=1, source_target_pairs={{0,1},{1,0},{2,3},{3,2},{4,5},{5,4},{6,7},{7,6},{8,9},{9,8},{10,11... | collective-permute-start | bytes 196616 | tf_op jit(solution)/shard_map/ppermute | solution.py:531
  41.6 8.7 %collective-permute-start.5 = (bf16[256,128]{1,0:T(8,128)(2,1)S(1)}, bf16[256,128]{1,0:T(8,128)(2,1)S(1)}, u32[]{:S(2)}, u32[]{:S(2)}) collective-permute-start(bf16[256,128]{1,0:T(8,128)(2,1)S(1)} %get-tuple-element.46), channel_id=1, source_target_pairs={{0,2},{1,3},{2,0},{3,1},{4,6},{5,7},{6,4},{7,5},{8,10},{9,11},{10,... | collective-permute-start | bytes 196616 | tf_op jit(solution)/shard_map/ppermute | solution.py:531
  43.3 7.0 %collective-permute-start.6 = (bf16[256,128]{1,0:T(8,128)(2,1)S(1)}, bf16[256,128]{1,0:T(8,128)(2,1)S(1)}, u32[]{:S(2)}, u32[]{:S(2)}) collective-permute-start(bf16[256,128]{1,0:T(8,128)(2,1)S(1)} %get-tuple-element.47), channel_id=1, source_target_pairs={{0,3},{1,2},{2,1},{3,0},{4,7},{5,6},{6,5},{7,4},{8,11},{9,10},{10,... | collective-permute-start | bytes 196616 | tf_op jit(solution)/shard_map/ppermute | solution.py:531
  46.0 7.6 %collective-permute-start.11 = (bf16[128,256]{1,0:T(8,128)(2,1)S(1)}, bf16[128,256]{1,0:T(8,128)(2,1)S(1)}, u32[]{:S(2)}, u32[]{:S(2)}) collective-permute-start(bf16[128,256]{1,0:T(8,128)(2,1)S(1)} %get-tuple-element.53), channel_id=1, source_target_pairs={{0,8},{4,12},{8,0},{12,4},{16,24},{20,28},{24,16},{28,20},{1,9},{5... | collective-permute-start | bytes 196616 | tf_op jit(solution)/shard_map/ppermute | solution.py:531
  47.1 8.0 %collective-permute-start.12 = (bf16[128,256]{1,0:T(8,128)(2,1)S(1)}, bf16[128,256]{1,0:T(8,128)(2,1)S(1)}, u32[]{:S(2)}, u32[]{:S(2)}) collective-permute-start(bf16[128,256]{1,0:T(8,128)(2,1)S(1)} %get-tuple-element.54), channel_id=1, source_target_pairs={{0,16},{4,20},{8,24},{12,28},{16,0},{20,4},{24,8},{28,12},{1,17},{... | collective-permute-start | bytes 196616 | tf_op jit(solution)/shard_map/ppermute | solution.py:531
  47.9 7.1 %collective-permute-start.13 = (bf16[128,256]{1,0:T(8,128)(2,1)S(1)}, bf16[128,256]{1,0:T(8,128)(2,1)S(1)}, u32[]{:S(2)}, u32[]{:S(2)}) collective-permute-start(bf16[128,256]{1,0:T(8,128)(2,1)S(1)} %get-tuple-element.55), channel_id=1, source_target_pairs={{0,24},{4,28},{8,16},{12,20},{16,8},{20,12},{24,0},{28,4},{1,25},{... | collective-permute-start | bytes 196616 | tf_op jit(solution)/shard_map/ppermute | solution.py:531
  50.6 7.3 %collective-permute-start.23 = (bf16[128,256]{1,0:T(8,128)(2,1)S(1)}, bf16[128,256]{1,0:T(8,128)(2,1)S(1)}, u32[]{:S(2)}, u32[]{:S(2)}) collective-permute-start(bf16[128,256]{1,0:T(8,128)(2,1)S(1)} %get-tuple-element.61.refs_4_), channel_id=1, source_target_pairs={{0,3},{1,2},{2,1},{3,0},{4,7},{5,6},{6,5},{7,4},{8,11},{9,10},{10,... | collective-permute-start | bytes 196616 | tf_op jit(solution)/shard_map/ppermute | solution.py:531
  52.3 7.1 %collective-permute-start.22 = (bf16[128,256]{1,0:T(8,128)(2,1)S(1)}, bf16[128,256]{1,0:T(8,128)(2,1)S(1)}, u32[]{:S(2)}, u32[]{:S(2)}) collective-permute-start(bf16[128,256]{1,0:T(8,128)(2,1)S(1)} %get-tuple-element.61.refs_4_), channel_id=1, source_target_pairs={{0,2},{1,3},{2,0},{3,1},{4,6},{5,7},{6,4},{7,5},{8,10},{9,11},{10,... | collective-permute-start | bytes 196616 | tf_op jit(solution)/shard_map/ppermute | solution.py:531
  53.6 5.8 %collective-permute-start.21 = (bf16[128,256]{1,0:T(8,128)(2,1)S(1)}, bf16[128,256]{1,0:T(8,128)(2,1)S(1)}, u32[]{:S(2)}, u32[]{:S(2)}) collective-permute-start(bf16[128,256]{1,0:T(8,128)(2,1)S(1)} %get-tuple-element.61.refs_4_), channel_id=1, source_target_pairs={{0,1},{1,0},{2,3},{3,2},{4,5},{5,4},{6,7},{7,6},{8,9},{9,8},{10,11... | collective-permute-start | bytes 196616 | tf_op jit(solution)/shard_map/ppermute | solution.py:531
  55.3 5.3 %collective-permute-start.16 = (bf16[256,128]{1,0:T(8,128)(2,1)S(1)}, bf16[256,128]{1,0:T(8,128)(2,1)S(1)}, u32[]{:S(2)}, u32[]{:S(2)}) collective-permute-start(bf16[256,128]{1,0:T(8,128)(2,1)S(1)} %item_update.2.refs_0_.refs_4_.own_ref), channel_id=1, source_target_pairs={{0,24},{4,28},{8,16},{12,20},{16,8},{20,12},{24,0},{28,4},{1,25},{... | collective-permute-start | bytes 196616 | tf_op jit(solution)/shard_map/ppermute | solution.py:531
  56.7 4.6 %collective-permute-start.15 = (bf16[256,128]{1,0:T(8,128)(2,1)S(1)}, bf16[256,128]{1,0:T(8,128)(2,1)S(1)}, u32[]{:S(2)}, u32[]{:S(2)}) collective-permute-start(bf16[256,128]{1,0:T(8,128)(2,1)S(1)} %item_update.2.refs_0_.refs_4_.own_ref), channel_id=1, source_target_pairs={{0,16},{4,20},{8,24},{12,28},{16,0},{20,4},{24,8},{28,12},{1,17},{... | collective-permute-start | bytes 196616 | tf_op jit(solution)/shard_map/ppermute | solution.py:531
  57.9 4.3 %collective-permute-start.14 = (bf16[256,128]{1,0:T(8,128)(2,1)S(1)}, bf16[256,128]{1,0:T(8,128)(2,1)S(1)}, u32[]{:S(2)}, u32[]{:S(2)}) collective-permute-start(bf16[256,128]{1,0:T(8,128)(2,1)S(1)} %item_update.2.refs_0_.refs_4_.own_ref), channel_id=1, source_target_pairs={{0,8},{4,12},{8,0},{12,4},{16,24},{20,28},{24,16},{28,20},{1,9},{5... | collective-permute-start | bytes 196616 | tf_op jit(solution)/shard_map/ppermute | solution.py:531
  60.1 2.1 %collective-permute-start.24 = (bf16[4,128,256]{2,1,0:T(8,128)(2,1)S(1)}, bf16[4,128,256]{2,1,0:T(8,128)(2,1)S(1)}, u32[]{:S(2)}, u32[]{:S(2)}) collective-permute-start(bf16[4,128,256]{2,1,0:T(8,128)(2,1)S(1)} %get-tuple-element.63), channel_id=1, source_target_pairs={{0,4},{4,0},{8,12},{12,8},{16,20},{20,16},{24,28},{28,24},{1,5},{5... | collective-permute-start | bytes 786440 | tf_op jit(solution)/shard_map/ppermute | solution.py:536
  62.2 3.7 %collective-permute-start.17 = (bf16[4,256,128]{2,1,0:T(8,128)(2,1)S(1)}, bf16[4,256,128]{2,1,0:T(8,128)(2,1)S(1)}, u32[]{:S(2)}, u32[]{:S(2)}) collective-permute-start(bf16[4,256,128]{2,1,0:T(8,128)(2,1)S(1)} %merge.3), channel_id=1, source_target_pairs={{0,4},{4,0},{8,12},{12,8},{16,20},{20,16},{24,28},{28,24},{1,5},{5... | collective-permute-start | bytes 786440 | tf_op jit(solution)/shard_map/ppermute | solution.py:536
  62.3 7.4 %collective-permute-start.25 = (bf16[128,256]{1,0:T(8,128)(2,1)S(1)}, bf16[128,256]{1,0:T(8,128)(2,1)S(1)}, u32[]{:S(2)}, u32[]{:S(2)}) collective-permute-start(bf16[128,256]{1,0:T(8,128)(2,1)S(1)} %get-tuple-element.65), channel_id=1, source_target_pairs={{0,8},{4,12},{8,0},{12,4},{16,24},{20,28},{24,16},{28,20},{1,9},{5... | collective-permute-start | bytes 196616 | tf_op jit(solution)/shard_map/ppermute | solution.py:531
  63.4 8.2 %collective-permute-start.26 = (bf16[128,256]{1,0:T(8,128)(2,1)S(1)}, bf16[128,256]{1,0:T(8,128)(2,1)S(1)}, u32[]{:S(2)}, u32[]{:S(2)}) collective-permute-start(bf16[128,256]{1,0:T(8,128)(2,1)S(1)} %get-tuple-element.66), channel_id=1, source_target_pairs={{0,16},{4,20},{8,24},{12,28},{16,0},{20,4},{24,8},{28,12},{1,17},{... | collective-permute-start | bytes 196616 | tf_op jit(solution)/shard_map/ppermute | solution.py:531
  64.5 7.1 %collective-permute-start.27 = (bf16[128,256]{1,0:T(8,128)(2,1)S(1)}, bf16[128,256]{1,0:T(8,128)(2,1)S(1)}, u32[]{:S(2)}, u32[]{:S(2)}) collective-permute-start(bf16[128,256]{1,0:T(8,128)(2,1)S(1)} %get-tuple-element.67), channel_id=1, source_target_pairs={{0,24},{4,28},{8,16},{12,20},{16,8},{20,12},{24,0},{28,4},{1,25},{... | collective-permute-start | bytes 196616 | tf_op jit(solution)/shard_map/ppermute | solution.py:531
  67.1 5.4 %collective-permute-start.18 = (bf16[256,128]{1,0:T(8,128)(2,1)S(1)}, bf16[256,128]{1,0:T(8,128)(2,1)S(1)}, u32[]{:S(2)}, u32[]{:S(2)}) collective-permute-start(bf16[256,128]{1,0:T(8,128)(2,1)S(1)} %get-tuple-element.57), channel_id=1, source_target_pairs={{0,1},{1,0},{2,3},{3,2},{4,5},{5,4},{6,7},{7,6},{8,9},{9,8},{10,11... | collective-permute-start | bytes 196616 | tf_op jit(solution)/shard_map/ppermute | solution.py:531
  68.4 7.8 %collective-permute-start.19 = (bf16[256,128]{1,0:T(8,128)(2,1)S(1)}, bf16[256,128]{1,0:T(8,128)(2,1)S(1)}, u32[]{:S(2)}, u32[]{:S(2)}) collective-permute-start(bf16[256,128]{1,0:T(8,128)(2,1)S(1)} %get-tuple-element.58), channel_id=1, source_target_pairs={{0,2},{1,3},{2,0},{3,1},{4,6},{5,7},{6,4},{7,5},{8,10},{9,11},{10,... | collective-permute-start | bytes 196616 | tf_op jit(solution)/shard_map/ppermute | solution.py:531
  69.7 6.6 %collective-permute-start.20 = (bf16[256,128]{1,0:T(8,128)(2,1)S(1)}, bf16[256,128]{1,0:T(8,128)(2,1)S(1)}, u32[]{:S(2)}, u32[]{:S(2)}) collective-permute-start(bf16[256,128]{1,0:T(8,128)(2,1)S(1)} %get-tuple-element.59), channel_id=1, source_target_pairs={{0,3},{1,2},{2,1},{3,0},{4,7},{5,6},{6,5},{7,4},{8,11},{9,10},{10,... | collective-permute-start | bytes 196616 | tf_op jit(solution)/shard_map/ppermute | solution.py:531

commit v6 on v5

--- a/solution.py
+++ b/solution.py
@@ -11,7 +11,7 @@
 TILE = 128
 LANES = 128
 CODE_ROWS = 8
-GROUP = 8
+GROUP = 4
 KEPT = 1
 F32 = jnp.float32
 BF16 = jnp.bfloat16
@@ -372,11 +372,16 @@
     return [k if power_of_two(n) else (n - k) % n for k in range(n)]
 
 
-def user_sum_kernel(cols, *refs):
-    adj_refs, items_refs, out_refs = refs[:cols], refs[cols:-cols], refs[-cols:]
+def user_sum_kernel(cols, first, began, *refs):
+    adj_refs, refs, out_refs = refs[:cols], refs[cols:-cols], refs[-cols:]
+    begun, items_refs = (refs[:cols], refs[cols:]) if began else (None, refs)
     items = jnp.concatenate([ref[...].reshape(-1, ref.shape[-1]) for ref in items_refs], axis=0)
-    for adj_ref, out_ref in zip(adj_refs, out_refs, strict=True):
-        out_ref[...] = jnp.dot(adj_ref[...], items, preferred_element_type=F32).astype(BF16)
+    lanes = slice(first, first + items.shape[0])
+    for k, (adj_ref, out_ref) in enumerate(zip(adj_refs, out_refs, strict=True)):
+        total = jnp.dot(adj_ref[:, lanes], items, preferred_element_type=F32)
+        if began:
+            total = total + begun[k][...]
+        out_ref[...] = total.astype(out_ref.dtype)
 
 
 def merge_kernel(*refs):
@@ -395,21 +400,22 @@
     )(*blocks)
 
 
-def user_sums(adjacency, items):
+def user_sums(adjacency, items, first=0, begun=(), dtype=BF16):
     cols = len(adjacency)
-    upd, n = adjacency[0].shape
+    upd = adjacency[0].shape[0]
+    n = sum(block.size for block in items) // items[0].shape[-1]
     d = items[0].shape[-1]
     return pl.pallas_call(
-        functools.partial(user_sum_kernel, cols),
-        out_shape=(jax.ShapeDtypeStruct((upd, d), BF16),) * cols,
-        in_specs=[vmem_spec()] * (cols + len(items)),
+        functools.partial(user_sum_kernel, cols, first, len(begun) > 0),
+        out_shape=(jax.ShapeDtypeStruct((upd, d), dtype),) * cols,
+        in_specs=[vmem_spec()] * (cols + len(begun) + len(items)),
         out_specs=(vmem_spec(),) * cols,
         compiler_params=params(),
         cost_estimate=pl.CostEstimate(
             flops=2 * cols * upd * n * d, bytes_accessed=2 * cols * upd * n, transcendentals=0
         ),
         name="user_sums",
-    )(*adjacency, *items)
+    )(*adjacency, *begun, *items)
 
 
 def item_sum_kernel(cols, *refs):
@@ -590,7 +596,13 @@
             all_items = [*all_items, swap(merged, "row", rows)]
         *away, kept = item_sums(adjacency, all_users_t, sides, chips)
         came = [swap(part, "row", rows) for part in away]
-        user_parts = user_sums(adjacency, all_items)
+        if n > 0 and sides > 1:
+            begun = user_sums(adjacency, all_items[:chips], dtype=F32)
+            user_parts = user_sums(
+                adjacency, all_items[chips:], chips * ipd, begun
+            )
+        else:
+            user_parts = user_sums(adjacency, all_items)
         item_parts = item_add([kept, *came])
         item_parts = exchange(item_parts, "row", chips, sides)
         user_parts = exchange(user_parts, "col", cols)

time: 77.4 us -> 77.7 us (level)
    pallas_call x2 -> x3, Pallas kernels: 2.49 us -> 2.63 us  [user_sums(): pl.pallas_call(functools.partial(user_sum_kernel, cols, first, len(begun)...]
where the time goes in v6:
time: 77.7 us; the launch traced here: 77.3 us
  starting transfers between devices  40 us (51%)
  waiting for transfers between devices  18.4 us (24%)
  Pallas kernels  16.6 us (21%)
  local copies, waits for them, and re-layouts  1.39 us (2%)
  between operations  0.84 us (1%)
    ppermute x24, starting transfers between devices, exchange(): received.append(lax.ppermute(blocks[k], axis, pairs))  32.4 us
    ppermute x24, waiting for transfers between devices, exchange(): received.append(lax.ppermute(blocks[k], axis, pairs))  11.9 us
    all_to_all x1, starting transfers between devices, per_device(): lax.all_to_all(send, ('row', 'col'), split_axis=0, concat_axis=0, tiled=T...  7.33 us
    all_to_all x1, waiting for transfers between devices, per_device(): lax.all_to_all(send, ('row', 'col'), split_axis=0, concat_axis=0, tiled=T...  6.56 us
    pallas_call x1, Pallas kernels, dequantize(): pl.pallas_call(functools.partial(dequantize_kernel, shape), out_shape=(ja...  5.02 us
    pallas_call x1, Pallas kernels, dispatch(): pl.pallas_call(functools.partial(dispatch_kernel, devices, capacity), out...  3.22 us
    pallas_call x3, Pallas kernels, user_sums(): pl.pallas_call(functools.partial(user_sum_kernel, cols, first, len(begun)...  2.63 us
    pallas_call x1, Pallas kernels, segment(): pl.pallas_call(functools.partial(segment_kernel, capacity, upd, cols), ou...  1.88 us
  transfers between devices with their start and end apart: 29, of which 9 were waited for; matrix products, arithmetic and copies ran while one was open for 0% of the time, Pallas kernels for 14%

profile of v6, /device:TPU:0, one launch (start us, length us, event | category | flops | bytes accessed | tf_op | source)
XLA Modules:
  0.0 77.3 jit_solution(7852085805803300627)
XLA Ops:
  0.6 3.2 %dispatch.1 = bf16[32,56,128]{2,1,0:T(8,128)(2,1)} custom-call(s32[1]{0:T(128)} %bitcast.me_ref, bf16[64,1024]{1,0:T(8,128)(2,1)} %bitcast.6, s32[1,1024]{1,0:T(1,128)} %bitcast.8, s32[1,1024]{1,0:T(1,128)} %bitcast.9, s32[1,1024]{1,0:T(1,128)} %bitcast.10), custom_call_target="tpu_custom_call" | custom-call | tf_op jit(solution)/shard_map/dispatch/pallas_call | solution.py:213
  3.9 7.3 %all-to-all-start = ((bf16[32,56,128]{2,1,0:T(8,128)(2,1)}), bf16[32,56,128]{2,1,0:T(8,128)(2,1)S(1)}, u32[]{:S(2)}, u32[]{:S(2)}) async-start(bf16[32,56,128]{2,1,0:T(8,128)(2,1)} %dispatch.1), calls=%async_computation | async-start | bytes 917504 | tf_op jit(solution)/shard_map/all_to_all | solution.py:583
  11.2 0.7 copy-done.4
  11.9 0.7 copy-done.5
  12.6 5.0 %dequantize.1 = (bf16[256,2048]{1,0:T(8,128)(2,1)S(1)}, bf16[256,2048]{1,0:T(8,128)(2,1)}, bf16[256,2048]{1,0:T(8,128)(2,1)}, bf16[256,2048]{1,0:T(8,128)(2,1)}) custom-call(s32[1]{0:T(128)} %bitcast.me_ref, s32[8,16]{1,0:T(8,128)S(1)} %copy-done.4, f32[8,16]{1,0:T(8,128)S(1)} %copy-done.5, bf16[1024,2048]{1,0:T(8,128)(2,1)} %values_ref.1), custom_call_target="tpu_custom_call" | custom-call | flops 2097152 | bytes 8388608 | tf_op jit(solution)/shard_map/dequantize/pallas_call | solution.py:356
  17.6 6.6 %all-to-all-done.recv_ref = bf16[32,56,128]{2,1,0:T(8,128)(2,1)S(1)} async-done(((bf16[32,56,128]{2,1,0:T(8,128)(2,1)}), bf16[32,56,128]{2,1,0:T(8,128)(2,1)S(1)}, u32[]{:S(2)}, u32[]{:S(2)}) %all-to-all-start) | async-done | bytes 458784 | tf_op jit(solution)/shard_map/all_to_all | solution.py:583
  24.2 1.9 %segment.1 = (bf16[256,128]{1,0:T(8,128)(2,1)S(1)}, bf16[128,256]{1,0:T(8,128)(2,1)S(1)}, bf16[256,128]{1,0:T(8,128)(2,1)S(1)}, bf16[256,2048]{1,0:T(8,128)(2,1)...) custom-call(s32[1]{0:T(128)} %bitcast.me_ref, bf16[32,56,128]{2,1,0:T(8,128)(2,1)S(1)} %all-to-all-done.recv_ref, ...), custom_call_target="tpu_custom_call" | custom-call | tf_op jit(solution)/shard_map/segment/pallas_call | solution.py:287
  26.1 2.2 %collective-permute-start.2 = (bf16[256,128]{1,0:T(8,128)(2,1)S(1)}, bf16[256,128]{1,0:T(8,128)(2,1)S(1)}, u32[]{:S(2)}, u32[]{:S(2)}) collective-permute-start(bf16[256,128]{1,0:T(8,128)(2,1)S(1)} %get-tuple-element.47.refs_0_.refs_4_.own_ref), channel_id=1, source_target_pairs={{0,24},{4,28},{8,16},{12,20},{16,8},{20,12},{24,0},{28,4},{1,25},{... | collective-permute-start | bytes 196616 | tf_op jit(solution)/shard_map/ppermute | solution.py:537
  28.3 0.8 %collective-permute-start.1 = (bf16[256,128]{1,0:T(8,128)(2,1)S(1)}, bf16[256,128]{1,0:T(8,128)(2,1)S(1)}, u32[]{:S(2)}, u32[]{:S(2)}) collective-permute-start(bf16[256,128]{1,0:T(8,128)(2,1)S(1)} %get-tuple-element.47.refs_0_.refs_4_.own_ref), channel_id=1, source_target_pairs={{0,16},{4,20},{8,24},{12,28},{16,0},{20,4},{24,8},{28,12},{1,17},{... | collective-permute-start | bytes 196616 | tf_op jit(solution)/shard_map/ppermute | solution.py:537
  29.1 0.5 collective-permute-start
  29.7 2.8 %collective-permute-start.9 = (bf16[128,256]{1,0:T(8,128)(2,1)S(1)}, bf16[128,256]{1,0:T(8,128)(2,1)S(1)}, u32[]{:S(2)}, u32[]{:S(2)}) collective-permute-start(bf16[128,256]{1,0:T(8,128)(2,1)S(1)} %get-tuple-element.53.refs_4_), channel_id=1, source_target_pairs={{0,3},{1,2},{2,1},{3,0},{4,7},{5,6},{6,5},{7,4},{8,11},{9,10},{10,... | collective-permute-start | bytes 196616 | tf_op jit(solution)/shard_map/ppermute | solution.py:537
  32.5 1.1 %collective-permute-start.8 = (bf16[128,256]{1,0:T(8,128)(2,1)S(1)}, bf16[128,256]{1,0:T(8,128)(2,1)S(1)}, u32[]{:S(2)}, u32[]{:S(2)}) collective-permute-start(bf16[128,256]{1,0:T(8,128)(2,1)S(1)} %get-tuple-element.53.refs_4_), channel_id=1, source_target_pairs={{0,2},{1,3},{2,0},{3,1},{4,6},{5,7},{6,4},{7,5},{8,10},{9,11},{10,... | collective-permute-start | bytes 196616 | tf_op jit(solution)/shard_map/ppermute | solution.py:537
  33.5 0.9 %collective-permute-start.7 = (bf16[128,256]{1,0:T(8,128)(2,1)S(1)}, bf16[128,256]{1,0:T(8,128)(2,1)S(1)}, u32[]{:S(2)}, u32[]{:S(2)}) collective-permute-start(bf16[128,256]{1,0:T(8,128)(2,1)S(1)} %get-tuple-element.53.refs_4_), channel_id=1, source_target_pairs={{0,1},{1,0},{2,3},{3,2},{4,5},{5,4},{6,7},{7,6},{8,9},{9,8},{10,11... | collective-permute-start | bytes 196616 | tf_op jit(solution)/shard_map/ppermute | solution.py:537
  34.6 2.0 %collective-permute-done.9.refs_7_ = bf16[128,256]{1,0:T(8,128)(2,1)S(1)} collective-permute-done((bf16[128,256]{1,0:T(8,128)(2,1)S(1)}, bf16[128,256]{1,0:T(8,128)(2,1)S(1)}, u32[]{:S(2)}, u32[]{:S(2)}) %collective-permute-start.9) | collective-permute-done | bytes 65568 | tf_op jit(solution)/shard_map/ppermute | solution.py:537
  36.5 2.9 %collective-permute-done.8.refs_6_ = bf16[128,256]{1,0:T(8,128)(2,1)S(1)} collective-permute-done((bf16[128,256]{1,0:T(8,128)(2,1)S(1)}, bf16[128,256]{1,0:T(8,128)(2,1)S(1)}, u32[]{:S(2)}, u32[]{:S(2)}) %collective-permute-start.8) | collective-permute-done | bytes 65568 | tf_op jit(solution)/shard_map/ppermute | solution.py:537
  39.4 0.7 item_sums.2
  40.2 1.2 %user_sums.3 = (bf16[256,128]{1,0:T(8,128)(2,1)S(1)}, bf16[256,128]{1,0:T(8,128)(2,1)S(1)}, bf16[256,128]{1,0:T(8,128)(2,1)S(1)}, bf16[256,128]{1,0:T(8,128)(2,1)S(1)}) custom-call(bf16[256,2048]{1,0:T(8,128)(2,1)S(1)} %get-tuple-element.43.refs_0_, bf16[256,2048]{1,0:T(8,128)(2,1)S(1)} %get-tuple-element.44.refs_1_, ...), custom_call_target="tpu_custom_call" | custom-call | flops 536870912 | bytes 4194304 | tf_op jit(solution)/shard_map/user_sums/pallas_call | solution.py:408
  41.5 0.1 collective-permute-start.4
  41.6 1.8 %collective-permute-start.5 = (bf16[256,128]{1,0:T(8,128)(2,1)S(1)}, bf16[256,128]{1,0:T(8,128)(2,1)S(1)}, u32[]{:S(2)}, u32[]{:S(2)}) collective-permute-start(bf16[256,128]{1,0:T(8,128)(2,1)S(1)} %get-tuple-element.50), channel_id=1, source_target_pairs={{0,2},{1,3},{2,0},{3,1},{4,6},{5,7},{6,4},{7,5},{8,10},{9,11},{10,... | collective-permute-start | bytes 196616 | tf_op jit(solution)/shard_map/ppermute | solution.py:537
  43.3 2.6 %collective-permute-start.6 = (bf16[256,128]{1,0:T(8,128)(2,1)S(1)}, bf16[256,128]{1,0:T(8,128)(2,1)S(1)}, u32[]{:S(2)}, u32[]{:S(2)}) collective-permute-start(bf16[256,128]{1,0:T(8,128)(2,1)S(1)} %get-tuple-element.51), channel_id=1, source_target_pairs={{0,3},{1,2},{2,1},{3,0},{4,7},{5,6},{6,5},{7,4},{8,11},{9,10},{10,... | collective-permute-start | bytes 196616 | tf_op jit(solution)/shard_map/ppermute | solution.py:537
  46.0 1.1 %collective-permute-start.11 = (bf16[128,256]{1,0:T(8,128)(2,1)S(1)}, bf16[128,256]{1,0:T(8,128)(2,1)S(1)}, u32[]{:S(2)}, u32[]{:S(2)}) collective-permute-start(bf16[128,256]{1,0:T(8,128)(2,1)S(1)} %get-tuple-element.57), channel_id=1, source_target_pairs={{0,8},{4,12},{8,0},{12,4},{16,24},{20,28},{24,16},{28,20},{1,9},{5... | collective-permute-start | bytes 196616 | tf_op jit(solution)/shard_map/ppermute | solution.py:537
  47.1 0.8 %collective-permute-start.12 = (bf16[128,256]{1,0:T(8,128)(2,1)S(1)}, bf16[128,256]{1,0:T(8,128)(2,1)S(1)}, u32[]{:S(2)}, u32[]{:S(2)}) collective-permute-start(bf16[128,256]{1,0:T(8,128)(2,1)S(1)} %get-tuple-element.58), channel_id=1, source_target_pairs={{0,16},{4,20},{8,24},{12,28},{16,0},{20,4},{24,8},{28,12},{1,17},{... | collective-permute-start | bytes 196616 | tf_op jit(solution)/shard_map/ppermute | solution.py:537
  47.9 1.6 %collective-permute-start.13 = (bf16[128,256]{1,0:T(8,128)(2,1)S(1)}, bf16[128,256]{1,0:T(8,128)(2,1)S(1)}, u32[]{:S(2)}, u32[]{:S(2)}) collective-permute-start(bf16[128,256]{1,0:T(8,128)(2,1)S(1)} %get-tuple-element.59), channel_id=1, source_target_pairs={{0,24},{4,28},{8,16},{12,20},{16,8},{20,12},{24,0},{28,4},{1,25},{... | collective-permute-start | bytes 196616 | tf_op jit(solution)/shard_map/ppermute | solution.py:537
  49.5 0.8 collective-permute-done.5.refs_2_
  50.3 0.3 user_update.2
  50.6 1.8 %collective-permute-start.23 = (bf16[128,256]{1,0:T(8,128)(2,1)S(1)}, bf16[128,256]{1,0:T(8,128)(2,1)S(1)}, u32[]{:S(2)}, u32[]{:S(2)}) collective-permute-start(bf16[128,256]{1,0:T(8,128)(2,1)S(1)} %get-tuple-element.69.refs_4_), channel_id=1, source_target_pairs={{0,3},{1,2},{2,1},{3,0},{4,7},{5,6},{6,5},{7,4},{8,11},{9,10},{10,... | collective-permute-start | bytes 196616 | tf_op jit(solution)/shard_map/ppermute | solution.py:537
  52.3 1.3 %collective-permute-start.22 = (bf16[128,256]{1,0:T(8,128)(2,1)S(1)}, bf16[128,256]{1,0:T(8,128)(2,1)S(1)}, u32[]{:S(2)}, u32[]{:S(2)}) collective-permute-start(bf16[128,256]{1,0:T(8,128)(2,1)S(1)} %get-tuple-element.69.refs_4_), channel_id=1, source_target_pairs={{0,2},{1,3},{2,0},{3,1},{4,6},{5,7},{6,4},{7,5},{8,10},{9,11},{10,... | collective-permute-start | bytes 196616 | tf_op jit(solution)/shard_map/ppermute | solution.py:537
  53.6 1.4 %collective-permute-start.21 = (bf16[128,256]{1,0:T(8,128)(2,1)S(1)}, bf16[128,256]{1,0:T(8,128)(2,1)S(1)}, u32[]{:S(2)}, u32[]{:S(2)}) collective-permute-start(bf16[128,256]{1,0:T(8,128)(2,1)S(1)} %get-tuple-element.69.refs_4_), channel_id=1, source_target_pairs={{0,1},{1,0},{2,3},{3,2},{4,5},{5,4},{6,7},{7,6},{8,9},{9,8},{10,11... | collective-permute-start | bytes 196616 | tf_op jit(solution)/shard_map/ppermute | solution.py:537
  55.0 0.3 item_update.2.refs_4_.refs_0_.own_ref
  55.3 1.4 %collective-permute-start.16 = (bf16[256,128]{1,0:T(8,128)(2,1)S(1)}, bf16[256,128]{1,0:T(8,128)(2,1)S(1)}, u32[]{:S(2)}, u32[]{:S(2)}) collective-permute-start(bf16[256,128]{1,0:T(8,128)(2,1)S(1)} %item_update.2.refs_4_.refs_0_.own_ref), channel_id=1, source_target_pairs={{0,24},{4,28},{8,16},{12,20},{16,8},{20,12},{24,0},{28,4},{1,25},{... | collective-permute-start | bytes 196616 | tf_op jit(solution)/shard_map/ppermute | solution.py:537
  56.7 1.2 %collective-permute-start.15 = (bf16[256,128]{1,0:T(8,128)(2,1)S(1)}, bf16[256,128]{1,0:T(8,128)(2,1)S(1)}, u32[]{:S(2)}, u32[]{:S(2)}) collective-permute-start(bf16[256,128]{1,0:T(8,128)(2,1)S(1)} %item_update.2.refs_4_.refs_0_.own_ref), channel_id=1, source_target_pairs={{0,16},{4,20},{8,24},{12,28},{16,0},{20,4},{24,8},{28,12},{1,17},{... | collective-permute-start | bytes 196616 | tf_op jit(solution)/shard_map/ppermute | solution.py:537
  57.9 1.0 %collective-permute-start.14 = (bf16[256,128]{1,0:T(8,128)(2,1)S(1)}, bf16[256,128]{1,0:T(8,128)(2,1)S(1)}, u32[]{:S(2)}, u32[]{:S(2)}) collective-permute-start(bf16[256,128]{1,0:T(8,128)(2,1)S(1)} %item_update.2.refs_4_.refs_0_.own_ref), channel_id=1, source_target_pairs={{0,8},{4,12},{8,0},{12,4},{16,24},{20,28},{24,16},{28,20},{1,9},{5... | collective-permute-start | bytes 196616 | tf_op jit(solution)/shard_map/ppermute | solution.py:537
  58.9 0.5 collective-permute-done.22.refs_6_
  59.4 0.7 item_sums.3
  60.2 0.4 collective-permute-done.16.refs_7_.refs_3_
  60.6 0.7 collective-permute-done.15.refs_6_.refs_2_
  61.2 0.9 %collective-permute-done.14.refs_5_.refs_1_ = bf16[256,128]{1,0:T(8,128)(2,1)S(1)} collective-permute-done((bf16[256,128]{1,0:T(8,128)(2,1)S(1)}, bf16[256,128]{1,0:T(8,128)(2,1)S(1)}, u32[]{:S(2)}, u32[]{:S(2)}) %collective-permute-start.14) | collective-permute-done | bytes 65568 | tf_op jit(solution)/shard_map/ppermute | solution.py:537
  62.3 1.0 %collective-permute-start.25 = (bf16[128,256]{1,0:T(8,128)(2,1)S(1)}, bf16[128,256]{1,0:T(8,128)(2,1)S(1)}, u32[]{:S(2)}, u32[]{:S(2)}) collective-permute-start(bf16[128,256]{1,0:T(8,128)(2,1)S(1)} %get-tuple-element.73), channel_id=1, source_target_pairs={{0,8},{4,12},{8,0},{12,4},{16,24},{20,28},{24,16},{28,20},{1,9},{5... | collective-permute-start | bytes 196616 | tf_op jit(solution)/shard_map/ppermute | solution.py:537
  63.4 0.7 user_sums.4
  64.1 1.2 %collective-permute-start.26 = (bf16[128,256]{1,0:T(8,128)(2,1)S(1)}, bf16[128,256]{1,0:T(8,128)(2,1)S(1)}, u32[]{:S(2)}, u32[]{:S(2)}) collective-permute-start(bf16[128,256]{1,0:T(8,128)(2,1)S(1)} %get-tuple-element.74), channel_id=1, source_target_pairs={{0,16},{4,20},{8,24},{12,28},{16,0},{20,4},{24,8},{28,12},{1,17},{... | collective-permute-start | bytes 196616 | tf_op jit(solution)/shard_map/ppermute | solution.py:537
  65.3 1.4 %collective-permute-start.27 = (bf16[128,256]{1,0:T(8,128)(2,1)S(1)}, bf16[128,256]{1,0:T(8,128)(2,1)S(1)}, u32[]{:S(2)}, u32[]{:S(2)}) collective-permute-start(bf16[128,256]{1,0:T(8,128)(2,1)S(1)} %get-tuple-element.75), channel_id=1, source_target_pairs={{0,24},{4,28},{8,16},{12,20},{16,8},{20,12},{24,0},{28,4},{1,25},{... | collective-permute-start | bytes 196616 | tf_op jit(solution)/shard_map/ppermute | solution.py:537
  66.6 0.7 user_sums.5
  67.3 1.3 %collective-permute-start.18 = (bf16[256,128]{1,0:T(8,128)(2,1)S(1)}, bf16[256,128]{1,0:T(8,128)(2,1)S(1)}, u32[]{:S(2)}, u32[]{:S(2)}) collective-permute-start(bf16[256,128]{1,0:T(8,128)(2,1)S(1)} %get-tuple-element.65), channel_id=1, source_target_pairs={{0,1},{1,0},{2,3},{3,2},{4,5},{5,4},{6,7},{7,6},{8,9},{9,8},{10,11... | collective-permute-start | bytes 196616 | tf_op jit(solution)/shard_map/ppermute | solution.py:537
  68.7 1.2 %collective-permute-start.19 = (bf16[256,128]{1,0:T(8,128)(2,1)S(1)}, bf16[256,128]{1,0:T(8,128)(2,1)S(1)}, u32[]{:S(2)}, u32[]{:S(2)}) collective-permute-start(bf16[256,128]{1,0:T(8,128)(2,1)S(1)} %get-tuple-element.66), channel_id=1, source_target_pairs={{0,2},{1,3},{2,0},{3,1},{4,6},{5,7},{6,4},{7,5},{8,10},{9,11},{10,... | collective-permute-start | bytes 196616 | tf_op jit(solution)/shard_map/ppermute | solution.py:537
  69.9 1.9 %collective-permute-start.20 = (bf16[256,128]{1,0:T(8,128)(2,1)S(1)}, bf16[256,128]{1,0:T(8,128)(2,1)S(1)}, u32[]{:S(2)}, u32[]{:S(2)}) collective-permute-start(bf16[256,128]{1,0:T(8,128)(2,1)S(1)} %get-tuple-element.67), channel_id=1, source_target_pairs={{0,3},{1,2},{2,1},{3,0},{4,7},{5,6},{6,5},{7,4},{8,11},{9,10},{10,... | collective-permute-start | bytes 196616 | tf_op jit(solution)/shard_map/ppermute | solution.py:537
  71.8 0.9 %item_update.3 = bf16[256,128]{1,0:T(8,128)(2,1)} custom-call(bf16[256,128]{1,0:T(8,128)(2,1)S(1)} %item_update.2.refs_4_.refs_0_.own_ref, bf16[2,128,128]{2,1,0:T(8,128)(2,1)S(1)} %copy-done, bf16[2,128,128]{2,1,0:T(8,128)(2,1)S(1)} %copy-done.1, bf16[128,256]{1,0:T(8,128)(2,1)S(1)} %get-tuple-element.72.refs_0_, ...), custom_call_target="tpu_custom_call" | custom-call | tf_op jit(solution)/shard_map/item_update/pallas_call | solution.py:521
  72.7 3.7 %collective-permute-done.19.refs_2_ = bf16[256,128]{1,0:T(8,128)(2,1)S(1)} collective-permute-done((bf16[256,128]{1,0:T(8,128)(2,1)S(1)}, bf16[256,128]{1,0:T(8,128)(2,1)S(1)}, u32[]{:S(2)}, u32[]{:S(2)}) %collective-permute-start.19) | collective-permute-done | bytes 65568 | tf_op jit(solution)/shard_map/ppermute | solution.py:537
  76.4 0.9 %user_update.3 = (bf16[256,128]{1,0:T(8,128)(2,1)}, bf16[128,256]{1,0:T(8,128)(2,1)}) custom-call(bf16[256,128]{1,0:T(8,128)(2,1)S(1)} %get-tuple-element.52.own_ref, bf16[2,128,128]{2,1,0:T(8,128)(2,1)S(1)} %copy-done, bf16[2,128,128]{2,1,0:T(8,128)(2,1)S(1)} %copy-done.1, bf16[256,128]{1,0:T(8,128)(2,1)S(1)} %get-tuple-element.64.refs_0_, ...), custom_call_target="tpu_custom_call" | custom-call | tf_op jit(solution)/shard_map/user_update/pallas_call | solution.py:501
  (38 shorter events, 0.5 us)
Async XLA Ops:
  3.9 20.3 %copy-start.2 = (bf16[64,128]{1,0:T(8,128)(2,1)S(1)}, bf16[64,128]{1,0:T(8,128)(2,1)}, u32[]{:S(2)}) copy-start(bf16[64,128]{1,0:T(8,128)(2,1)} %proj_wide_ref.1) | copy-start | bytes 49156
  3.9 20.3 %copy-start.3 = (bf16[32,128]{1,0:T(8,128)(2,1)S(1)}, bf16[32,128]{1,0:T(8,128)(2,1)}, u32[]{:S(2)}) copy-start(bf16[32,128]{1,0:T(8,128)(2,1)} %proj_narrow_ref.1) | copy-start | bytes 24580
  3.9 20.3 %all-to-all-start = ((bf16[32,56,128]{2,1,0:T(8,128)(2,1)}), bf16[32,56,128]{2,1,0:T(8,128)(2,1)S(1)}, u32[]{:S(2)}, u32[]{:S(2)}) async-start(bf16[32,56,128]{2,1,0:T(8,128)(2,1)} %dispatch.1), calls=%async_computation | async-start | bytes 917504 | tf_op jit(solution)/shard_map/all_to_all | solution.py:583
  11.2 0.7 copy-start.4
  11.9 0.7 copy-start.5
  26.1 7.4 %collective-permute-start.2 = (bf16[256,128]{1,0:T(8,128)(2,1)S(1)}, bf16[256,128]{1,0:T(8,128)(2,1)S(1)}, u32[]{:S(2)}, u32[]{:S(2)}) collective-permute-start(bf16[256,128]{1,0:T(8,128)(2,1)S(1)} %get-tuple-element.47.refs_0_.refs_4_.own_ref), channel_id=1, source_target_pairs={{0,24},{4,28},{8,16},{12,20},{16,8},{20,12},{24,0},{28,4},{1,25},{... | collective-permute-start | bytes 196616 | tf_op jit(solution)/shard_map/ppermute | solution.py:537
  28.3 6.2 %collective-permute-start.1 = (bf16[256,128]{1,0:T(8,128)(2,1)S(1)}, bf16[256,128]{1,0:T(8,128)(2,1)S(1)}, u32[]{:S(2)}, u32[]{:S(2)}) collective-permute-start(bf16[256,128]{1,0:T(8,128)(2,1)S(1)} %get-tuple-element.47.refs_0_.refs_4_.own_ref), channel_id=1, source_target_pairs={{0,16},{4,20},{8,24},{12,28},{16,0},{20,4},{24,8},{28,12},{1,17},{... | collective-permute-start | bytes 196616 | tf_op jit(solution)/shard_map/ppermute | solution.py:537
  29.1 5.3 %collective-permute-start = (bf16[256,128]{1,0:T(8,128)(2,1)S(1)}, bf16[256,128]{1,0:T(8,128)(2,1)S(1)}, u32[]{:S(2)}, u32[]{:S(2)}) collective-permute-start(bf16[256,128]{1,0:T(8,128)(2,1)S(1)} %get-tuple-element.47.refs_0_.refs_4_.own_ref), channel_id=1, source_target_pairs={{0,8},{4,12},{8,0},{12,4},{16,24},{20,28},{24,16},{28,20},{1,9},{5... | collective-permute-start | bytes 196616 | tf_op jit(solution)/shard_map/ppermute | solution.py:537
  29.7 6.9 %collective-permute-start.9 = (bf16[128,256]{1,0:T(8,128)(2,1)S(1)}, bf16[128,256]{1,0:T(8,128)(2,1)S(1)}, u32[]{:S(2)}, u32[]{:S(2)}) collective-permute-start(bf16[128,256]{1,0:T(8,128)(2,1)S(1)} %get-tuple-element.53.refs_4_), channel_id=1, source_target_pairs={{0,3},{1,2},{2,1},{3,0},{4,7},{5,6},{6,5},{7,4},{8,11},{9,10},{10,... | collective-permute-start | bytes 196616 | tf_op jit(solution)/shard_map/ppermute | solution.py:537
  32.5 6.9 %collective-permute-start.8 = (bf16[128,256]{1,0:T(8,128)(2,1)S(1)}, bf16[128,256]{1,0:T(8,128)(2,1)S(1)}, u32[]{:S(2)}, u32[]{:S(2)}) collective-permute-start(bf16[128,256]{1,0:T(8,128)(2,1)S(1)} %get-tuple-element.53.refs_4_), channel_id=1, source_target_pairs={{0,2},{1,3},{2,0},{3,1},{4,6},{5,7},{6,4},{7,5},{8,10},{9,11},{10,... | collective-permute-start | bytes 196616 | tf_op jit(solution)/shard_map/ppermute | solution.py:537
  33.5 5.9 %collective-permute-start.7 = (bf16[128,256]{1,0:T(8,128)(2,1)S(1)}, bf16[128,256]{1,0:T(8,128)(2,1)S(1)}, u32[]{:S(2)}, u32[]{:S(2)}) collective-permute-start(bf16[128,256]{1,0:T(8,128)(2,1)S(1)} %get-tuple-element.53.refs_4_), channel_id=1, source_target_pairs={{0,1},{1,0},{2,3},{3,2},{4,5},{5,4},{6,7},{7,6},{8,9},{9,8},{10,11... | collective-permute-start | bytes 196616 | tf_op jit(solution)/shard_map/ppermute | solution.py:537
  34.5 5.7 %collective-permute-start.3 = (bf16[4,256,128]{2,1,0:T(8,128)(2,1)S(1)}, bf16[4,256,128]{2,1,0:T(8,128)(2,1)S(1)}, u32[]{:S(2)}, u32[]{:S(2)}) collective-permute-start(bf16[4,256,128]{2,1,0:T(8,128)(2,1)S(1)} %merge.2), channel_id=1, source_target_pairs={{0,4},{4,0},{8,12},{12,8},{16,20},{20,16},{24,28},{28,24},{1,5},{5... | collective-permute-start | bytes 786440 | tf_op jit(solution)/shard_map/ppermute | solution.py:542
  39.4 10.9 %copy-start = (bf16[2,128,128]{2,1,0:T(8,128)(2,1)S(1)}, bf16[2,128,128]{2,1,0:T(8,128)(2,1)}, u32[]{:S(2)}) copy-start(bf16[2,128,128]{2,1,0:T(8,128)(2,1)} %sum_ref.7) | copy-start | bytes 196612
  39.4 10.9 %copy-start.1 = (bf16[2,128,128]{2,1,0:T(8,128)(2,1)S(1)}, bf16[2,128,128]{2,1,0:T(8,128)(2,1)}, u32[]{:S(2)}) copy-start(bf16[2,128,128]{2,1,0:T(8,128)(2,1)} %product_ref.7) | copy-start | bytes 196612
  40.1 5.8 %collective-permute-start.10 = (bf16[4,128,256]{2,1,0:T(8,128)(2,1)S(1)}, bf16[4,128,256]{2,1,0:T(8,128)(2,1)S(1)}, u32[]{:S(2)}, u32[]{:S(2)}) collective-permute-start(bf16[4,128,256]{2,1,0:T(8,128)(2,1)S(1)} %get-tuple-element.55), channel_id=1, source_target_pairs={{0,4},{4,0},{8,12},{12,8},{16,20},{20,16},{24,28},{28,24},{1,5},{5... | collective-permute-start | bytes 786440 | tf_op jit(solution)/shard_map/ppermute | solution.py:542
  41.5 6.4 %collective-permute-start.4 = (bf16[256,128]{1,0:T(8,128)(2,1)S(1)}, bf16[256,128]{1,0:T(8,128)(2,1)S(1)}, u32[]{:S(2)}, u32[]{:S(2)}) collective-permute-start(bf16[256,128]{1,0:T(8,128)(2,1)S(1)} %get-tuple-element.49), channel_id=1, source_target_pairs={{0,1},{1,0},{2,3},{3,2},{4,5},{5,4},{6,7},{7,6},{8,9},{9,8},{10,11... | collective-permute-start | bytes 196616 | tf_op jit(solution)/shard_map/ppermute | solution.py:537
  41.6 8.7 %collective-permute-start.5 = (bf16[256,128]{1,0:T(8,128)(2,1)S(1)}, bf16[256,128]{1,0:T(8,128)(2,1)S(1)}, u32[]{:S(2)}, u32[]{:S(2)}) collective-permute-start(bf16[256,128]{1,0:T(8,128)(2,1)S(1)} %get-tuple-element.50), channel_id=1, source_target_pairs={{0,2},{1,3},{2,0},{3,1},{4,6},{5,7},{6,4},{7,5},{8,10},{9,11},{10,... | collective-permute-start | bytes 196616 | tf_op jit(solution)/shard_map/ppermute | solution.py:537
  43.3 7.0 %collective-permute-start.6 = (bf16[256,128]{1,0:T(8,128)(2,1)S(1)}, bf16[256,128]{1,0:T(8,128)(2,1)S(1)}, u32[]{:S(2)}, u32[]{:S(2)}) collective-permute-start(bf16[256,128]{1,0:T(8,128)(2,1)S(1)} %get-tuple-element.51), channel_id=1, source_target_pairs={{0,3},{1,2},{2,1},{3,0},{4,7},{5,6},{6,5},{7,4},{8,11},{9,10},{10,... | collective-permute-start | bytes 196616 | tf_op jit(solution)/shard_map/ppermute | solution.py:537
  46.0 7.6 %collective-permute-start.11 = (bf16[128,256]{1,0:T(8,128)(2,1)S(1)}, bf16[128,256]{1,0:T(8,128)(2,1)S(1)}, u32[]{:S(2)}, u32[]{:S(2)}) collective-permute-start(bf16[128,256]{1,0:T(8,128)(2,1)S(1)} %get-tuple-element.57), channel_id=1, source_target_pairs={{0,8},{4,12},{8,0},{12,4},{16,24},{20,28},{24,16},{28,20},{1,9},{5... | collective-permute-start | bytes 196616 | tf_op jit(solution)/shard_map/ppermute | solution.py:537
  47.1 7.9 %collective-permute-start.12 = (bf16[128,256]{1,0:T(8,128)(2,1)S(1)}, bf16[128,256]{1,0:T(8,128)(2,1)S(1)}, u32[]{:S(2)}, u32[]{:S(2)}) collective-permute-start(bf16[128,256]{1,0:T(8,128)(2,1)S(1)} %get-tuple-element.58), channel_id=1, source_target_pairs={{0,16},{4,20},{8,24},{12,28},{16,0},{20,4},{24,8},{28,12},{1,17},{... | collective-permute-start | bytes 196616 | tf_op jit(solution)/shard_map/ppermute | solution.py:537
  47.9 7.1 %collective-permute-start.13 = (bf16[128,256]{1,0:T(8,128)(2,1)S(1)}, bf16[128,256]{1,0:T(8,128)(2,1)S(1)}, u32[]{:S(2)}, u32[]{:S(2)}) collective-permute-start(bf16[128,256]{1,0:T(8,128)(2,1)S(1)} %get-tuple-element.59), channel_id=1, source_target_pairs={{0,24},{4,28},{8,16},{12,20},{16,8},{20,12},{24,0},{28,4},{1,25},{... | collective-permute-start | bytes 196616 | tf_op jit(solution)/shard_map/ppermute | solution.py:537
  50.6 7.3 %collective-permute-start.23 = (bf16[128,256]{1,0:T(8,128)(2,1)S(1)}, bf16[128,256]{1,0:T(8,128)(2,1)S(1)}, u32[]{:S(2)}, u32[]{:S(2)}) collective-permute-start(bf16[128,256]{1,0:T(8,128)(2,1)S(1)} %get-tuple-element.69.refs_4_), channel_id=1, source_target_pairs={{0,3},{1,2},{2,1},{3,0},{4,7},{5,6},{6,5},{7,4},{8,11},{9,10},{10,... | collective-permute-start | bytes 196616 | tf_op jit(solution)/shard_map/ppermute | solution.py:537
  52.3 7.1 %collective-permute-start.22 = (bf16[128,256]{1,0:T(8,128)(2,1)S(1)}, bf16[128,256]{1,0:T(8,128)(2,1)S(1)}, u32[]{:S(2)}, u32[]{:S(2)}) collective-permute-start(bf16[128,256]{1,0:T(8,128)(2,1)S(1)} %get-tuple-element.69.refs_4_), channel_id=1, source_target_pairs={{0,2},{1,3},{2,0},{3,1},{4,6},{5,7},{6,4},{7,5},{8,10},{9,11},{10,... | collective-permute-start | bytes 196616 | tf_op jit(solution)/shard_map/ppermute | solution.py:537
  53.6 5.8 %collective-permute-start.21 = (bf16[128,256]{1,0:T(8,128)(2,1)S(1)}, bf16[128,256]{1,0:T(8,128)(2,1)S(1)}, u32[]{:S(2)}, u32[]{:S(2)}) collective-permute-start(bf16[128,256]{1,0:T(8,128)(2,1)S(1)} %get-tuple-element.69.refs_4_), channel_id=1, source_target_pairs={{0,1},{1,0},{2,3},{3,2},{4,5},{5,4},{6,7},{7,6},{8,9},{9,8},{10,11... | collective-permute-start | bytes 196616 | tf_op jit(solution)/shard_map/ppermute | solution.py:537
  55.3 5.3 %collective-permute-start.16 = (bf16[256,128]{1,0:T(8,128)(2,1)S(1)}, bf16[256,128]{1,0:T(8,128)(2,1)S(1)}, u32[]{:S(2)}, u32[]{:S(2)}) collective-permute-start(bf16[256,128]{1,0:T(8,128)(2,1)S(1)} %item_update.2.refs_4_.refs_0_.own_ref), channel_id=1, source_target_pairs={{0,24},{4,28},{8,16},{12,20},{16,8},{20,12},{24,0},{28,4},{1,25},{... | collective-permute-start | bytes 196616 | tf_op jit(solution)/shard_map/ppermute | solution.py:537
  56.7 4.6 %collective-permute-start.15 = (bf16[256,128]{1,0:T(8,128)(2,1)S(1)}, bf16[256,128]{1,0:T(8,128)(2,1)S(1)}, u32[]{:S(2)}, u32[]{:S(2)}) collective-permute-start(bf16[256,128]{1,0:T(8,128)(2,1)S(1)} %item_update.2.refs_4_.refs_0_.own_ref), channel_id=1, source_target_pairs={{0,16},{4,20},{8,24},{12,28},{16,0},{20,4},{24,8},{28,12},{1,17},{... | collective-permute-start | bytes 196616 | tf_op jit(solution)/shard_map/ppermute | solution.py:537
  57.9 4.3 %collective-permute-start.14 = (bf16[256,128]{1,0:T(8,128)(2,1)S(1)}, bf16[256,128]{1,0:T(8,128)(2,1)S(1)}, u32[]{:S(2)}, u32[]{:S(2)}) collective-permute-start(bf16[256,128]{1,0:T(8,128)(2,1)S(1)} %item_update.2.refs_4_.refs_0_.own_ref), channel_id=1, source_target_pairs={{0,8},{4,12},{8,0},{12,4},{16,24},{20,28},{24,16},{28,20},{1,9},{5... | collective-permute-start | bytes 196616 | tf_op jit(solution)/shard_map/ppermute | solution.py:537
  60.1 2.1 %collective-permute-start.24 = (bf16[4,128,256]{2,1,0:T(8,128)(2,1)S(1)}, bf16[4,128,256]{2,1,0:T(8,128)(2,1)S(1)}, u32[]{:S(2)}, u32[]{:S(2)}) collective-permute-start(bf16[4,128,256]{2,1,0:T(8,128)(2,1)S(1)} %get-tuple-element.71), channel_id=1, source_target_pairs={{0,4},{4,0},{8,12},{12,8},{16,20},{20,16},{24,28},{28,24},{1,5},{5... | collective-permute-start | bytes 786440 | tf_op jit(solution)/shard_map/ppermute | solution.py:542
  62.2 4.5 %collective-permute-start.17 = (bf16[4,256,128]{2,1,0:T(8,128)(2,1)S(1)}, bf16[4,256,128]{2,1,0:T(8,128)(2,1)S(1)}, u32[]{:S(2)}, u32[]{:S(2)}) collective-permute-start(bf16[4,256,128]{2,1,0:T(8,128)(2,1)S(1)} %merge.3), channel_id=1, source_target_pairs={{0,4},{4,0},{8,12},{12,8},{16,20},{20,16},{24,28},{28,24},{1,5},{5... | collective-permute-start | bytes 786440 | tf_op jit(solution)/shard_map/ppermute | solution.py:542
  62.3 7.6 %collective-permute-start.25 = (bf16[128,256]{1,0:T(8,128)(2,1)S(1)}, bf16[128,256]{1,0:T(8,128)(2,1)S(1)}, u32[]{:S(2)}, u32[]{:S(2)}) collective-permute-start(bf16[128,256]{1,0:T(8,128)(2,1)S(1)} %get-tuple-element.73), channel_id=1, source_target_pairs={{0,8},{4,12},{8,0},{12,4},{16,24},{20,28},{24,16},{28,20},{1,9},{5... | collective-permute-start | bytes 196616 | tf_op jit(solution)/shard_map/ppermute | solution.py:537
  64.1 7.7 %collective-permute-start.26 = (bf16[128,256]{1,0:T(8,128)(2,1)S(1)}, bf16[128,256]{1,0:T(8,128)(2,1)S(1)}, u32[]{:S(2)}, u32[]{:S(2)}) collective-permute-start(bf16[128,256]{1,0:T(8,128)(2,1)S(1)} %get-tuple-element.74), channel_id=1, source_target_pairs={{0,16},{4,20},{8,24},{12,28},{16,0},{20,4},{24,8},{28,12},{1,17},{... | collective-permute-start | bytes 196616 | tf_op jit(solution)/shard_map/ppermute | solution.py:537
  65.3 6.6 %collective-permute-start.27 = (bf16[128,256]{1,0:T(8,128)(2,1)S(1)}, bf16[128,256]{1,0:T(8,128)(2,1)S(1)}, u32[]{:S(2)}, u32[]{:S(2)}) collective-permute-start(bf16[128,256]{1,0:T(8,128)(2,1)S(1)} %get-tuple-element.75), channel_id=1, source_target_pairs={{0,24},{4,28},{8,16},{12,20},{16,8},{20,12},{24,0},{28,4},{1,25},{... | collective-permute-start | bytes 196616 | tf_op jit(solution)/shard_map/ppermute | solution.py:537
  67.3 5.4 %collective-permute-start.18 = (bf16[256,128]{1,0:T(8,128)(2,1)S(1)}, bf16[256,128]{1,0:T(8,128)(2,1)S(1)}, u32[]{:S(2)}, u32[]{:S(2)}) collective-permute-start(bf16[256,128]{1,0:T(8,128)(2,1)S(1)} %get-tuple-element.65), channel_id=1, source_target_pairs={{0,1},{1,0},{2,3},{3,2},{4,5},{5,4},{6,7},{7,6},{8,9},{9,8},{10,11... | collective-permute-start | bytes 196616 | tf_op jit(solution)/shard_map/ppermute | solution.py:537
  68.7 7.8 %collective-permute-start.19 = (bf16[256,128]{1,0:T(8,128)(2,1)S(1)}, bf16[256,128]{1,0:T(8,128)(2,1)S(1)}, u32[]{:S(2)}, u32[]{:S(2)}) collective-permute-start(bf16[256,128]{1,0:T(8,128)(2,1)S(1)} %get-tuple-element.66), channel_id=1, source_target_pairs={{0,2},{1,3},{2,0},{3,1},{4,6},{5,7},{6,4},{7,5},{8,10},{9,11},{10,... | collective-permute-start | bytes 196616 | tf_op jit(solution)/shard_map/ppermute | solution.py:537
  69.9 6.5 %collective-permute-start.20 = (bf16[256,128]{1,0:T(8,128)(2,1)S(1)}, bf16[256,128]{1,0:T(8,128)(2,1)S(1)}, u32[]{:S(2)}, u32[]{:S(2)}) collective-permute-start(bf16[256,128]{1,0:T(8,128)(2,1)S(1)} %get-tuple-element.67), channel_id=1, source_target_pairs={{0,3},{1,2},{2,1},{3,0},{4,7},{5,6},{6,5},{7,4},{8,11},{9,10},{10,... | collective-permute-start | bytes 196616 | tf_op jit(solution)/shard_map/ppermute | solution.py:537
